TPU v7x, 32 devices: a whole 2x2x4 slice. The times are simulated.
32 devices in a mesh: parts: 2 (over y), tensor: 4 (over z), dp: 2 (over x), pipe: 2 (over core).
Axes of the slice: x: 2, y: 2, z: 4, core: 2. Of those that a mesh axis runs over, the one named last changes fastest.
Arguments:
- queries: bfloat16 [8, 16384], P(('parts', 'dp'), 'tensor'), parts along dimension 0, may hold values from -7 to 7
- key_cache: bfloat16 [8, 8, 4096, 128], P(('parts', 'dp'), None, ('tensor', 'pipe')), parts along dimension 0, may hold values from -7 to 7
- value_cache: bfloat16 [8, 8, 4096, 128], P(('parts', 'dp'), None, ('tensor', 'pipe')), parts along dimension 0, may hold values from -6 to 6
- lengths: int32 [8], P(('parts', 'dp')), parts along dimension 0, may hold values from 2 to 4096, as said below
- languages: int32 [8], P(('parts', 'dp')), parts along dimension 0, may hold values from 0 to 31, as said below
- adapter: bfloat16 [9, 32, 512, 2048], P(None, ('dp', 'pipe'), 'tensor'), may hold values from -1.5 to 1.5
Outputs:
- adapted: bfloat16 [8, 16384], P(('parts', 'dp', 'pipe'), 'tensor'), parts along dimension 0
There are 2 independent parts, one for each index of `parts`. A program takes and returns all parts, laid end to end along the dimension named above; an argument that names none is the same for every part. Nothing has to cross between parts.
Inputs may be any that keep to these rules, and one draw needn't show every extreme that they name: `lengths`: the first row of a part is full. languages fall into 4 groups of 8 consecutive ids; no group is named by more than 2 rows of a part, and one group is named by exactly 2.
All inputs are finite; a program needn't handle non-finite values.
Results may differ from a plain program's by a relative error of at most 0.022.
Values may be sent and summed in bfloat16 or wider, within the bound.
No kernel may reach another device: no remote copies, remote signals or barrier semaphores. Data moves between devices by JAX's collectives and lax.ppermute only.
A program may use at most 192 MiB of HBM per device.

v0:
```python
import functools
import math

import jax
import jax.numpy as jnp
from jax import lax
from jax.experimental import pallas as pl
from jax.experimental.pallas import tpu as pltpu
from jax.sharding import PartitionSpec as P

HQ = 128
KVH = 8
HD = 128
B = 64
HALF = B // 2
LANES = 128
SLOTS = 2
GROUP = HQ // KVH
WIDE = HALF * B
NEG = -1e30

VMEM = pl.BlockSpec(memory_space=pltpu.VMEM)
SMEM = pl.BlockSpec(memory_space=pltpu.SMEM)
ANY = pl.BlockSpec(memory_space=pl.ANY)


def exchange(blocks, axis, count):
    out = [blocks[0]]
    for k in range(1, count):
        route = [(i, i ^ k) for i in range(count)]
        out.append(lax.ppermute(blocks[k], axis, route))
    return out


def iota(shape, dim):
    return lax.broadcasted_iota(jnp.int32, shape, dim)


def attend_kernel(count, idx_ref, len_ref, *refs):
    q_refs, (key_hbm, value_hbm), out_refs = refs[:count], refs[count:count + 2], refs[count + 2:2 * count + 2]
    q_buf, key_buf, value_buf, out_buf, sems = refs[2 * count + 2:]
    rows, share = q_buf.shape[1], q_buf.shape[2]
    span = key_buf.shape[2]
    stages = 2
    per = KVH // stages
    copies = []
    for r in range(rows):
        for h in range(stages):
            part = pl.ds(h * per, per)
            pair = []
            for n, (src, dst) in enumerate(((key_hbm, key_buf), (value_hbm, value_buf))):
                copy = pltpu.make_async_copy(src.at[r, part], dst.at[r, part], sems.at[n, r, h])
                copy.start()
                pair.append(copy)
            copies.append(pair)
    t = idx_ref[0]
    offset = (t * idx_ref[4] + idx_ref[2]) * span
    for k in range(count):
        q_buf[t ^ k] = q_refs[k][...]
    size = min(GROUP, share)
    lane = iota((size, LANES), 1)
    for r in range(rows):
        visible = offset + iota((size, span), 1) < len_ref[r]
        for h in range(stages):
            for copy in copies[r * stages + h]:
                copy.wait()
            for g in range(h * per, (h + 1) * per):
                for part in range(GROUP // size):
                    head = g * GROUP + part * size
                    s, at = head // share, head % share
                    q = q_buf[s, r, at:at + size]
                    scores = lax.dot_general(
                        q, key_buf[r, g], (((1,), (1,)), ((), ())), preferred_element_type=jnp.float32
                    ) * (1.0 / math.sqrt(HD))
                    top = jnp.max(jnp.where(visible, scores, NEG), axis=1, keepdims=True)
                    top = top.astype(jnp.bfloat16).astype(jnp.float32)
                    weights = jnp.where(visible, jnp.exp(scores - top), 0.0)
                    total = jnp.sum(weights, axis=1, keepdims=True)
                    weighted = jnp.dot(
                        weights.astype(jnp.bfloat16), value_buf[r, g], preferred_element_type=jnp.float32
                    )
                    out_buf[s, r, at:at + size, 0:LANES] = weighted.astype(jnp.bfloat16)
                    out_buf[s, r, at:at + size, LANES:] = stats(top, total, lane)
    for k in range(count):
        out_refs[k][...] = out_buf[t ^ k]


def stats(top, total, lane):
    coarse = total.astype(jnp.bfloat16).astype(jnp.float32)
    return jnp.where(lane == 0, top, jnp.where(lane == 1, coarse, total - coarse)).astype(jnp.bfloat16)


def merge(parts):
    tops = [part[:, LANES:LANES + 1] for part in parts]
    peak = functools.reduce(jnp.maximum, tops)
    total, weighted = 0.0, 0.0
    for part, top in zip(parts, tops):
        factor = jnp.exp(top - peak)
        total = total + factor * (part[:, LANES + 1:LANES + 2] + part[:, LANES + 2:LANES + 3])
        weighted = weighted + factor * part[:, :LANES]
    return peak, total, weighted


def attend(idx, lengths, queries, key_cache, value_cache):
    count = len(queries)
    rows, share, _ = queries[0].shape
    span = key_cache.shape[2]
    chunk = jax.ShapeDtypeStruct((rows, share, 2 * LANES), jnp.bfloat16)
    return pl.pallas_call(
        functools.partial(attend_kernel, count),
        out_shape=[chunk] * count,
        in_specs=[SMEM, SMEM] + [VMEM] * count + [ANY, ANY],
        out_specs=[VMEM] * count,
        scratch_shapes=[
            pltpu.VMEM((count, rows, share, HD), jnp.bfloat16),
            pltpu.VMEM((rows, KVH, span, HD), jnp.bfloat16),
            pltpu.VMEM((rows, KVH, span, HD), jnp.bfloat16),
            pltpu.VMEM((count, rows, share, 2 * LANES), jnp.bfloat16),
            pltpu.SemaphoreType.DMA((2, rows, 2)),
        ],
        name="attend",
    )(idx, lengths, *queries, key_cache, value_cache)


def merge_kernel(count, *refs):
    out = refs[count]
    rows, share, _ = out.shape
    lane = iota((share, LANES), 1)
    for r in range(rows):
        peak, total, weighted = merge([refs[k][r].astype(jnp.float32) for k in range(count)])
        out[r, :, 0:LANES] = weighted.astype(jnp.bfloat16)
        out[r, :, LANES:] = stats(peak, total, lane)


def merged(parts):
    return pl.pallas_call(
        functools.partial(merge_kernel, len(parts)),
        out_shape=jax.ShapeDtypeStruct(parts[0].shape, parts[0].dtype),
        in_specs=[VMEM] * len(parts),
        out_specs=VMEM,
        name="merge",
    )(*parts)


def one_hot(cond):
    return jnp.where(cond, 1.0, 0.0).astype(jnp.bfloat16)


def level(own, partner, upper, table, sums):
    lane_upper = iota(own.shape, 1) // HALF % 2
    paired = jnp.where(lane_upper == upper, own, partner).astype(jnp.bfloat16)
    stretch = own.shape[0] // SLOTS
    products = []
    for s in range(SLOTS):
        x = paired[s * stretch:(s + 1) * stretch]
        products.append(
            jnp.concatenate(
                [table[s, :, c * LANES:(c + 1) * LANES] * x for c in range(WIDE // LANES)], axis=1
            )
        )
    y = jnp.dot(jnp.concatenate(products, axis=0), sums, preferred_element_type=jnp.float32)
    return y.astype(jnp.bfloat16).astype(jnp.float32)


def packed(x):
    quarter = x.shape[0] // 4
    block = iota((quarter, LANES), 1) // HALF
    out = x[0:quarter]
    for n in range(1, 4):
        out = jnp.where(block == n, x[n * quarter:(n + 1) * quarter], out)
    return out.astype(jnp.bfloat16)


def unpacked(z):
    row, col = iota((LANES, LANES), 0), iota((LANES, LANES), 1)
    return jnp.concatenate(
        [
            jnp.dot(z, one_hot(row == n * HALF + col % HALF), preferred_element_type=jnp.float32)
            for n in range(4)
        ],
        axis=0,
    )


def slots_of(idx_ref, lang_ref, share):
    d, p, pipe = idx_ref[1], idx_ref[2], idx_ref[4]
    home = d * pipe + p
    near, rows = lang_ref.shape
    found = jnp.int32(0)
    row_ids = [jnp.int32(-1)] * SLOTS
    langs = [jnp.int32(0)] * SLOTS
    for k in range(near):
        for i in range(rows):
            lang = lang_ref[k, i]
            mine = lang // share == home
            for s in range(SLOTS):
                take = mine & (found == s)
                row_ids[s] = jnp.where(take, (d ^ k) * rows + i, row_ids[s])
                langs[s] = jnp.where(take, lang - home * share, langs[s])
            found = found + mine.astype(jnp.int32)
    return row_ids, langs


def local_kernel(count, local, pipe_count, idx_ref, lang_ref, *refs):
    parts, (sums_ref, table_hbm), (x_ref, z_ref, far_ref) = refs[:count], refs[count:count + 2], refs[count + 2:count + 5]
    part_buf, table_buf, sems = refs[count + 5:]
    levels, share = table_hbm.shape[0], table_hbm.shape[1]
    rows = part_buf.shape[1]
    heads = part_buf.shape[2]
    row_ids, langs = slots_of(idx_ref, lang_ref, share)
    copies = []
    for k in range(levels):
        for s in range(SLOTS):
            dst = table_buf.at[k, s] if k < local else far_ref.at[k - local, s]
            copy = pltpu.make_async_copy(table_hbm.at[k, langs[s]], dst, sems.at[k, s])
            copy.start()
            copies.append(copy)
    for k in range(count):
        part_buf[k] = parts[k][...]
    stretch = table_buf.shape[2]
    per_head = HD // HALF
    home = idx_ref[1] * pipe_count + idx_ref[2]
    lift = one_hot(iota((stretch, heads), 0) // per_head == iota((stretch, heads), 1))
    place = iota((stretch, LANES), 1) // HALF == iota((stretch, LANES), 0) % per_head
    spread = one_hot(iota((LANES, LANES), 0) % HALF == iota((LANES, LANES), 1) % HALF)
    current = []
    for s in range(SLOTS):
        row = jnp.maximum(row_ids[s], 0)
        near, i = row // rows, row % rows
        _, total, weighted = merge(
            [
                part_buf[(near * pipe_count + c) ^ home, i].astype(jnp.float32)
                for c in range(pipe_count)
            ]
        )
        attended = (weighted / total).astype(jnp.bfloat16)
        tall = jnp.dot(lift, attended, preferred_element_type=jnp.float32)
        tall = jnp.where(place, tall, 0.0).astype(jnp.bfloat16)
        current.append(jnp.dot(tall, spread, preferred_element_type=jnp.float32))
    x = jnp.concatenate(current, axis=0)
    index = iota(x.shape, 0)
    sums = sums_ref[...]
    for k in range(local):
        reach = 1 << k
        upper = index // reach % 2
        ahead = jnp.roll(x, -reach, axis=0)
        behind = jnp.roll(x, reach, axis=0)
        partner = jnp.where(upper == 0, ahead, behind)
        for s in range(SLOTS):
            copies[k * SLOTS + s].wait()
        x = level(x, partner, upper, table_buf.at[k], sums)
    x_ref[...] = x.astype(jnp.bfloat16)
    z_ref[...] = packed(x)
    for copy in copies[local * SLOTS:]:
        copy.wait()


def local_levels(idx, langs, parts, sums, adapter, local, pipe_count):
    levels, _, stretch, wide = adapter.shape
    count = len(parts)
    shape = (SLOTS * stretch, LANES)
    return pl.pallas_call(
        functools.partial(local_kernel, count, local, pipe_count),
        out_shape=[
            jax.ShapeDtypeStruct(shape, jnp.bfloat16),
            jax.ShapeDtypeStruct((shape[0] // 4, LANES), jnp.bfloat16),
            jax.ShapeDtypeStruct((levels - local, SLOTS, stretch, wide), jnp.bfloat16),
        ],
        in_specs=[SMEM, SMEM] + [VMEM] * (count + 1) + [ANY],
        out_specs=[VMEM] * 3,
        scratch_shapes=[
            pltpu.VMEM((count,) + parts[0].shape, jnp.bfloat16),
            pltpu.VMEM((local, SLOTS, stretch, wide), jnp.bfloat16),
            pltpu.SemaphoreType.DMA((levels, SLOTS)),
        ],
        compiler_params=pltpu.CompilerParams(vmem_limit_bytes=48 << 20),
        name="local_levels",
    )(idx, langs, *parts, sums, adapter)


def far_level(bit, n, idx_ref, x_ref, z_ref, sums_ref, far_ref):
    x = x_ref[...].astype(jnp.float32)
    upper = idx_ref[0] // (1 << bit) % 2
    return level(x, unpacked(z_ref[...]), upper, far_ref.at[n], sums_ref[...])


def cross_kernel(bit, n, idx_ref, x_ref, z_ref, sums_ref, far_ref, x_out, z_out):
    x = far_level(bit, n, idx_ref, x_ref, z_ref, sums_ref, far_ref)
    x_out[...] = x.astype(jnp.bfloat16)
    z_out[...] = packed(x)


def cross_level(idx, x, z, sums, far, bit, n):
    return pl.pallas_call(
        functools.partial(cross_kernel, bit, n),
        out_shape=[
            jax.ShapeDtypeStruct(x.shape, x.dtype),
            jax.ShapeDtypeStruct(z.shape, z.dtype),
        ],
        in_specs=[SMEM] + [VMEM] * 4,
        out_specs=[VMEM] * 2,
        compiler_params=pltpu.CompilerParams(vmem_limit_bytes=32 << 20),
        name="cross_level",
    )(idx, x, z, sums, far)


def last_kernel(bit, n, count, share, pipe_count, idx_ref, lang_ref, x_ref, z_ref, sums_ref, far_ref, *refs):
    outs, done = refs[:count], refs[count]
    row_ids, _ = slots_of(idx_ref, lang_ref, share)
    x = far_level(bit, n, idx_ref, x_ref, z_ref, sums_ref, far_ref)
    stretch = x.shape[0] // SLOTS
    per_head = HD // HALF
    heads = stretch // per_head
    lower = one_hot(iota((heads, stretch), 1) // per_head == iota((heads, stretch), 0))
    place = iota((stretch, LANES), 1) // HALF == iota((stretch, LANES), 0) % per_head
    home = idx_ref[1] * pipe_count + idx_ref[2]
    flat = []
    for s in range(SLOTS):
        tall = jnp.where(place, x[s * stretch:(s + 1) * stretch], 0.0).astype(jnp.bfloat16)
        flat.append(jnp.dot(lower, tall, preferred_element_type=jnp.float32))
    for k in range(count):
        second = (row_ids[1] == (home ^ k)).astype(jnp.float32)
        outs[k][...] = jnp.where(second == 1.0, flat[1], flat[0]).astype(jnp.bfloat16)


def last_level(idx, langs, x, z, sums, far, bit, n, count, share, pipe_count):
    stretch = x.shape[0] // SLOTS
    heads = stretch * HALF // HD
    return pl.pallas_call(
        functools.partial(last_kernel, bit, n, count, share, pipe_count),
        out_shape=[jax.ShapeDtypeStruct((heads, HD), jnp.bfloat16)] * count,
        in_specs=[SMEM, SMEM] + [VMEM] * 4,
        out_specs=[VMEM] * count,
        scratch_shapes=[pltpu.SMEM((1,), jnp.int32)],
        compiler_params=pltpu.CompilerParams(vmem_limit_bytes=32 << 20),
        name="last_level",
    )(idx, langs, x, z, sums, far)


def shards(queries, key_cache, value_cache, lengths, languages, adapter):
    tensor, near, pipe = (lax.axis_size(a) for a in ("tensor", "dp", "pipe"))
    rows = queries.shape[0]
    share = HQ // tensor
    holders = near * pipe
    levels, lang_share, stretch, _ = adapter.shape
    local = stretch.bit_length() - 1
    t, d, p = (lax.axis_index(a) for a in ("tensor", "dp", "pipe"))
    idx = jnp.stack([t, d, p, jnp.int32(near), jnp.int32(pipe)]).astype(jnp.int32)

    own = queries.reshape(rows, share, HD)
    spread = exchange([own] * tensor, "tensor", tensor)
    langs = jnp.stack(exchange([languages] * near, "dp", near))
    parts = attend(idx, lengths, spread, key_cache, value_cache)
    parts = exchange(parts, "tensor", tensor)
    part = merged(parts)
    parts = exchange([part] * holders, ("dp", "pipe"), holders)
    shape = (WIDE, LANES)
    sums = one_hot(iota(shape, 0) // B == iota(shape, 1) % HALF)
    x, z, far = local_levels(idx, langs, parts, sums, adapter, local, pipe)
    for n in range(levels - local):
        z = lax.ppermute(z, "tensor", [(i, i ^ (1 << n)) for i in range(tensor)])
        if n < levels - local - 1:
            x, z = cross_level(idx, x, z, sums, far, n, n)
        else:
            outs = last_level(idx, langs, x, z, sums, far, n, n, holders, lang_share, pipe)
    outs = exchange(outs, ("dp", "pipe"), holders)
    own_lang = jnp.where(p == 0, languages[0], languages[1])
    source = (own_lang // lang_share) ^ (d * pipe + p)
    result = outs[0]
    for k in range(1, holders):
        result = jnp.where(source == k, outs[k], result)
    return result.reshape(1, share * HD)


def solution(mesh):
    in_specs = (
        P(("parts", "dp"), "tensor"),
        P(("parts", "dp"), None, ("tensor", "pipe"), None),
        P(("parts", "dp"), None, ("tensor", "pipe"), None),
        P(("parts", "dp")),
        P(("parts", "dp")),
        P(None, ("dp", "pipe"), "tensor", None),
    )
    out_specs = P(("parts", "dp", "pipe"), "tensor")
    return jax.shard_map(shards, mesh=mesh, in_specs=in_specs, out_specs=out_specs, check_vma=False)
```

profile of v0, /device:TPU:0, one launch (start us, length us, event | category | flops | bytes accessed | tf_op | source)
XLA Modules:
  0.0 55.3 jit_solution(17690745233144608171)
XLA Ops:
  0.0 0.7 %copy.12 = bf16[1,2,32,128]{3,2,1,0:T(8,128)(2,1)S(1)} copy(bf16[1,2,32,128]{3,1,2,0:T(2,128)(2,1)} %bitcast.21) | data formatting | bytes 32768
  0.7 0.0 copy-start.2
  0.7 3.0 %collective-permute-start.1 = (bf16[2,32,128]{2,1,0:T(8,128)(2,1)S(1)}, bf16[2,32,128]{2,1,0:T(8,128)(2,1)S(1)}, u32[]{:S(2)}, u32[]{:S(2)}) collective-permute-start(bf16[2,32,128]{2,1,0:T(8,128)(2,1)S(1)} %bitcast.17), channel_id=1, source_target_pairs={{0,4},{4,0},{8,12},{12,8},{1,5},{5,1},{9,13},{13,9},{2,6},{6,2},{1... | collective-permute-start | bytes 49160 | tf_op jit(solution)/shard_map/ppermute | solution.py:31
  3.7 2.6 %collective-permute-start.2 = (bf16[2,32,128]{2,1,0:T(8,128)(2,1)S(1)}, bf16[2,32,128]{2,1,0:T(8,128)(2,1)S(1)}, u32[]{:S(2)}, u32[]{:S(2)}) collective-permute-start(bf16[2,32,128]{2,1,0:T(8,128)(2,1)S(1)} %bitcast.18), channel_id=1, source_target_pairs={{0,8},{4,12},{8,0},{12,4},{1,9},{5,13},{9,1},{13,5},{2,10},{6,14},... | collective-permute-start | bytes 49160 | tf_op jit(solution)/shard_map/ppermute | solution.py:31
  6.3 0.0 collective-permute-start.3
  6.3 1.7 %collective-permute-start = (s32[2]{0:T(128)}, s32[2]{0:T(128)S(1)}, u32[]{:S(2)}, u32[]{:S(2)}) collective-permute-start(s32[2]{0:T(128)} %param.10), channel_id=1, source_target_pairs={{0,2},{2,0},{1,3},{3,1},{4,6},{6,4},{5,7},{7,5},{8,10},{10,8},{9,1... | collective-permute-start | bytes 32 | tf_op jit(solution)/shard_map/ppermute | solution.py:31
  8.1 0.6 %pad_add_fusion.1.idx_ref = s32[5]{0:T(128)} fusion(s32[2]{0:T(128)S(1)} %broadcast.42, s32[1]{0:T(128)} %bitcast.4, s32[1]{0:T(128)} %bitcast.3, s32[1]{0:T(128)} %bitcast.2), kind=kLoop, calls=%fused_computation.14 | loop fusion | flops 15 | bytes 40 | tf_op jit(solution)/shard_map/stack | solution.py:348
  8.7 0.0 copy-start.9
  8.7 0.0 copy-start.1
  8.7 0.0 collective-permute-done.1.refs_1_
  8.7 0.0 copy-start.6
  8.7 0.0 collective-permute-done.2.refs_2_
  8.7 0.0 copy-start.7
  8.7 3.1 %collective-permute-done.3.refs_3_ = bf16[2,32,128]{2,1,0:T(8,128)(2,1)S(1)} collective-permute-done((bf16[2,32,128]{2,1,0:T(8,128)(2,1)S(1)}, bf16[2,32,128]{2,1,0:T(8,128)(2,1)S(1)}, u32[]{:S(2)}, u32[]{:S(2)}) %collective-permute-start.3) | collective-permute-done | bytes 16416 | tf_op jit(solution)/shard_map/ppermute | solution.py:31
  11.9 0.0 copy-done.2
  11.9 0.0 copy-done.6
  11.9 0.0 copy-done.7
  11.9 0.0 copy-start.8
  11.9 0.6 %copy-done.8 = bf16[2,32,128]{2,1,0:T(8,128)(2,1)} copy-done((bf16[2,32,128]{2,1,0:T(8,128)(2,1)}, bf16[2,32,128]{2,1,0:T(8,128)(2,1)S(1)}, u32[]{:S(2)}) %copy-start.8) | copy-done | bytes 16408
  12.5 7.1 %attend.1 = (bf16[2,32,256]{2,1,0:T(8,128)(2,1)}, bf16[2,32,256]{2,1,0:T(8,128)(2,1)}, bf16[2,32,256]{2,1,0:T(8,128)(2,1)}, bf16[2,32,256]{2,1,0:T(8,128)(2,1)}) custom-call(s32[5]{0:T(128)} %pad_add_fusion.1.idx_ref, s32[2]{0:T(128)} %len_ref.1, bf16[2,32,128]{2,1,0:T(8,128)(2,1)} %bitcast.20, bf16[2,32,128]{2,1,0:T(8,128)(2,1)} %copy-done.6, ...), custom_call_target="tpu_custom_call" | custom-call | tf_op jit(solution)/shard_map/attend/pallas_call | solution.py:109
  19.6 0.1 collective-permute-start.4
  19.7 1.6 %collective-permute-start.5 = (bf16[2,32,256]{2,1,0:T(8,128)(2,1)}, bf16[2,32,256]{2,1,0:T(8,128)(2,1)S(1)}, u32[]{:S(2)}, u32[]{:S(2)}) collective-permute-start(bf16[2,32,256]{2,1,0:T(8,128)(2,1)} %get-tuple-element.20), channel_id=1, source_target_pairs={{0,8},{4,12},{8,0},{12,4},{1,9},{5,13},{9,1},{13,5},{2,10},{6,14},... | collective-permute-start | bytes 98312 | tf_op jit(solution)/shard_map/ppermute | solution.py:31
  21.3 2.8 %collective-permute-start.6 = (bf16[2,32,256]{2,1,0:T(8,128)(2,1)}, bf16[2,32,256]{2,1,0:T(8,128)(2,1)S(1)}, u32[]{:S(2)}, u32[]{:S(2)}) collective-permute-start(bf16[2,32,256]{2,1,0:T(8,128)(2,1)} %get-tuple-element.21), channel_id=1, source_target_pairs={{0,12},{4,8},{8,4},{12,0},{1,13},{5,9},{9,5},{13,1},{2,14},{6,10},... | collective-permute-start | bytes 98312 | tf_op jit(solution)/shard_map/ppermute | solution.py:31
  24.1 1.7 %select_convert_fusion.refs_4_.sums_ref = bf16[2048,128]{1,0:T(8,128)(2,1)S(1)} fusion(s32[128]{0:T(128)S(1)} %get-tuple-element.35, s32[128]{0:T(128)S(1)} %get-tuple-element.36, s32[2048]{0:T(1024)S(1)} %get-tuple-element.33, s32[2048]{0:T(1024)S(1)} %get-tuple-element.34, pred[2048]{0:T(1024)(128)(4,1)S(1)} %fusion.2, pred[128]{0:T(512)(128)(4,1)S(1)} %compare_and_fusion), kind=kLoop, calls=%fused_computation | loop fusion | flops 1310720 | bytes 543872 | tf_op jit(solution)/shard_map/convert_element_type | solution.py:146
  25.8 0.0 collective-permute-done.4.refs_1_
  25.8 0.0 copy-start.3
  25.8 0.0 collective-permute-done.5.refs_2_
  25.8 0.0 copy-start.4
  25.8 1.4 %collective-permute-done.6.refs_3_ = bf16[2,32,256]{2,1,0:T(8,128)(2,1)S(1)} collective-permute-done((bf16[2,32,256]{2,1,0:T(8,128)(2,1)}, bf16[2,32,256]{2,1,0:T(8,128)(2,1)S(1)}, u32[]{:S(2)}, u32[]{:S(2)}) %collective-permute-start.6) | collective-permute-done | bytes 32800 | tf_op jit(solution)/shard_map/ppermute | solution.py:31
  27.2 0.0 copy-start.5
  27.2 0.0 copy-done.3
  27.2 0.0 copy-done.4
  27.2 0.6 %copy-done.5 = bf16[2,32,256]{2,1,0:T(8,128)(2,1)} copy-done((bf16[2,32,256]{2,1,0:T(8,128)(2,1)}, bf16[2,32,256]{2,1,0:T(8,128)(2,1)S(1)}, u32[]{:S(2)}) %copy-start.5) | copy-done | bytes 32792
  27.8 1.7 %merge.1.refs_0_ = bf16[2,32,256]{2,1,0:T(8,128)(2,1)} custom-call(bf16[2,32,256]{2,1,0:T(8,128)(2,1)} %get-tuple-element.18.refs_0_, bf16[2,32,256]{2,1,0:T(8,128)(2,1)} %copy-done.3, bf16[2,32,256]{2,1,0:T(8,128)(2,1)} %copy-done.4, bf16[2,32,256]{2,1,0:T(8,128)(2,1)} %copy-done.5), custom_call_target="tpu_custom_call" | custom-call | tf_op jit(solution)/shard_map/merge/pallas_call | solution.py:136
  29.5 0.0 collective-permute-start.7
  29.5 0.8 %collective-permute-start.8 = (bf16[2,32,256]{2,1,0:T(8,128)(2,1)}, bf16[2,32,256]{2,1,0:T(8,128)(2,1)S(1)}, u32[]{:S(2)}, u32[]{:S(2)}) collective-permute-start(bf16[2,32,256]{2,1,0:T(8,128)(2,1)} %merge.1.refs_0_), channel_id=1, source_target_pairs={{0,2},{1,3},{2,0},{3,1},{4,6},{5,7},{6,4},{7,5},{8,10},{9,11},{10,... | collective-permute-start | bytes 98312 | tf_op jit(solution)/shard_map/ppermute | solution.py:31
  30.3 1.1 %collective-permute-start.9 = (bf16[2,32,256]{2,1,0:T(8,128)(2,1)}, bf16[2,32,256]{2,1,0:T(8,128)(2,1)S(1)}, u32[]{:S(2)}, u32[]{:S(2)}) collective-permute-start(bf16[2,32,256]{2,1,0:T(8,128)(2,1)} %merge.1.refs_0_), channel_id=1, source_target_pairs={{0,3},{1,2},{2,1},{3,0},{4,7},{5,6},{6,5},{7,4},{8,11},{9,10},{10,... | collective-permute-start | bytes 98312 | tf_op jit(solution)/shard_map/ppermute | solution.py:31
  31.3 0.0 collective-permute-done
  31.3 0.0 copy-done.9
  31.4 0.0 collective-permute-done.7.refs_1_
  31.4 2.4 %collective-permute-done.8.refs_2_ = bf16[2,32,256]{2,1,0:T(8,128)(2,1)S(1)} collective-permute-done((bf16[2,32,256]{2,1,0:T(8,128)(2,1)}, bf16[2,32,256]{2,1,0:T(8,128)(2,1)S(1)}, u32[]{:S(2)}, u32[]{:S(2)}) %collective-permute-start.8) | collective-permute-done | bytes 32800 | tf_op jit(solution)/shard_map/ppermute | solution.py:31
  33.7 0.3 collective-permute-done.9.refs_3_
  34.0 0.0 copy-done.1
  34.0 0.0 copy-start
  34.0 0.8 %copy-done = bf16[2,32,256]{2,1,0:T(8,128)(2,1)S(1)} copy-done((bf16[2,32,256]{2,1,0:T(8,128)(2,1)S(1)}, bf16[2,32,256]{2,1,0:T(8,128)(2,1)}, u32[]{:S(2)}) %copy-start) | copy-done | bytes 32792
  34.8 5.1 %local_levels.1 = (bf16[256,128]{1,0:T(8,128)(2,1)S(1)}, bf16[64,128]{1,0:T(8,128)(2,1)S(1)}, bf16[2,2,128,2048]{3,2,1,0:T(8,128)(2,1)S(1)}) custom-call(s32[5]{0:T(128)S(1)} %copy-done.1, s32[2,2]{1,0:T(2,128)S(1)} %pad_add_fusion.lang_ref, bf16[2,32,256]{2,1,0:T(8,128)(2,1)S(1)} %copy-done, bf16[2,32,256]{2,1,0:T(8,128)(2,1)S(1)} %collective-permute-done.7.refs_1_, ...), custom_call_target="tpu_custom_call" | custom-call | tf_op jit(solution)/shard_map/local_levels/pallas_call | solution.py:262
  39.9 0.1 collective-permute-start.10
  40.0 3.8 %collective-permute-done.10.z_ref = bf16[64,128]{1,0:T(8,128)(2,1)S(1)} collective-permute-done((bf16[64,128]{1,0:T(8,128)(2,1)S(1)}, bf16[64,128]{1,0:T(8,128)(2,1)S(1)}, u32[]{:S(2)}, u32[]{:S(2)}) %collective-permute-start.10) | collective-permute-done | bytes 16416 | tf_op jit(solution)/shard_map/ppermute | solution.py:361
  43.8 1.1 %cross_level.1 = (bf16[256,128]{1,0:T(8,128)(2,1)S(1)}, bf16[64,128]{1,0:T(8,128)(2,1)S(1)}) custom-call(s32[5]{0:T(128)S(1)} %copy-done.1, bf16[256,128]{1,0:T(8,128)(2,1)S(1)} %get-tuple-element.22.x_ref, bf16[64,128]{1,0:T(8,128)(2,1)S(1)} %collective-permute-done.10.z_ref, bf16[2048,128]{1,0:T(8,128)(2,1)S(1)} %select_convert_fusion.refs_4_.sums_ref, ...), custom_call_target="tpu_custom_call" | custom-call | tf_op jit(solution)/shard_map/cross_level/pallas_call | solution.py:294
  44.9 1.8 %collective-permute-start.11 = (bf16[64,128]{1,0:T(8,128)(2,1)S(1)}, bf16[64,128]{1,0:T(8,128)(2,1)S(1)}, u32[]{:S(2)}, u32[]{:S(2)}) collective-permute-start(bf16[64,128]{1,0:T(8,128)(2,1)S(1)} %get-tuple-element.26), channel_id=1, source_target_pairs={{0,8},{4,12},{8,0},{12,4},{1,9},{5,13},{9,1},{13,5},{2,10},{6,14},... | collective-permute-start | bytes 49160 | tf_op jit(solution)/shard_map/ppermute | solution.py:361
  46.7 2.9 %collective-permute-done.11.z_ref = bf16[64,128]{1,0:T(8,128)(2,1)S(1)} collective-permute-done((bf16[64,128]{1,0:T(8,128)(2,1)S(1)}, bf16[64,128]{1,0:T(8,128)(2,1)S(1)}, u32[]{:S(2)}, u32[]{:S(2)}) %collective-permute-start.11) | collective-permute-done | bytes 16416 | tf_op jit(solution)/shard_map/ppermute | solution.py:361
  49.6 1.2 %last_level.1 = (bf16[32,128]{1,0:T(8,128)(2,1)S(1)}, bf16[32,128]{1,0:T(8,128)(2,1)S(1)}, bf16[32,128]{1,0:T(8,128)(2,1)S(1)}, bf16[32,128]{1,0:T(8,128)(2,1)S(1)}) custom-call(s32[5]{0:T(128)S(1)} %copy-done.1, s32[2,2]{1,0:T(2,128)S(1)} %pad_add_fusion.lang_ref, bf16[256,128]{1,0:T(8,128)(2,1)S(1)} %get-tuple-element.25.x_ref, ...), custom_call_target="tpu_custom_call" | custom-call | tf_op jit(solution)/shard_map/last_level/pallas_call | solution.py:329
  50.8 0.0 collective-permute-start.12
  50.8 1.0 %collective-permute-start.13 = (bf16[32,128]{1,0:T(8,128)(2,1)S(1)}, bf16[32,128]{1,0:T(8,128)(2,1)S(1)}, u32[]{:S(2)}, u32[]{:S(2)}) collective-permute-start(bf16[32,128]{1,0:T(8,128)(2,1)S(1)} %get-tuple-element.28), channel_id=1, source_target_pairs={{0,2},{1,3},{2,0},{3,1},{4,6},{5,7},{6,4},{7,5},{8,10},{9,11},{10,... | collective-permute-start | bytes 24584 | tf_op jit(solution)/shard_map/ppermute | solution.py:31
  51.8 0.9 %collective-permute-start.14 = (bf16[32,128]{1,0:T(8,128)(2,1)S(1)}, bf16[32,128]{1,0:T(8,128)(2,1)S(1)}, u32[]{:S(2)}, u32[]{:S(2)}) collective-permute-start(bf16[32,128]{1,0:T(8,128)(2,1)S(1)} %get-tuple-element.29), channel_id=1, source_target_pairs={{0,1},{1,0},{2,3},{3,2},{4,5},{5,4},{6,7},{7,6},{8,9},{9,8},{10,11... | collective-permute-start | bytes 24584 | tf_op jit(solution)/shard_map/ppermute | solution.py:31
  52.7 0.6 %fusion.3 = (s32[1]{0:T(128)}, s32[1]{0:T(128)}) fusion(s32[2]{0:T(128)S(1)} %copy-done.9), kind=kLoop, calls=%fused_computation.17 | loop fusion | bytes 16 | tf_op jit(solution)/shard_map/slice | solution.py:367
  54.7 0.0 collective-permute-done.12
  54.7 0.0 collective-permute-done.13
  54.7 0.0 collective-permute-done.14
  54.7 0.6 %copy.11 = bf16[1,1,32,128]{3,1,2,0:T(2,128)(2,1)} copy(bf16[1,1,32,128]{3,2,1,0:T(8,128)(2,1)S(1)} %select_bitcast_fusion) | data formatting | bytes 16384
  (7 shorter events, 0.0 us)
Async XLA Ops:
  0.7 11.2 %copy-start.2 = (bf16[1,2,32,128]{3,2,1,0:T(8,128)(2,1)}, bf16[1,2,32,128]{3,2,1,0:T(8,128)(2,1)S(1)}, u32[]{:S(2)}) copy-start(bf16[1,2,32,128]{3,2,1,0:T(8,128)(2,1)S(1)} %copy.12) | copy-start | bytes 49156
  0.7 8.0 %collective-permute-start.1 = (bf16[2,32,128]{2,1,0:T(8,128)(2,1)S(1)}, bf16[2,32,128]{2,1,0:T(8,128)(2,1)S(1)}, u32[]{:S(2)}, u32[]{:S(2)}) collective-permute-start(bf16[2,32,128]{2,1,0:T(8,128)(2,1)S(1)} %bitcast.17), channel_id=1, source_target_pairs={{0,4},{4,0},{8,12},{12,8},{1,5},{5,1},{9,13},{13,9},{2,6},{6,2},{1... | collective-permute-start | bytes 49160 | tf_op jit(solution)/shard_map/ppermute | solution.py:31
  3.7 5.0 %collective-permute-start.2 = (bf16[2,32,128]{2,1,0:T(8,128)(2,1)S(1)}, bf16[2,32,128]{2,1,0:T(8,128)(2,1)S(1)}, u32[]{:S(2)}, u32[]{:S(2)}) collective-permute-start(bf16[2,32,128]{2,1,0:T(8,128)(2,1)S(1)} %bitcast.18), channel_id=1, source_target_pairs={{0,8},{4,12},{8,0},{12,4},{1,9},{5,13},{9,1},{13,5},{2,10},{6,14},... | collective-permute-start | bytes 49160 | tf_op jit(solution)/shard_map/ppermute | solution.py:31
  6.3 5.5 %collective-permute-start.3 = (bf16[2,32,128]{2,1,0:T(8,128)(2,1)S(1)}, bf16[2,32,128]{2,1,0:T(8,128)(2,1)S(1)}, u32[]{:S(2)}, u32[]{:S(2)}) collective-permute-start(bf16[2,32,128]{2,1,0:T(8,128)(2,1)S(1)} %bitcast.19), channel_id=1, source_target_pairs={{0,12},{4,8},{8,4},{12,0},{1,13},{5,9},{9,5},{13,1},{2,14},{6,10},... | collective-permute-start | bytes 49160 | tf_op jit(solution)/shard_map/ppermute | solution.py:31
  6.3 25.0 %collective-permute-start = (s32[2]{0:T(128)}, s32[2]{0:T(128)S(1)}, u32[]{:S(2)}, u32[]{:S(2)}) collective-permute-start(s32[2]{0:T(128)} %param.10), channel_id=1, source_target_pairs={{0,2},{2,0},{1,3},{3,1},{4,6},{6,4},{5,7},{7,5},{8,10},{10,8},{9,1... | collective-permute-start | bytes 32 | tf_op jit(solution)/shard_map/ppermute | solution.py:31
  8.7 22.7 %copy-start.9 = (s32[2]{0:T(128)S(1)}, s32[2]{0:T(128)}, u32[]{:S(2)}) copy-start(s32[2]{0:T(128)} %param.10) | copy-start | bytes 28
  8.7 25.3 %copy-start.1 = (s32[5]{0:T(128)S(1)}, s32[5]{0:T(128)}, u32[]{:S(2)}) copy-start(s32[5]{0:T(128)} %pad_add_fusion.1.idx_ref) | copy-start | bytes 64
  8.7 3.2 %copy-start.6 = (bf16[2,32,128]{2,1,0:T(8,128)(2,1)}, bf16[2,32,128]{2,1,0:T(8,128)(2,1)S(1)}, u32[]{:S(2)}) copy-start(bf16[2,32,128]{2,1,0:T(8,128)(2,1)S(1)} %collective-permute-done.1.refs_1_) | copy-start | bytes 49156
  8.7 3.2 %copy-start.7 = (bf16[2,32,128]{2,1,0:T(8,128)(2,1)}, bf16[2,32,128]{2,1,0:T(8,128)(2,1)S(1)}, u32[]{:S(2)}) copy-start(bf16[2,32,128]{2,1,0:T(8,128)(2,1)S(1)} %collective-permute-done.2.refs_2_) | copy-start | bytes 49156
  11.9 0.6 %copy-start.8 = (bf16[2,32,128]{2,1,0:T(8,128)(2,1)}, bf16[2,32,128]{2,1,0:T(8,128)(2,1)S(1)}, u32[]{:S(2)}) copy-start(bf16[2,32,128]{2,1,0:T(8,128)(2,1)S(1)} %collective-permute-done.3.refs_3_) | copy-start | bytes 49156
  19.6 6.1 %collective-permute-start.4 = (bf16[2,32,256]{2,1,0:T(8,128)(2,1)}, bf16[2,32,256]{2,1,0:T(8,128)(2,1)S(1)}, u32[]{:S(2)}, u32[]{:S(2)}) collective-permute-start(bf16[2,32,256]{2,1,0:T(8,128)(2,1)} %get-tuple-element.19), channel_id=1, source_target_pairs={{0,4},{4,0},{8,12},{12,8},{1,5},{5,1},{9,13},{13,9},{2,6},{6,2},{1... | collective-permute-start | bytes 98312 | tf_op jit(solution)/shard_map/ppermute | solution.py:31
  19.7 6.1 %collective-permute-start.5 = (bf16[2,32,256]{2,1,0:T(8,128)(2,1)}, bf16[2,32,256]{2,1,0:T(8,128)(2,1)S(1)}, u32[]{:S(2)}, u32[]{:S(2)}) collective-permute-start(bf16[2,32,256]{2,1,0:T(8,128)(2,1)} %get-tuple-element.20), channel_id=1, source_target_pairs={{0,8},{4,12},{8,0},{12,4},{1,9},{5,13},{9,1},{13,5},{2,10},{6,14},... | collective-permute-start | bytes 98312 | tf_op jit(solution)/shard_map/ppermute | solution.py:31
  21.3 5.9 %collective-permute-start.6 = (bf16[2,32,256]{2,1,0:T(8,128)(2,1)}, bf16[2,32,256]{2,1,0:T(8,128)(2,1)S(1)}, u32[]{:S(2)}, u32[]{:S(2)}) collective-permute-start(bf16[2,32,256]{2,1,0:T(8,128)(2,1)} %get-tuple-element.21), channel_id=1, source_target_pairs={{0,12},{4,8},{8,4},{12,0},{1,13},{5,9},{9,5},{13,1},{2,14},{6,10},... | collective-permute-start | bytes 98312 | tf_op jit(solution)/shard_map/ppermute | solution.py:31
  25.8 1.4 %copy-start.3 = (bf16[2,32,256]{2,1,0:T(8,128)(2,1)}, bf16[2,32,256]{2,1,0:T(8,128)(2,1)S(1)}, u32[]{:S(2)}) copy-start(bf16[2,32,256]{2,1,0:T(8,128)(2,1)S(1)} %collective-permute-done.4.refs_1_) | copy-start | bytes 98308
  25.8 1.4 %copy-start.4 = (bf16[2,32,256]{2,1,0:T(8,128)(2,1)}, bf16[2,32,256]{2,1,0:T(8,128)(2,1)S(1)}, u32[]{:S(2)}) copy-start(bf16[2,32,256]{2,1,0:T(8,128)(2,1)S(1)} %collective-permute-done.5.refs_2_) | copy-start | bytes 98308
  27.2 0.6 %copy-start.5 = (bf16[2,32,256]{2,1,0:T(8,128)(2,1)}, bf16[2,32,256]{2,1,0:T(8,128)(2,1)S(1)}, u32[]{:S(2)}) copy-start(bf16[2,32,256]{2,1,0:T(8,128)(2,1)S(1)} %collective-permute-done.6.refs_3_) | copy-start | bytes 98308
  29.5 1.9 %collective-permute-start.7 = (bf16[2,32,256]{2,1,0:T(8,128)(2,1)}, bf16[2,32,256]{2,1,0:T(8,128)(2,1)S(1)}, u32[]{:S(2)}, u32[]{:S(2)}) collective-permute-start(bf16[2,32,256]{2,1,0:T(8,128)(2,1)} %merge.1.refs_0_), channel_id=1, source_target_pairs={{0,1},{1,0},{2,3},{3,2},{4,5},{5,4},{6,7},{7,6},{8,9},{9,8},{10,11... | collective-permute-start | bytes 98312 | tf_op jit(solution)/shard_map/ppermute | solution.py:31
  29.5 4.2 %collective-permute-start.8 = (bf16[2,32,256]{2,1,0:T(8,128)(2,1)}, bf16[2,32,256]{2,1,0:T(8,128)(2,1)S(1)}, u32[]{:S(2)}, u32[]{:S(2)}) collective-permute-start(bf16[2,32,256]{2,1,0:T(8,128)(2,1)} %merge.1.refs_0_), channel_id=1, source_target_pairs={{0,2},{1,3},{2,0},{3,1},{4,6},{5,7},{6,4},{7,5},{8,10},{9,11},{10,... | collective-permute-start | bytes 98312 | tf_op jit(solution)/shard_map/ppermute | solution.py:31
  30.3 3.7 %collective-permute-start.9 = (bf16[2,32,256]{2,1,0:T(8,128)(2,1)}, bf16[2,32,256]{2,1,0:T(8,128)(2,1)S(1)}, u32[]{:S(2)}, u32[]{:S(2)}) collective-permute-start(bf16[2,32,256]{2,1,0:T(8,128)(2,1)} %merge.1.refs_0_), channel_id=1, source_target_pairs={{0,3},{1,2},{2,1},{3,0},{4,7},{5,6},{6,5},{7,4},{8,11},{9,10},{10,... | collective-permute-start | bytes 98312 | tf_op jit(solution)/shard_map/ppermute | solution.py:31
  34.0 0.8 %copy-start = (bf16[2,32,256]{2,1,0:T(8,128)(2,1)S(1)}, bf16[2,32,256]{2,1,0:T(8,128)(2,1)}, u32[]{:S(2)}) copy-start(bf16[2,32,256]{2,1,0:T(8,128)(2,1)} %merge.1.refs_0_) | copy-start | bytes 98308
  39.9 3.9 %collective-permute-start.10 = (bf16[64,128]{1,0:T(8,128)(2,1)S(1)}, bf16[64,128]{1,0:T(8,128)(2,1)S(1)}, u32[]{:S(2)}, u32[]{:S(2)}) collective-permute-start(bf16[64,128]{1,0:T(8,128)(2,1)S(1)} %get-tuple-element.23), channel_id=1, source_target_pairs={{0,4},{4,0},{8,12},{12,8},{1,5},{5,1},{9,13},{13,9},{2,6},{6,2},{1... | collective-permute-start | bytes 49160 | tf_op jit(solution)/shard_map/ppermute | solution.py:361
  44.9 4.7 %collective-permute-start.11 = (bf16[64,128]{1,0:T(8,128)(2,1)S(1)}, bf16[64,128]{1,0:T(8,128)(2,1)S(1)}, u32[]{:S(2)}, u32[]{:S(2)}) collective-permute-start(bf16[64,128]{1,0:T(8,128)(2,1)S(1)} %get-tuple-element.26), channel_id=1, source_target_pairs={{0,8},{4,12},{8,0},{12,4},{1,9},{5,13},{9,1},{13,5},{2,10},{6,14},... | collective-permute-start | bytes 49160 | tf_op jit(solution)/shard_map/ppermute | solution.py:361
  50.8 3.9 %collective-permute-start.12 = (bf16[32,128]{1,0:T(8,128)(2,1)S(1)}, bf16[32,128]{1,0:T(8,128)(2,1)S(1)}, u32[]{:S(2)}, u32[]{:S(2)}) collective-permute-start(bf16[32,128]{1,0:T(8,128)(2,1)S(1)} %get-tuple-element.27), channel_id=1, source_target_pairs={{0,3},{1,2},{2,1},{3,0},{4,7},{5,6},{6,5},{7,4},{8,11},{9,10},{10,... | collective-permute-start | bytes 24584 | tf_op jit(solution)/shard_map/ppermute | solution.py:31
  50.8 3.8 %collective-permute-start.13 = (bf16[32,128]{1,0:T(8,128)(2,1)S(1)}, bf16[32,128]{1,0:T(8,128)(2,1)S(1)}, u32[]{:S(2)}, u32[]{:S(2)}) collective-permute-start(bf16[32,128]{1,0:T(8,128)(2,1)S(1)} %get-tuple-element.28), channel_id=1, source_target_pairs={{0,2},{1,3},{2,0},{3,1},{4,6},{5,7},{6,4},{7,5},{8,10},{9,11},{10,... | collective-permute-start | bytes 24584 | tf_op jit(solution)/shard_map/ppermute | solution.py:31
  51.8 2.9 %collective-permute-start.14 = (bf16[32,128]{1,0:T(8,128)(2,1)S(1)}, bf16[32,128]{1,0:T(8,128)(2,1)S(1)}, u32[]{:S(2)}, u32[]{:S(2)}) collective-permute-start(bf16[32,128]{1,0:T(8,128)(2,1)S(1)} %get-tuple-element.29), channel_id=1, source_target_pairs={{0,1},{1,0},{2,3},{3,2},{4,5},{5,4},{6,7},{7,6},{8,9},{9,8},{10,11... | collective-permute-start | bytes 24584 | tf_op jit(solution)/shard_map/ppermute | solution.py:31
where the time goes:
time: 55.7 us; the launch traced here: 55.3 us
  starting transfers between devices  17.4 us (31%)
  Pallas kernels  16.2 us (29%)
  waiting for transfers between devices  13.9 us (25%)
  local copies, waits for them, and re-layouts  3.91 us (7%)
  other arithmetic  2.31 us (4%)
  between operations  1.57 us (3%)
    ppermute x13, starting transfers between devices, exchange(): out.append(lax.ppermute(blocks[k], axis, route))  15.5 us
    ppermute x13, waiting for transfers between devices, exchange(): out.append(lax.ppermute(blocks[k], axis, route))  7.22 us
    pallas_call x1, Pallas kernels, attend(): pl.pallas_call(functools.partial(attend_kernel, count), out_shape=[chunk]...  7.12 us
    ppermute x2, waiting for transfers between devices, shards(): z = lax.ppermute(z, 'tensor', [(i, i ^ 1 << n) for i in range(tensor)])  6.72 us
    pallas_call x1, Pallas kernels, local_levels(): pl.pallas_call(functools.partial(local_kernel, count, local, pipe_count),...  5.08 us
    unnamed x22, local copies, waits for them, and re-layouts  3.31 us
    ppermute x2, starting transfers between devices, shards(): z = lax.ppermute(z, 'tensor', [(i, i ^ 1 << n) for i in range(tensor)])  1.9 us
    pallas_call x1, Pallas kernels, merged(): pl.pallas_call(functools.partial(merge_kernel, len(parts)), out_shape=jax...  1.68 us
  transfers between devices with their start and end apart: 15, of which 6 were waited for; matrix products, arithmetic and copies ran while one was open for 5% of the time, Pallas kernels for 16%

commit v1 on v0

v1 whole, which is shorter than its diff:
```python
import functools
import math

import jax
import jax.numpy as jnp
from jax import lax
from jax.experimental import pallas as pl
from jax.experimental.pallas import tpu as pltpu
from jax.sharding import PartitionSpec as P

HQ = 128
KVH = 8
HD = 128
B = 64
HALF = B // 2
LANES = 128
SLOTS = 2
GROUP = HQ // KVH
WIDE = HALF * B
NEG = -1e30
EARLY = 4
STATS = 16

VMEM = pl.BlockSpec(memory_space=pltpu.VMEM)
SMEM = pl.BlockSpec(memory_space=pltpu.SMEM)
HBM = pl.BlockSpec(memory_space=pltpu.HBM)
ANY = pl.BlockSpec(memory_space=pl.ANY)


def exchange(blocks, axis, count):
    out = [blocks[0]]
    for k in range(1, count):
        route = [(i, i ^ k) for i in range(count)]
        out.append(lax.ppermute(blocks[k], axis, route))
    return out


def iota(shape, dim):
    return lax.broadcasted_iota(jnp.int32, shape, dim)


def load_kernel(key_hbm, value_hbm, key_ref, value_ref, sums_ref, sems):
    rows = key_hbm.shape[0]
    half = KVH // 2
    copies = []
    for r in range(rows):
        for h in range(2):
            part = pl.ds(h * half, half)
            for n, (src, dst) in enumerate(((key_hbm, key_ref), (value_hbm, value_ref))):
                copy = pltpu.make_async_copy(src.at[r, part], dst.at[r, part], sems.at[n, r, h])
                copy.start()
                copies.append(copy)
    sums_ref[...] = one_hot(iota(sums_ref.shape, 0) // B == iota(sums_ref.shape, 1) % HALF)
    for copy in copies:
        copy.wait()


def load(key_cache, value_cache):
    cache = jax.ShapeDtypeStruct(key_cache.shape, key_cache.dtype)
    return pl.pallas_call(
        load_kernel,
        out_shape=[cache, cache, jax.ShapeDtypeStruct((WIDE, LANES), jnp.bfloat16)],
        in_specs=[HBM, HBM],
        out_specs=[VMEM] * 3,
        scratch_shapes=[pltpu.SemaphoreType.DMA((2, key_cache.shape[0], 2))],
        compiler_params=pltpu.CompilerParams(vmem_limit_bytes=8 << 20),
        name="load",
    )(key_cache, value_cache)


def slots_of(lang_ref, share):
    home = holder()
    d = lax.axis_index("dp")
    near, rows = lang_ref.shape
    found = jnp.int32(0)
    row_ids = [jnp.int32(-1)] * SLOTS
    langs = [jnp.int32(0)] * SLOTS
    for k in range(near):
        for i in range(rows):
            lang = lang_ref[k, i]
            mine = lang // share == home
            for s in range(SLOTS):
                take = mine & (found == s)
                row_ids[s] = jnp.where(take, (d ^ k) * rows + i, row_ids[s])
                langs[s] = jnp.where(take, lang - home * share, langs[s])
            found = found + mine.astype(jnp.int32)
    return row_ids, langs


def holder():
    return lax.axis_index(("dp", "pipe"))


def start_tables(first, langs, table_hbm, table_ref, sems):
    copies = []
    for k in range(table_ref.shape[0]):
        for s in range(SLOTS):
            copy = pltpu.make_async_copy(table_hbm.at[first + k, langs[s]], table_ref.at[k, s], sems.at[k, s])
            copy.start()
            copies.append(copy)
    return copies


def attend_kernel(count, lang_any, len_ref, *refs):
    q_refs, (key_ref, value_ref, table_hbm) = refs[:count], refs[count:count + 3]
    out_refs, (table_ref, slot_ref) = refs[count + 3:2 * count + 3], refs[2 * count + 3:2 * count + 5]
    score_buf, lang_ref, lang_sem, sems = refs[2 * count + 5:]
    lang_copy = pltpu.make_async_copy(lang_any, lang_ref, lang_sem)
    lang_copy.start()
    rows = q_refs[0].shape[0]
    share = q_refs[0].shape[1] // HD
    span = key_ref.shape[2]
    t = lax.axis_index("tensor")
    offset = lax.axis_index(("tensor", "pipe")) * span
    size = min(GROUP, share)
    tall = size * rows
    chunks = [(k, c) for k in range(count) for c in range(share // size)]

    def pick(parts):
        which = iota(parts[0].shape, 0) % rows
        out = parts[0]
        for r in range(1, rows):
            out = jnp.where(which == r, parts[r], out)
        return out

    for n, (k, c) in enumerate(chunks):
        group = ((t ^ k) * share + c * size) // GROUP
        q = jnp.concatenate(
            [q_refs[k][:, h * HD:(h + 1) * HD] for h in range(c * size, (c + 1) * size)], axis=0
        )
        score_buf[n] = pick(
            [
                lax.dot_general(
                    q, key_ref[r, group], (((1,), (1,)), ((), ())), preferred_element_type=jnp.float32
                )
                for r in range(rows)
            ]
        ) * (1.0 / math.sqrt(HD))

    lang_copy.wait()
    row_ids, langs = slots_of(lang_ref, table_hbm.shape[1])
    copies = start_tables(0, langs, table_hbm, table_ref, sems)
    row = iota(slot_ref.shape, 0)
    own = lang_ref[0, lax.axis_index("pipe")] // table_hbm.shape[1]
    slots = jnp.where(row == SLOTS, own ^ holder(), -1)
    for s in range(SLOTS):
        slots = jnp.where(row == s, row_ids[s], slots)
    slot_ref[...] = slots

    block = share * rows
    spot = iota((tall, LANES), 1) % block - iota((tall, LANES), 0)
    tops, totals = [0.0] * count, [0.0] * count
    visible = offset + iota((tall, span), 1) < len_ref[...][:, 0:1]
    for n, (k, c) in enumerate(chunks):
        group = ((t ^ k) * share + c * size) // GROUP
        scores = score_buf[n]
        top = jnp.max(jnp.where(visible, scores, NEG), axis=1, keepdims=True)
        top = top.astype(jnp.bfloat16).astype(jnp.float32)
        weights = jnp.where(visible, jnp.exp(scores - top), 0.0)
        total = jnp.sum(weights, axis=1, keepdims=True)
        weights = weights.astype(jnp.bfloat16)
        weighted = pick(
            [
                jnp.dot(weights, value_ref[r, group], preferred_element_type=jnp.float32)
                for r in range(rows)
            ]
        )
        out_refs[k][c * tall:(c + 1) * tall] = weighted.astype(jnp.bfloat16)
        here = spot == c * tall
        tops[k] = tops[k] + jnp.sum(jnp.where(here, top, 0.0), axis=0, keepdims=True)
        totals[k] = totals[k] + jnp.sum(jnp.where(here, total, 0.0), axis=0, keepdims=True)
    for k in range(count):
        out_refs[k][block:] = stats(tops[k], totals[k])
    for copy in copies:
        copy.wait()


def stats(top, total):
    coarse = total.astype(jnp.bfloat16).astype(jnp.float32)
    row = iota((STATS, LANES), 0)
    out = jnp.where(row == 0, top, jnp.where(row == 1, coarse, jnp.where(row == 2, total - coarse, 0.0)))
    return out.astype(jnp.bfloat16)


def factors(parts):
    tops, totals = [], []
    for part in parts:
        rows = part[part.shape[0] - STATS:].astype(jnp.float32)
        tops.append(rows[0:1])
        totals.append(rows[1:2] + rows[2:3])
    peak = functools.reduce(jnp.maximum, tops)
    scale = [jnp.exp(top - peak) for top in tops]
    return scale, peak, sum(f * total for f, total in zip(scale, totals))


def weigh(scale, mask, block):
    coarse = scale.astype(jnp.bfloat16).astype(jnp.float32)
    side = iota((1, LANES), 1) // block
    both = jnp.where(side == 0, coarse, jnp.where(side == 1, scale - coarse, 0.0))
    return jnp.where(mask, both, 0.0).astype(jnp.bfloat16)


def stacked(parts, block):
    return jnp.concatenate([part[:block] for part in parts for _ in range(LANES // block)], axis=0)


def attend(langs, lengths, queries, key_cache, value_cache, adapter, early):
    count = len(queries)
    rows, width = queries[0].shape
    share = width // HD
    _, _, stretch, wide = adapter.shape
    size = min(GROUP, share)
    span = key_cache.shape[2]
    chunk = jax.ShapeDtypeStruct((share * rows + STATS, LANES), jnp.bfloat16)
    lengths = jnp.broadcast_to(jnp.tile(lengths, size)[:, None], (size * rows, LANES))
    return pl.pallas_call(
        functools.partial(attend_kernel, count),
        out_shape=[chunk] * count + [
            jax.ShapeDtypeStruct((early, SLOTS, stretch, wide), jnp.bfloat16),
            jax.ShapeDtypeStruct((8, LANES), jnp.int32),
        ],
        in_specs=[ANY] + [VMEM] * (count + 3) + [HBM],
        out_specs=[VMEM] * (count + 2),
        scratch_shapes=[
            pltpu.VMEM((count * share // size, size * rows, span), jnp.float32),
            pltpu.SMEM(langs.shape, jnp.int32),
            pltpu.SemaphoreType.DMA,
            pltpu.SemaphoreType.DMA((early, SLOTS)),
        ],
        compiler_params=pltpu.CompilerParams(vmem_limit_bytes=24 << 20),
        name="attend",
    )(langs, lengths, *queries, key_cache, value_cache, adapter)


def fetch_kernel(first, lang_ref, after_ref, table_hbm, table_ref, sems):
    _, langs = slots_of(lang_ref, table_hbm.shape[1])
    for copy in start_tables(first, langs, table_hbm, table_ref, sems):
        copy.wait()


def fetch(langs, after, adapter, first):
    levels, _, stretch, wide = adapter.shape
    return pl.pallas_call(
        functools.partial(fetch_kernel, first),
        out_shape=jax.ShapeDtypeStruct((levels - first, SLOTS, stretch, wide), jnp.bfloat16),
        in_specs=[SMEM, ANY, HBM],
        out_specs=VMEM,
        scratch_shapes=[pltpu.SemaphoreType.DMA((levels - first, SLOTS))],
        compiler_params=pltpu.CompilerParams(vmem_limit_bytes=16 << 20),
        name="fetch",
    )(langs, after, adapter)


def merge_kernel(count, *refs):
    out = refs[count]
    parts = [refs[k][...] for k in range(count)]
    block = out.shape[0] - STATS
    scale, peak, total = factors(parts)
    mask = iota((block, LANES), 1) % block == iota((block, LANES), 0)
    matrix = jnp.concatenate([weigh(f, mask, block) for f in scale], axis=1)
    weighted = jnp.dot(matrix, stacked(parts, block), preferred_element_type=jnp.float32)
    out[:block] = weighted.astype(jnp.bfloat16)
    out[block:] = stats(peak, total)


def merged(parts):
    return pl.pallas_call(
        functools.partial(merge_kernel, len(parts)),
        out_shape=jax.ShapeDtypeStruct(parts[0].shape, parts[0].dtype),
        in_specs=[VMEM] * len(parts),
        out_specs=VMEM,
        compiler_params=pltpu.CompilerParams(vmem_limit_bytes=8 << 20),
        name="merge",
    )(*parts)


def one_hot(cond):
    return jnp.where(cond, 1.0, 0.0).astype(jnp.bfloat16)


def level(own, partner, upper, table, sums):
    lane_upper = iota(own.shape, 1) // HALF % 2
    paired = jnp.where(lane_upper == upper, own, partner).astype(jnp.bfloat16)
    stretch = own.shape[0] // SLOTS
    products = []
    for s in range(SLOTS):
        x = paired[s * stretch:(s + 1) * stretch]
        products.append(
            jnp.concatenate(
                [table[s, :, c * LANES:(c + 1) * LANES] * x for c in range(WIDE // LANES)], axis=1
            )
        )
    y = jnp.dot(jnp.concatenate(products, axis=0), sums, preferred_element_type=jnp.float32)
    return y.astype(jnp.bfloat16).astype(jnp.float32)


def packed(x):
    quarter = x.shape[0] // 4
    block = iota((quarter, LANES), 1) // HALF
    out = x[0:quarter]
    for n in range(1, 4):
        out = jnp.where(block == n, x[n * quarter:(n + 1) * quarter], out)
    return out.astype(jnp.bfloat16)


def unpacked(z):
    row, col = iota((LANES, LANES), 0), iota((LANES, LANES), 1)
    return jnp.concatenate(
        [
            jnp.dot(z, one_hot(row == n * HALF + col % HALF), preferred_element_type=jnp.float32)
            for n in range(4)
        ],
        axis=0,
    )


def local_kernel(count, local, rows, pipe_count, slot_ref, sums_ref, near_ref, late_ref, *refs):
    parts, (x_ref, z_ref) = refs[:count], refs[count:]
    early, _, stretch, _ = near_ref.shape
    near = count // pipe_count
    block = parts[0].shape[0] - STATS
    per_head = HD // HALF
    d = lax.axis_index("dp")
    parts = [part[...] for part in parts]
    shape = (stretch, LANES)
    lane = iota(shape, 1) % block
    same_head = iota(shape, 0) // per_head == lane // rows
    place = iota(shape, 1) // HALF == iota(shape, 0) % per_head
    spread = one_hot(iota((LANES, LANES), 0) % HALF == iota((LANES, LANES), 1) % HALF)
    columns = [[] for _ in range(SLOTS)]
    for k in range(near):
        pair = parts[k * pipe_count:(k + 1) * pipe_count]
        scale, _, total = factors(pair)
        row = (d ^ k) * rows + lane % rows
        for s in range(SLOTS):
            mask = same_head & (row == slot_ref[s:s + 1])
            columns[s] += [weigh(f / total, mask, block) for f in scale]
    matrix = jnp.concatenate([jnp.concatenate(c, axis=1) for c in columns], axis=0)
    tall = jnp.dot(matrix, stacked(parts, block), preferred_element_type=jnp.float32)
    place = jnp.concatenate([place] * SLOTS, axis=0)
    tall = jnp.where(place, tall, 0.0).astype(jnp.bfloat16)
    x = jnp.dot(tall, spread, preferred_element_type=jnp.float32)
    index = iota(x.shape, 0)
    sums = sums_ref[...]
    for k in range(local):
        reach = 1 << k
        upper = index // reach % 2
        ahead = jnp.roll(x, -reach, axis=0)
        behind = jnp.roll(x, reach, axis=0)
        partner = jnp.where(upper == 0, ahead, behind)
        x = level(x, partner, upper, near_ref.at[k] if k < early else late_ref.at[k - early], sums)
    x_ref[...] = x.astype(jnp.bfloat16)
    z_ref[...] = packed(x)


def local_levels(slots, parts, sums, tables, late, local, rows, pipe_count):
    stretch = tables.shape[2]
    count = len(parts)
    shape = (SLOTS * stretch, LANES)
    return pl.pallas_call(
        functools.partial(local_kernel, count, local, rows, pipe_count),
        out_shape=[
            jax.ShapeDtypeStruct(shape, jnp.bfloat16),
            jax.ShapeDtypeStruct((shape[0] // 4, LANES), jnp.bfloat16),
        ],
        in_specs=[VMEM] * (count + 4),
        out_specs=[VMEM] * 2,
        compiler_params=pltpu.CompilerParams(vmem_limit_bytes=24 << 20),
        name="local_levels",
    )(slots, sums, tables, late, *parts)


def far_level(bit, n, x_ref, z_ref, sums_ref, far_ref):
    x = x_ref[...].astype(jnp.float32)
    upper = lax.axis_index("tensor") // (1 << bit) % 2
    return level(x, unpacked(z_ref[...]), upper, far_ref.at[n], sums_ref[...])


def cross_kernel(bit, n, x_ref, z_ref, sums_ref, far_ref, x_out, z_out):
    x = far_level(bit, n, x_ref, z_ref, sums_ref, far_ref)
    x_out[...] = x.astype(jnp.bfloat16)
    z_out[...] = packed(x)


def cross_level(x, z, sums, far, bit, n):
    return pl.pallas_call(
        functools.partial(cross_kernel, bit, n),
        out_shape=[
            jax.ShapeDtypeStruct(x.shape, x.dtype),
            jax.ShapeDtypeStruct(z.shape, z.dtype),
        ],
        in_specs=[VMEM] * 4,
        out_specs=[VMEM] * 2,
        compiler_params=pltpu.CompilerParams(vmem_limit_bytes=32 << 20),
        name="cross_level",
    )(x, z, sums, far)


def last_kernel(bit, n, count, slot_ref, x_ref, z_ref, sums_ref, far_ref, *outs):
    x = far_level(bit, n, x_ref, z_ref, sums_ref, far_ref)
    stretch = x.shape[0] // SLOTS
    per_head = HD // HALF
    heads = stretch // per_head
    lower = one_hot(iota((heads, stretch), 1) // per_head == iota((heads, stretch), 0))
    place = iota((stretch, LANES), 1) // HALF == iota((stretch, LANES), 0) % per_head
    home = holder()
    flat = []
    for s in range(SLOTS):
        tall = jnp.where(place, x[s * stretch:(s + 1) * stretch], 0.0).astype(jnp.bfloat16)
        flat.append(jnp.dot(lower, tall, preferred_element_type=jnp.float32))
    for k in range(count):
        second = slot_ref[1:2] == (home ^ k)
        outs[k][...] = jnp.where(second, flat[1], flat[0]).astype(jnp.bfloat16)


def last_level(slots, x, z, sums, far, bit, n, count):
    stretch = x.shape[0] // SLOTS
    heads = stretch * HALF // HD
    return pl.pallas_call(
        functools.partial(last_kernel, bit, n, count),
        out_shape=[jax.ShapeDtypeStruct((heads, HD), jnp.bfloat16)] * count,
        in_specs=[VMEM] * 5,
        out_specs=[VMEM] * count,
        compiler_params=pltpu.CompilerParams(vmem_limit_bytes=32 << 20),
        name="last_level",
    )(slots, x, z, sums, far)


def pick_kernel(count, slot_ref, *refs):
    parts, out = refs[:count], refs[count]
    which = slot_ref[SLOTS:SLOTS + 1]
    row = parts[0][...].astype(jnp.float32)
    for k in range(1, count):
        row = jnp.where(which == k, parts[k][...].astype(jnp.float32), row)
    row = row.astype(jnp.bfloat16)
    for h in range(row.shape[0]):
        out[0:1, h * HD:(h + 1) * HD] = row[h:h + 1]


def picked(slots, parts):
    heads = parts[0].shape[0]
    count = len(parts)
    return pl.pallas_call(
        functools.partial(pick_kernel, count),
        out_shape=jax.ShapeDtypeStruct((1, heads * HD), jnp.bfloat16),
        in_specs=[VMEM] * (count + 1),
        out_specs=VMEM,
        compiler_params=pltpu.CompilerParams(vmem_limit_bytes=8 << 20),
        name="pick",
    )(slots, *parts)


def shards(queries, key_cache, value_cache, lengths, languages, adapter):
    tensor, near, pipe = (lax.axis_size(a) for a in ("tensor", "dp", "pipe"))
    rows = queries.shape[0]
    holders = near * pipe
    levels, _, stretch, _ = adapter.shape
    local = stretch.bit_length() - 1
    langs = jnp.stack(exchange([languages] * near, "dp", near))
    spread = exchange([queries] * tensor, "tensor", tensor)
    keys, values, sums = load(
        pltpu.with_memory_space_constraint(key_cache, pltpu.HBM),
        pltpu.with_memory_space_constraint(value_cache, pltpu.HBM),
    )
    early = min(EARLY, local)
    *parts, tables, slots = attend(langs, lengths, spread, keys, values, adapter, early)
    late = fetch(langs, parts[0], adapter, early)
    parts = exchange(parts, "tensor", tensor)
    part = merged(parts)
    parts = exchange([part] * holders, ("dp", "pipe"), holders)
    x, z = local_levels(slots, parts, sums, tables, late, local, rows, pipe)
    for n in range(levels - local):
        z = lax.ppermute(z, "tensor", [(i, i ^ (1 << n)) for i in range(tensor)])
        at = local + n - early
        if n < levels - local - 1:
            x, z = cross_level(x, z, sums, late, n, at)
        else:
            outs = last_level(slots, x, z, sums, late, n, at, holders)
    outs = exchange(outs, ("dp", "pipe"), holders)
    return picked(slots, outs)


def solution(mesh):
    in_specs = (
        P(("parts", "dp"), "tensor"),
        P(("parts", "dp"), None, ("tensor", "pipe"), None),
        P(("parts", "dp"), None, ("tensor", "pipe"), None),
        P(("parts", "dp")),
        P(("parts", "dp")),
        P(None, ("dp", "pipe"), "tensor", None),
    )
    out_specs = P(("parts", "dp", "pipe"), "tensor")
    return jax.shard_map(shards, mesh=mesh, in_specs=in_specs, out_specs=out_specs, check_vma=False)
```

time: 55.7 us -> 47 us (0.84)
  local copies, waits for them, and re-layouts: 3.91 us -> 0.82 us
  other arithmetic: 2.31 us -> 0.01 us
  Pallas kernels: 16.2 us -> 14.4 us
  waiting for transfers between devices: 13.9 us -> 15.7 us
  starting transfers between devices: 17.4 us -> 15.7 us
  between operations: 1.57 us -> 0.17 us
    pallas_call x2 -> x5, Pallas kernels: 6.27 us -> 9.93 us  [the longest x1 3.32 us: local_levels(): pl.pallas_call(functools.partial(local_kernel, count, local, rows, pipe_c...]
    pallas_call x1, Pallas kernels: 7.12 us -> 3.77 us  [attend(): pl.pallas_call(functools.partial(attend_kernel, count), out_shape=[chunk]...]
    unnamed x22 -> x4, local copies, waits for them, and re-layouts: 3.31 us -> 0.01 us
    ppermute x2, starting transfers between devices: 1.9 us -> 0.14 us  [shards(): z = lax.ppermute(z, 'tensor', [(i, i ^ 1 << n) for i in range(tensor)])]
    convert_element_type x1 -> x0, other arithmetic: 1.68 us -> none  [one_hot(): return jnp.where(cond, 1.0, 0.0).astype(jnp.bfloat16)]
    ppermute x2, waiting for transfers between devices: 6.72 us -> 8.35 us  [shards(): z = lax.ppermute(z, 'tensor', [(i, i ^ 1 << n) for i in range(tensor)])]
    pallas_call x1, Pallas kernels: 1.68 us -> 0.16 us  [merged(): pl.pallas_call(functools.partial(merge_kernel, len(parts)), out_shape=jax...]
    another operation x1, local copies, waits for them, and re-layouts: 0.01 us -> 0.66 us  [attend(): jnp.tile(lengths, size)[:, None]]
  transfers between devices with their start and end apart: 15 -> 15, of which waited for: 6 -> 7; matrix products, arithmetic and copies ran while one was open for 5% -> 2% of each run, Pallas kernels for 16% -> 11%
where the time goes in v1:
time: 47 us; the launch traced here: 46.8 us
  starting transfers between devices  15.7 us (33%)
  waiting for transfers between devices  15.7 us (33%)
  Pallas kernels  14.4 us (31%)
  local copies, waits for them, and re-layouts  0.82 us (2%)
    ppermute x13, starting transfers between devices, exchange(): out.append(lax.ppermute(blocks[k], axis, route))  15.6 us
    ppermute x2, waiting for transfers between devices, shards(): z = lax.ppermute(z, 'tensor', [(i, i ^ 1 << n) for i in range(tensor)])  8.35 us
    ppermute x13, waiting for transfers between devices, exchange(): out.append(lax.ppermute(blocks[k], axis, route))  7.31 us
    pallas_call x1, Pallas kernels, attend(): pl.pallas_call(functools.partial(attend_kernel, count), out_shape=[chunk]...  3.77 us
    pallas_call x1, Pallas kernels, local_levels(): pl.pallas_call(functools.partial(local_kernel, count, local, rows, pipe_c...  3.32 us
    pallas_call x1, Pallas kernels, fetch(): pl.pallas_call(functools.partial(fetch_kernel, first), out_shape=jax.Shap...  3.13 us
    pallas_call x1, Pallas kernels, load(): pl.pallas_call(load_kernel, out_shape=[cache, cache, jax.ShapeDtypeStruct...  2.23 us
  transfers between devices with their start and end apart: 15, of which 7 were waited for; matrix products, arithmetic and copies ran while one was open for 2% of the time, Pallas kernels for 11%

profile of v1, /device:TPU:0, one launch (start us, length us, event | category | flops | bytes accessed | tf_op | source)
XLA Modules:
  0.0 46.8 jit_solution(12394198800110526918)
XLA Ops:
  0.0 4.0 %collective-permute-start.2 = (bf16[2,4096]{1,0:T(2,128)(2,1)}, bf16[2,4096]{1,0:T(2,128)(2,1)S(1)}, u32[]{:S(2)}, u32[]{:S(2)}) collective-permute-start(bf16[2,4096]{1,0:T(2,128)(2,1)} %refs_0_.1), channel_id=1, source_target_pairs={{0,8},{4,12},{8,0},{12,4},{1,9},{5,13},{9,1},{13,5},{2,10},{6,14},... | collective-permute-start | bytes 49160 | tf_op jit(solution)/shard_map/ppermute | solution.py:34
  4.0 1.6 %collective-permute-start.1 = (bf16[2,4096]{1,0:T(2,128)(2,1)}, bf16[2,4096]{1,0:T(2,128)(2,1)S(1)}, u32[]{:S(2)}, u32[]{:S(2)}) collective-permute-start(bf16[2,4096]{1,0:T(2,128)(2,1)} %refs_0_.1), channel_id=1, source_target_pairs={{0,4},{4,0},{8,12},{12,8},{1,5},{5,1},{9,13},{13,9},{2,6},{6,2},{1... | collective-permute-start | bytes 49160 | tf_op jit(solution)/shard_map/ppermute | solution.py:34
  5.6 0.0 collective-permute-start.3
  5.6 1.7 %collective-permute-start = (s32[2]{0:T(128)}, s32[2]{0:T(128)S(1)}, u32[]{:S(2)}, u32[]{:S(2)}) collective-permute-start(s32[2]{0:T(128)} %param.10), channel_id=1, source_target_pairs={{0,2},{2,0},{1,3},{3,1},{4,6},{6,4},{5,7},{7,5},{8,10},{10,8},{9,1... | collective-permute-start | bytes 32 | tf_op jit(solution)/shard_map/ppermute | solution.py:34
  7.3 0.7 %tile.2 = s32[16,2]{1,0:T(8,128)S(1)} broadcast(s32[2]{0:T(128)} %param.9), dimensions={1} | broadcast | bytes 136 | tf_op jit(solution)/shard_map/tile | solution.py:215
  8.0 0.1 broadcast_in_dim.7
  8.1 0.0 copy-start.1
  8.1 0.0 copy-start
  8.1 2.2 %load.1 = (bf16[2,8,512,128]{3,2,1,0:T(8,128)(2,1)S(1)}, bf16[2,8,512,128]{3,2,1,0:T(8,128)(2,1)S(1)}, bf16[2048,128]{1,0:T(8,128)(2,1)S(1)}) custom-call(bf16[2,8,512,128]{3,2,1,0:T(8,128)(2,1)} %key_hbm.1, bf16[2,8,512,128]{3,2,1,0:T(8,128)(2,1)} %value_hbm.1), custom_call_target="tpu_custom_call" | custom-call | tf_op jit(solution)/shard_map/load/pallas_call | solution.py:60
  10.3 0.0 collective-permute-done
  10.3 0.0 copy-done.1
  10.4 0.0 collective-permute-done.2.refs_2_
  10.4 0.0 collective-permute-done.1.refs_1_
  10.4 1.0 %collective-permute-done.3.refs_3_ = bf16[2,4096]{1,0:T(2,128)(2,1)S(1)} collective-permute-done((bf16[2,4096]{1,0:T(2,128)(2,1)}, bf16[2,4096]{1,0:T(2,128)(2,1)S(1)}, u32[]{:S(2)}, u32[]{:S(2)}) %collective-permute-start.3) | collective-permute-done | bytes 16416 | tf_op jit(solution)/shard_map/ppermute | solution.py:34
  11.4 0.1 broadcast_in_dim.8.len_ref
  11.4 0.0 copy-done
  11.4 3.8 %attend.1 = (bf16[80,128]{1,0:T(8,128)(2,1)S(1)}, bf16[80,128]{1,0:T(8,128)(2,1)S(1)}, bf16[80,128]{1,0:T(8,128)(2,1)S(1)}, bf16[80,128]{1,0:T(8,128)(2,1)S(1)},...) custom-call(s32[2,2]{1,0:T(2,128)S(1)} %pad_add_fusion.lang_any.lang_ref, ...), custom_call_target="tpu_custom_call" | custom-call | tf_op jit(solution)/shard_map/attend/pallas_call | solution.py:216
  15.2 0.1 collective-permute-start.4
  15.3 3.2 %collective-permute-start.5 = (bf16[80,128]{1,0:T(8,128)(2,1)S(1)}, bf16[80,128]{1,0:T(8,128)(2,1)S(1)}, u32[]{:S(2)}, u32[]{:S(2)}) collective-permute-start(bf16[80,128]{1,0:T(8,128)(2,1)S(1)} %get-tuple-element.29), channel_id=1, source_target_pairs={{0,8},{4,12},{8,0},{12,4},{1,9},{5,13},{9,1},{13,5},{2,10},{6,14},... | collective-permute-start | bytes 61448 | tf_op jit(solution)/shard_map/ppermute | solution.py:34
  18.5 1.2 %collective-permute-start.6 = (bf16[80,128]{1,0:T(8,128)(2,1)S(1)}, bf16[80,128]{1,0:T(8,128)(2,1)S(1)}, u32[]{:S(2)}, u32[]{:S(2)}) collective-permute-start(bf16[80,128]{1,0:T(8,128)(2,1)S(1)} %get-tuple-element.30), channel_id=1, source_target_pairs={{0,12},{4,8},{8,4},{12,0},{1,13},{5,9},{9,5},{13,1},{2,14},{6,10},... | collective-permute-start | bytes 61448 | tf_op jit(solution)/shard_map/ppermute | solution.py:34
  19.7 0.0 collective-permute-done.4.refs_1_
  19.7 0.6 %collective-permute-done.5.refs_2_ = bf16[80,128]{1,0:T(8,128)(2,1)S(1)} collective-permute-done((bf16[80,128]{1,0:T(8,128)(2,1)S(1)}, bf16[80,128]{1,0:T(8,128)(2,1)S(1)}, u32[]{:S(2)}, u32[]{:S(2)}) %collective-permute-start.5) | collective-permute-done | bytes 20512 | tf_op jit(solution)/shard_map/ppermute | solution.py:34
  20.2 3.8 %collective-permute-done.6.refs_3_ = bf16[80,128]{1,0:T(8,128)(2,1)S(1)} collective-permute-done((bf16[80,128]{1,0:T(8,128)(2,1)S(1)}, bf16[80,128]{1,0:T(8,128)(2,1)S(1)}, u32[]{:S(2)}, u32[]{:S(2)}) %collective-permute-start.6) | collective-permute-done | bytes 20512 | tf_op jit(solution)/shard_map/ppermute | solution.py:34
  24.1 0.2 merge.1.refs_0_
  24.2 0.1 collective-permute-start.9
  24.3 0.7 %collective-permute-start.8 = (bf16[80,128]{1,0:T(8,128)(2,1)S(1)}, bf16[80,128]{1,0:T(8,128)(2,1)S(1)}, u32[]{:S(2)}, u32[]{:S(2)}) collective-permute-start(bf16[80,128]{1,0:T(8,128)(2,1)S(1)} %merge.1.refs_0_), channel_id=1, source_target_pairs={{0,2},{1,3},{2,0},{3,1},{4,6},{5,7},{6,4},{7,5},{8,10},{9,11},{10,... | collective-permute-start | bytes 61448 | tf_op jit(solution)/shard_map/ppermute | solution.py:34
  25.0 1.1 %collective-permute-start.7 = (bf16[80,128]{1,0:T(8,128)(2,1)S(1)}, bf16[80,128]{1,0:T(8,128)(2,1)S(1)}, u32[]{:S(2)}, u32[]{:S(2)}) collective-permute-start(bf16[80,128]{1,0:T(8,128)(2,1)S(1)} %merge.1.refs_0_), channel_id=1, source_target_pairs={{0,1},{1,0},{2,3},{3,2},{4,5},{5,4},{6,7},{7,6},{8,9},{9,8},{10,11... | collective-permute-start | bytes 61448 | tf_op jit(solution)/shard_map/ppermute | solution.py:34
  26.1 3.1 %fetch.1.late_ref.far_ref = bf16[5,2,128,2048]{3,2,1,0:T(8,128)(2,1)S(1)} custom-call(s32[2,2]{1,0:T(2,128)S(1)} %pad_add_fusion.lang_any.lang_ref, bf16[80,128]{1,0:T(8,128)(2,1)S(1)} %get-tuple-element.27.after_ref.refs_0_, bf16[9,8,128,2048]{3,2,1,0:T(8,128)(2,1)} %table_hbm.1), custom_call_target="tpu_custom_call" | custom-call | tf_op jit(solution)/shard_map/fetch/pallas_call | solution.py:243
  29.3 0.0 collective-permute-done.9.refs_3_
  29.3 0.0 collective-permute-done.8.refs_2_
  29.3 0.0 collective-permute-done.7.refs_1_
  29.3 3.3 %local_levels.1 = (bf16[256,128]{1,0:T(8,128)(2,1)S(1)}, bf16[64,128]{1,0:T(8,128)(2,1)S(1)}) custom-call(s32[8,128]{1,0:T(8,128)S(1)} %get-tuple-element.24.slot_ref, bf16[2048,128]{1,0:T(8,128)(2,1)S(1)} %get-tuple-element.25.sums_ref, bf16[4,2,128,2048]{3,2,1,0:T(8,128)(2,1)S(1)} %get-tuple-element.26.near_ref, ...), custom_call_target="tpu_custom_call" | custom-call | tf_op jit(solution)/shard_map/local_levels/pallas_call | solution.py:360
  32.6 0.1 collective-permute-start.10
  32.7 3.7 %collective-permute-done.10.z_ref = bf16[64,128]{1,0:T(8,128)(2,1)S(1)} collective-permute-done((bf16[64,128]{1,0:T(8,128)(2,1)S(1)}, bf16[64,128]{1,0:T(8,128)(2,1)S(1)}, u32[]{:S(2)}, u32[]{:S(2)}) %collective-permute-start.10) | collective-permute-done | bytes 16416 | tf_op jit(solution)/shard_map/ppermute | solution.py:473
  36.5 0.6 %cross_level.1 = (bf16[256,128]{1,0:T(8,128)(2,1)S(1)}, bf16[64,128]{1,0:T(8,128)(2,1)S(1)}) custom-call(bf16[256,128]{1,0:T(8,128)(2,1)S(1)} %get-tuple-element.31.x_ref, bf16[64,128]{1,0:T(8,128)(2,1)S(1)} %collective-permute-done.10.z_ref, bf16[2048,128]{1,0:T(8,128)(2,1)S(1)} %get-tuple-element.25.sums_ref, ...), custom_call_target="tpu_custom_call" | custom-call | tf_op jit(solution)/shard_map/cross_level/pallas_call | solution.py:386
  37.0 0.1 collective-permute-start.11
  37.1 4.6 %collective-permute-done.11.z_ref = bf16[64,128]{1,0:T(8,128)(2,1)S(1)} collective-permute-done((bf16[64,128]{1,0:T(8,128)(2,1)S(1)}, bf16[64,128]{1,0:T(8,128)(2,1)S(1)}, u32[]{:S(2)}, u32[]{:S(2)}) %collective-permute-start.11) | collective-permute-done | bytes 16416 | tf_op jit(solution)/shard_map/ppermute | solution.py:473
  41.7 0.6 %last_level.1 = (bf16[32,128]{1,0:T(8,128)(2,1)S(1)}, bf16[32,128]{1,0:T(8,128)(2,1)S(1)}, bf16[32,128]{1,0:T(8,128)(2,1)S(1)}, bf16[32,128]{1,0:T(8,128)(2,1)S(1)}) custom-call(s32[8,128]{1,0:T(8,128)S(1)} %get-tuple-element.24.slot_ref, bf16[256,128]{1,0:T(8,128)(2,1)S(1)} %get-tuple-element.33.x_ref, bf16[64,128]{1,0:T(8,128)(2,1)S(1)} %collective-permute-done.11.z_ref, ...), custom_call_target="tpu_custom_call" | custom-call | tf_op jit(solution)/shard_map/last_level/pallas_call | solution.py:419
  42.3 0.0 collective-permute-start.12
  42.4 0.7 %collective-permute-start.13 = (bf16[32,128]{1,0:T(8,128)(2,1)S(1)}, bf16[32,128]{1,0:T(8,128)(2,1)S(1)}, u32[]{:S(2)}, u32[]{:S(2)}) collective-permute-start(bf16[32,128]{1,0:T(8,128)(2,1)S(1)} %get-tuple-element.37), channel_id=1, source_target_pairs={{0,2},{1,3},{2,0},{3,1},{4,6},{5,7},{6,4},{7,5},{8,10},{9,11},{10,... | collective-permute-start | bytes 24584 | tf_op jit(solution)/shard_map/ppermute | solution.py:34
  43.1 1.2 %collective-permute-start.14 = (bf16[32,128]{1,0:T(8,128)(2,1)S(1)}, bf16[32,128]{1,0:T(8,128)(2,1)S(1)}, u32[]{:S(2)}, u32[]{:S(2)}) collective-permute-start(bf16[32,128]{1,0:T(8,128)(2,1)S(1)} %get-tuple-element.38), channel_id=1, source_target_pairs={{0,3},{1,2},{2,1},{3,0},{4,7},{5,6},{6,5},{7,4},{8,11},{9,10},{10,... | collective-permute-start | bytes 24584 | tf_op jit(solution)/shard_map/ppermute | solution.py:34
  44.2 0.0 collective-permute-done.12.refs_1_
  44.3 1.8 %collective-permute-done.13.refs_2_ = bf16[32,128]{1,0:T(8,128)(2,1)S(1)} collective-permute-done((bf16[32,128]{1,0:T(8,128)(2,1)S(1)}, bf16[32,128]{1,0:T(8,128)(2,1)S(1)}, u32[]{:S(2)}, u32[]{:S(2)}) %collective-permute-start.13) | collective-permute-done | bytes 8224 | tf_op jit(solution)/shard_map/ppermute | solution.py:34
  46.1 0.1 collective-permute-done.14.refs_3_
  46.2 0.6 %pick.1 = bf16[1,4096]{1,0:T(2,128)(2,1)} custom-call(s32[8,128]{1,0:T(8,128)S(1)} %get-tuple-element.24.slot_ref, bf16[32,128]{1,0:T(8,128)(2,1)S(1)} %get-tuple-element.35.refs_0_, bf16[32,128]{1,0:T(8,128)(2,1)S(1)} %collective-permute-done.12.refs_1_, bf16[32,128]{1,0:T(8,128)(2,1)S(1)} %collective-permute-done.13.refs_2_, ...), custom_call_target="tpu_custom_call" | custom-call | tf_op jit(solution)/shard_map/pick/pallas_call | solution.py:443
  (1 shorter events, 0.0 us)
Async XLA Ops:
  0.0 10.4 %collective-permute-start.2 = (bf16[2,4096]{1,0:T(2,128)(2,1)}, bf16[2,4096]{1,0:T(2,128)(2,1)S(1)}, u32[]{:S(2)}, u32[]{:S(2)}) collective-permute-start(bf16[2,4096]{1,0:T(2,128)(2,1)} %refs_0_.1), channel_id=1, source_target_pairs={{0,8},{4,12},{8,0},{12,4},{1,9},{5,13},{9,1},{13,5},{2,10},{6,14},... | collective-permute-start | bytes 49160 | tf_op jit(solution)/shard_map/ppermute | solution.py:34
  4.0 6.3 %collective-permute-start.1 = (bf16[2,4096]{1,0:T(2,128)(2,1)}, bf16[2,4096]{1,0:T(2,128)(2,1)S(1)}, u32[]{:S(2)}, u32[]{:S(2)}) collective-permute-start(bf16[2,4096]{1,0:T(2,128)(2,1)} %refs_0_.1), channel_id=1, source_target_pairs={{0,4},{4,0},{8,12},{12,8},{1,5},{5,1},{9,13},{13,9},{2,6},{6,2},{1... | collective-permute-start | bytes 49160 | tf_op jit(solution)/shard_map/ppermute | solution.py:34
  5.6 5.7 %collective-permute-start.3 = (bf16[2,4096]{1,0:T(2,128)(2,1)}, bf16[2,4096]{1,0:T(2,128)(2,1)S(1)}, u32[]{:S(2)}, u32[]{:S(2)}) collective-permute-start(bf16[2,4096]{1,0:T(2,128)(2,1)} %refs_0_.1), channel_id=1, source_target_pairs={{0,12},{4,8},{8,4},{12,0},{1,13},{5,9},{9,5},{13,1},{2,14},{6,10},... | collective-permute-start | bytes 49160 | tf_op jit(solution)/shard_map/ppermute | solution.py:34
  5.6 4.7 %collective-permute-start = (s32[2]{0:T(128)}, s32[2]{0:T(128)S(1)}, u32[]{:S(2)}, u32[]{:S(2)}) collective-permute-start(s32[2]{0:T(128)} %param.10), channel_id=1, source_target_pairs={{0,2},{2,0},{1,3},{3,1},{4,6},{6,4},{5,7},{7,5},{8,10},{10,8},{9,1... | collective-permute-start | bytes 32 | tf_op jit(solution)/shard_map/ppermute | solution.py:34
  8.1 2.3 %copy-start.1 = (s32[2]{0:T(128)S(1)}, s32[2]{0:T(128)}, u32[]{:S(2)}) copy-start(s32[2]{0:T(128)} %param.10) | copy-start | bytes 28
  8.1 3.3 %copy-start = (bf16[2,4096]{1,0:T(2,128)(2,1)S(1)}, bf16[2,4096]{1,0:T(2,128)(2,1)}, u32[]{:S(2)}) copy-start(bf16[2,4096]{1,0:T(2,128)(2,1)} %refs_0_.1) | copy-start | bytes 49156
  15.2 4.5 %collective-permute-start.4 = (bf16[80,128]{1,0:T(8,128)(2,1)S(1)}, bf16[80,128]{1,0:T(8,128)(2,1)S(1)}, u32[]{:S(2)}, u32[]{:S(2)}) collective-permute-start(bf16[80,128]{1,0:T(8,128)(2,1)S(1)} %get-tuple-element.28), channel_id=1, source_target_pairs={{0,4},{4,0},{8,12},{12,8},{1,5},{5,1},{9,13},{13,9},{2,6},{6,2},{1... | collective-permute-start | bytes 61448 | tf_op jit(solution)/shard_map/ppermute | solution.py:34
  15.3 4.9 %collective-permute-start.5 = (bf16[80,128]{1,0:T(8,128)(2,1)S(1)}, bf16[80,128]{1,0:T(8,128)(2,1)S(1)}, u32[]{:S(2)}, u32[]{:S(2)}) collective-permute-start(bf16[80,128]{1,0:T(8,128)(2,1)S(1)} %get-tuple-element.29), channel_id=1, source_target_pairs={{0,8},{4,12},{8,0},{12,4},{1,9},{5,13},{9,1},{13,5},{2,10},{6,14},... | collective-permute-start | bytes 61448 | tf_op jit(solution)/shard_map/ppermute | solution.py:34
  18.5 5.6 %collective-permute-start.6 = (bf16[80,128]{1,0:T(8,128)(2,1)S(1)}, bf16[80,128]{1,0:T(8,128)(2,1)S(1)}, u32[]{:S(2)}, u32[]{:S(2)}) collective-permute-start(bf16[80,128]{1,0:T(8,128)(2,1)S(1)} %get-tuple-element.30), channel_id=1, source_target_pairs={{0,12},{4,8},{8,4},{12,0},{1,13},{5,9},{9,5},{13,1},{2,14},{6,10},... | collective-permute-start | bytes 61448 | tf_op jit(solution)/shard_map/ppermute | solution.py:34
  24.2 5.1 %collective-permute-start.9 = (bf16[80,128]{1,0:T(8,128)(2,1)S(1)}, bf16[80,128]{1,0:T(8,128)(2,1)S(1)}, u32[]{:S(2)}, u32[]{:S(2)}) collective-permute-start(bf16[80,128]{1,0:T(8,128)(2,1)S(1)} %merge.1.refs_0_), channel_id=1, source_target_pairs={{0,3},{1,2},{2,1},{3,0},{4,7},{5,6},{6,5},{7,4},{8,11},{9,10},{10,... | collective-permute-start | bytes 61448 | tf_op jit(solution)/shard_map/ppermute | solution.py:34
  24.3 5.0 %collective-permute-start.8 = (bf16[80,128]{1,0:T(8,128)(2,1)S(1)}, bf16[80,128]{1,0:T(8,128)(2,1)S(1)}, u32[]{:S(2)}, u32[]{:S(2)}) collective-permute-start(bf16[80,128]{1,0:T(8,128)(2,1)S(1)} %merge.1.refs_0_), channel_id=1, source_target_pairs={{0,2},{1,3},{2,0},{3,1},{4,6},{5,7},{6,4},{7,5},{8,10},{9,11},{10,... | collective-permute-start | bytes 61448 | tf_op jit(solution)/shard_map/ppermute | solution.py:34
  25.0 4.3 %collective-permute-start.7 = (bf16[80,128]{1,0:T(8,128)(2,1)S(1)}, bf16[80,128]{1,0:T(8,128)(2,1)S(1)}, u32[]{:S(2)}, u32[]{:S(2)}) collective-permute-start(bf16[80,128]{1,0:T(8,128)(2,1)S(1)} %merge.1.refs_0_), channel_id=1, source_target_pairs={{0,1},{1,0},{2,3},{3,2},{4,5},{5,4},{6,7},{7,6},{8,9},{9,8},{10,11... | collective-permute-start | bytes 61448 | tf_op jit(solution)/shard_map/ppermute | solution.py:34
  32.6 3.8 %collective-permute-start.10 = (bf16[64,128]{1,0:T(8,128)(2,1)S(1)}, bf16[64,128]{1,0:T(8,128)(2,1)S(1)}, u32[]{:S(2)}, u32[]{:S(2)}) collective-permute-start(bf16[64,128]{1,0:T(8,128)(2,1)S(1)} %get-tuple-element.32), channel_id=1, source_target_pairs={{0,4},{4,0},{8,12},{12,8},{1,5},{5,1},{9,13},{13,9},{2,6},{6,2},{1... | collective-permute-start | bytes 49160 | tf_op jit(solution)/shard_map/ppermute | solution.py:473
  37.0 4.7 %collective-permute-start.11 = (bf16[64,128]{1,0:T(8,128)(2,1)S(1)}, bf16[64,128]{1,0:T(8,128)(2,1)S(1)}, u32[]{:S(2)}, u32[]{:S(2)}) collective-permute-start(bf16[64,128]{1,0:T(8,128)(2,1)S(1)} %get-tuple-element.34), channel_id=1, source_target_pairs={{0,8},{4,12},{8,0},{12,4},{1,9},{5,13},{9,1},{13,5},{2,10},{6,14},... | collective-permute-start | bytes 49160 | tf_op jit(solution)/shard_map/ppermute | solution.py:473
  42.3 1.9 %collective-permute-start.12 = (bf16[32,128]{1,0:T(8,128)(2,1)S(1)}, bf16[32,128]{1,0:T(8,128)(2,1)S(1)}, u32[]{:S(2)}, u32[]{:S(2)}) collective-permute-start(bf16[32,128]{1,0:T(8,128)(2,1)S(1)} %get-tuple-element.36), channel_id=1, source_target_pairs={{0,1},{1,0},{2,3},{3,2},{4,5},{5,4},{6,7},{7,6},{8,9},{9,8},{10,11... | collective-permute-start | bytes 24584 | tf_op jit(solution)/shard_map/ppermute | solution.py:34
  42.4 3.7 %collective-permute-start.13 = (bf16[32,128]{1,0:T(8,128)(2,1)S(1)}, bf16[32,128]{1,0:T(8,128)(2,1)S(1)}, u32[]{:S(2)}, u32[]{:S(2)}) collective-permute-start(bf16[32,128]{1,0:T(8,128)(2,1)S(1)} %get-tuple-element.37), channel_id=1, source_target_pairs={{0,2},{1,3},{2,0},{3,1},{4,6},{5,7},{6,4},{7,5},{8,10},{9,11},{10,... | collective-permute-start | bytes 24584 | tf_op jit(solution)/shard_map/ppermute | solution.py:34
  43.1 3.1 %collective-permute-start.14 = (bf16[32,128]{1,0:T(8,128)(2,1)S(1)}, bf16[32,128]{1,0:T(8,128)(2,1)S(1)}, u32[]{:S(2)}, u32[]{:S(2)}) collective-permute-start(bf16[32,128]{1,0:T(8,128)(2,1)S(1)} %get-tuple-element.38), channel_id=1, source_target_pairs={{0,3},{1,2},{2,1},{3,0},{4,7},{5,6},{6,5},{7,4},{8,11},{9,10},{10,... | collective-permute-start | bytes 24584 | tf_op jit(solution)/shard_map/ppermute | solution.py:34

commit v2 on v1

v2 whole, which is shorter than its diff:
```python
import functools
import math

import jax
import jax.numpy as jnp
from jax import lax
from jax.experimental import pallas as pl
from jax.experimental.pallas import tpu as pltpu
from jax.sharding import PartitionSpec as P

HQ = 128
KVH = 8
HD = 128
B = 64
HALF = B // 2
LANES = 128
SLOTS = 2
GROUP = HQ // KVH
WIDE = HALF * B
NEG = -1e30
FLOOR = -1e29
FIRST = 3
STATS = 16

VMEM = pl.BlockSpec(memory_space=pltpu.VMEM)
SMEM = pl.BlockSpec(memory_space=pltpu.SMEM)
HBM = pl.BlockSpec(memory_space=pltpu.HBM)
ANY = pl.BlockSpec(memory_space=pl.ANY)


def exchange(blocks, axis, count):
    out = [blocks[0]]
    for k in range(1, count):
        route = [(i, i ^ k) for i in range(count)]
        out.append(lax.ppermute(blocks[k], axis, route))
    return out


def by_parity(tensor):
    return HQ // tensor >= GROUP


def half_of(index, tensor):
    if by_parity(tensor):
        half = index
        for n in range(1, (tensor - 1).bit_length()):
            half = half ^ (index >> n)
        return half & 1
    return index // (tensor // 2)


def reach_of(i, p, tensor):
    if by_parity(tensor):
        return (i << 1) | (half_of(i, tensor) ^ p)
    return p * (tensor // 2) + i


def place_of(shard, tensor):
    return shard >> 1 if by_parity(tensor) else shard % (tensor // 2)


def cores_exchange(blocks, tensor):
    out = []
    for i, block in enumerate(blocks):
        route = [(2 * t + p, 2 * (t ^ reach_of(i, p, tensor)) + p) for t in range(tensor) for p in range(2)]
        out.append(lax.ppermute(block, ("tensor", "pipe"), route))
    return out


def iota(shape, dim):
    return lax.broadcasted_iota(jnp.int32, shape, dim)


def start_half(flip, src_hbm, dst_ref, sems):
    rows = dst_ref.shape[0]
    tensor = lax.axis_size("tensor")
    half = half_of(lax.axis_index("tensor"), tensor) ^ lax.axis_index("pipe") ^ flip
    size = HQ // tensor // GROUP if by_parity(tensor) else KVH // 2
    copies = []
    for r in range(rows):
        for j in range(KVH // 2 // size):
            src = pl.ds(reach_of(j, half, tensor) * size if by_parity(tensor) else half * size, size)
            copy = pltpu.make_async_copy(src_hbm.at[r, src], dst_ref.at[r, pl.ds(j * size, size)], sems.at[r, j])
            copy.start()
            copies.append(copy)
    return copies


def send_kernel(*refs):
    caches, outs, sems = refs[:2], refs[2:4], refs[4]
    copies = []
    for n in range(2):
        copies += start_half(1, caches[n], outs[n], sems.at[n])
    for copy in copies:
        copy.wait()


def send_halves(key_cache, value_cache):
    rows, _, span, _ = key_cache.shape
    half = jax.ShapeDtypeStruct((rows, KVH // 2, span, HD), key_cache.dtype)
    return pl.pallas_call(
        send_kernel,
        out_shape=[half, half],
        in_specs=[HBM, HBM],
        out_specs=[VMEM, VMEM],
        scratch_shapes=[pltpu.SemaphoreType.DMA((2, rows, KVH // 2))],
        compiler_params=pltpu.CompilerParams(vmem_limit_bytes=8 << 20),
        name="send_halves",
    )(key_cache, value_cache)


def slots_of(lang_refs, rows, share):
    home = holder()
    d = lax.axis_index("dp")
    found = jnp.int32(0)
    row_ids = [jnp.int32(-1)] * SLOTS
    langs = [jnp.int32(0)] * SLOTS
    for k, lang_ref in enumerate(lang_refs):
        for i in range(rows):
            lang = lang_ref[i]
            mine = lang // share == home
            for s in range(SLOTS):
                take = mine & (found == s)
                row_ids[s] = jnp.where(take, (d ^ k) * rows + i, row_ids[s])
                langs[s] = jnp.where(take, lang - home * share, langs[s])
            found = found + mine.astype(jnp.int32)
    return row_ids, langs


def holder():
    return lax.axis_index(("dp", "pipe"))


def start_tables(first, langs, table_hbm, table_ref, sems):
    copies = []
    for k in range(table_ref.shape[0]):
        for s in range(SLOTS):
            copy = pltpu.make_async_copy(table_hbm.at[first + k, langs[s]], table_ref.at[k, s], sems.at[k, s])
            copy.start()
            copies.append(copy)
    return copies


def own_kernel(count, *refs):
    q_refs, (key_hbm, value_hbm) = refs[:count], refs[count:count + 2]
    wide_ref, score_ref, value_ref, sums_ref, key_buf, sems = refs[count + 2:]
    key_copies = start_half(0, key_hbm, key_buf, sems.at[0])
    value_copies = start_half(0, value_hbm, value_ref, sems.at[1])
    rows = q_refs[0].shape[0]
    chunks, tall, _ = wide_ref.shape
    size = tall // rows
    sums_ref[...] = one_hot(iota(sums_ref.shape, 0) // B == iota(sums_ref.shape, 1) % HALF)
    which = iota((tall, HD), 0) % rows
    wide = []
    for n in range(chunks):
        k, c = divmod(n, chunks // count)
        q = jnp.concatenate(
            [q_refs[k][:, h * HD:(h + 1) * HD] for h in range(c * size, (c + 1) * size)], axis=0
        )
        q = jnp.concatenate([jnp.where(which == r, q, jnp.zeros_like(q)) for r in range(rows)], axis=1)
        wide_ref[n] = q
        wide.append(q)
    for copy in key_copies:
        copy.wait()
    for n in range(chunks):
        score_ref[n] = scores_of(wide[n], key_buf, group_of(n, chunks, count, size))
    for copy in value_copies:
        copy.wait()


def beside(ref, group):
    return jnp.concatenate([ref[r, group] for r in range(ref.shape[0])], axis=1)


def scores_of(wide, key_ref, group):
    return lax.dot_general(
        wide, beside(key_ref, group), (((1,), (1,)), ((), ())), preferred_element_type=jnp.float32
    )


def group_of(n, chunks, count, size):
    k, c = divmod(n, chunks // count)
    tensor = 2 * count
    shard = lax.axis_index("tensor") ^ reach_of(k, lax.axis_index("pipe"), tensor)
    return (place_of(shard, tensor) * (HQ // tensor) + c * size) // GROUP


def attend_own(queries, key_cache, value_cache):
    count = len(queries)
    rows, width = queries[0].shape
    share = width // HD
    size = min(GROUP, share)
    span = key_cache.shape[2]
    chunks, tall = count * share // size, size * rows
    half = (rows, KVH // 2, span, HD)
    return pl.pallas_call(
        functools.partial(own_kernel, count),
        out_shape=[
            jax.ShapeDtypeStruct((chunks, tall, rows * HD), jnp.bfloat16),
            jax.ShapeDtypeStruct((chunks, tall, span), jnp.float32),
            jax.ShapeDtypeStruct(half, jnp.bfloat16),
            jax.ShapeDtypeStruct((WIDE, LANES), jnp.bfloat16),
        ],
        in_specs=[VMEM] * count + [HBM] * 2,
        out_specs=[VMEM] * 4,
        scratch_shapes=[
            pltpu.VMEM(half, jnp.bfloat16),
            pltpu.SemaphoreType.DMA((2, rows, KVH // 2)),
        ],
        compiler_params=pltpu.CompilerParams(vmem_limit_bytes=16 << 20),
        cost_estimate=pl.CostEstimate(flops=int(2e10), bytes_accessed=1 << 22, transcendentals=0),
        name="attend_own",
    )(*queries, key_cache, value_cache)


def attend_kernel(count, near, lang_share, *refs):
    scalars, refs = refs[:near + 1], refs[near + 1:]
    wide_ref, score_ref, own_value_ref, key_ref, value_ref = refs[:5]
    out_refs, (slot_ref, lang_ref, lang_sems) = refs[5:count + 5], refs[count + 5:]
    lang_copies = [
        pltpu.make_async_copy(src, lang_ref.at[k], lang_sems.at[k]) for k, src in enumerate(scalars)
    ]
    for copy in lang_copies:
        copy.start()
    rows, _, span, _ = key_ref.shape
    chunks, tall, _ = wide_ref.shape
    size = tall // rows
    share = size * (chunks // count)
    t, p = lax.axis_index("tensor"), lax.axis_index("pipe")
    other = [
        scores_of(wide_ref[n], key_ref, group_of(n, chunks, count, size)) for n in range(chunks)
    ]
    for copy in lang_copies:
        copy.wait()
    row_ids, langs = slots_of([lang_ref.at[k] for k in range(near)], rows, lang_share)
    row = iota(slot_ref.shape, 0)
    own = lang_ref[0, p] // lang_share
    slots = jnp.where(row == SLOTS, own ^ holder(), -1)
    for s in range(SLOTS):
        slots = jnp.where(row == s, row_ids[s], slots)
        slots = jnp.where(row == SLOTS + 1 + s, langs[s], slots)
    slot_ref[...] = slots

    block = share * rows
    spot = iota((tall, LANES), 1) % block - iota((tall, LANES), 0)
    tops, totals = [0.0] * count, [0.0] * count
    place = iota((tall, 2 * span), 1)
    start = jnp.where(place < span, p, (1 ^ p) - 1) + 2 * t
    which = iota((tall, 2 * span), 0) % rows
    length = lang_ref[near, 0]
    for r in range(1, rows):
        length = jnp.where(which == r, lang_ref[near, r], length)
    visible = start * span + place < length
    for n in range(chunks):
        k, c = divmod(n, chunks // count)
        group = group_of(n, chunks, count, size)
        scores = jnp.concatenate([score_ref[n], other[n]], axis=1)
        scores = jnp.where(visible, scores * (1.0 / math.sqrt(HD)), NEG)
        top = jnp.maximum(jnp.max(scores, axis=1, keepdims=True), FLOOR)
        top = top.astype(jnp.bfloat16).astype(jnp.float32)
        weights = jnp.exp(scores - top)
        total = jnp.sum(weights, axis=1, keepdims=True)
        weights = weights.astype(jnp.bfloat16)
        both = sum(
            jnp.dot(
                weights[:, side * span:(side + 1) * span],
                beside(values, group),
                preferred_element_type=jnp.float32,
            )
            for side, values in enumerate((own_value_ref, value_ref))
        )
        which = iota((tall, LANES), 0) % rows
        weighted = both[:, :HD]
        for r in range(1, rows):
            weighted = jnp.where(which == r, both[:, r * HD:(r + 1) * HD], weighted)
        out_refs[k][c * tall:(c + 1) * tall] = weighted.astype(jnp.bfloat16)
        here = spot == c * tall
        tops[k] = tops[k] + jnp.sum(jnp.where(here, top, 0.0), axis=0, keepdims=True)
        totals[k] = totals[k] + jnp.sum(jnp.where(here, total, 0.0), axis=0, keepdims=True)
    for k in range(count):
        out_refs[k][block:] = stats(tops[k], totals[k])


def stats(top, total):
    coarse = total.astype(jnp.bfloat16).astype(jnp.float32)
    row = iota((STATS, LANES), 0)
    out = jnp.where(row == 0, top, jnp.where(row == 1, coarse, jnp.where(row == 2, total - coarse, 0.0)))
    return out.astype(jnp.bfloat16)


def factors(parts):
    tops, totals = [], []
    for part in parts:
        rows = part[part.shape[0] - STATS:].astype(jnp.float32)
        tops.append(rows[0:1])
        totals.append(rows[1:2] + rows[2:3])
    peak = functools.reduce(jnp.maximum, tops)
    scale = [jnp.exp(top - peak) for top in tops]
    return scale, peak, sum(f * total for f, total in zip(scale, totals))


def weigh(scale, mask, block):
    coarse = scale.astype(jnp.bfloat16).astype(jnp.float32)
    side = iota((1, LANES), 1) // block
    both = jnp.where(side == 0, coarse, jnp.where(side == 1, scale - coarse, 0.0))
    return jnp.where(mask, both, 0.0).astype(jnp.bfloat16)


def stacked(parts, block):
    return jnp.concatenate([part[:block] for part in parts for _ in range(LANES // block)], axis=0)


def attend(langs, lengths, wide, scores, own_value, key, value, count, lang_share):
    near = len(langs)
    chunks, tall, _ = wide.shape
    rows = key.shape[0]
    chunk = jax.ShapeDtypeStruct((chunks // count * tall + STATS, LANES), jnp.bfloat16)
    return pl.pallas_call(
        functools.partial(attend_kernel, count, near, lang_share),
        out_shape=[chunk] * count + [jax.ShapeDtypeStruct((8, LANES), jnp.int32)],
        in_specs=[ANY] * (near + 1) + [VMEM] * 5,
        out_specs=[VMEM] * (count + 1),
        scratch_shapes=[
            pltpu.SMEM((near + 1, rows), jnp.int32),
            pltpu.SemaphoreType.DMA((near + 1,)),
        ],
        compiler_params=pltpu.CompilerParams(vmem_limit_bytes=16 << 20),
        name="attend",
    )(*langs, lengths, wide, scores, own_value, key, value)


def fetch_kernel(first, slot_ref, _, table_hbm, table_ref, sems):
    places = slot_ref[SLOTS + 1:2 * SLOTS + 1].astype(jnp.float32)
    langs = [jnp.max(places[s:s + 1]).astype(jnp.int32) for s in range(SLOTS)]
    for copy in start_tables(first, langs, table_hbm, table_ref, sems):
        copy.wait()


def fetch(slots, after, adapter, first, count):
    _, _, stretch, wide = adapter.shape
    return pl.pallas_call(
        functools.partial(fetch_kernel, first),
        out_shape=jax.ShapeDtypeStruct((count, SLOTS, stretch, wide), jnp.bfloat16),
        in_specs=[VMEM, ANY, HBM],
        out_specs=VMEM,
        scratch_shapes=[pltpu.SemaphoreType.DMA((count, SLOTS))],
        compiler_params=pltpu.CompilerParams(vmem_limit_bytes=16 << 20),
        name="fetch",
    )(slots, after, adapter)


def merge_kernel(count, *refs):
    out = refs[-1]
    parts = [refs[k][...] for k in range(count)]
    block = out.shape[0] - STATS
    scale, peak, total = factors(parts)
    mask = iota((block, LANES), 1) % block == iota((block, LANES), 0)
    matrix = jnp.concatenate([weigh(f, mask, block) for f in scale], axis=1)
    weighted = jnp.dot(matrix, stacked(parts, block), preferred_element_type=jnp.float32)
    out[:block] = weighted.astype(jnp.bfloat16)
    out[block:] = stats(peak, total)


def merged(parts, after):
    return pl.pallas_call(
        functools.partial(merge_kernel, len(parts)),
        out_shape=jax.ShapeDtypeStruct(parts[0].shape, parts[0].dtype),
        in_specs=[VMEM] * len(parts) + [ANY],
        out_specs=VMEM,
        compiler_params=pltpu.CompilerParams(vmem_limit_bytes=8 << 20),
        name="merge",
    )(*parts, after)


def one_hot(cond):
    return jnp.where(cond, 1.0, 0.0).astype(jnp.bfloat16)


def level(own, partner, upper, table, sums):
    lane_upper = iota(own.shape, 1) // HALF % 2
    paired = jnp.where(lane_upper == upper, own, partner).astype(jnp.bfloat16)
    products = jnp.concatenate(
        [table[:, c * LANES:(c + 1) * LANES] * paired for c in range(WIDE // LANES)], axis=1
    )
    y = jnp.dot(products, sums, preferred_element_type=jnp.float32)
    return y.astype(jnp.bfloat16).astype(jnp.float32)


def packed(x):
    quarter = x.shape[0] // 4
    block = iota((quarter, LANES), 1) // HALF
    out = x[0:quarter]
    for n in range(1, 4):
        out = jnp.where(block == n, x[n * quarter:(n + 1) * quarter], out)
    return out.astype(jnp.bfloat16)


def unpacked(z):
    row, col = iota((LANES, LANES), 0), iota((LANES, LANES), 1)
    return jnp.concatenate(
        [
            jnp.dot(z, one_hot(row == n * HALF + col % HALF), preferred_element_type=jnp.float32)
            for n in range(4)
        ],
        axis=0,
    )


def local_kernel(count, groups, local, rows, pipe_count, slot_ref, sums_ref, *refs):
    tables, parts, (x_ref, z_ref) = refs[:groups], refs[groups:groups + count], refs[groups + count:]
    stretch = tables[0].shape[2]
    near = count // pipe_count
    block = parts[0].shape[0] - STATS
    per_head = HD // HALF
    d = lax.axis_index("dp")
    parts = [part[...] for part in parts]
    shape = (stretch, LANES)
    lane = iota(shape, 1) % block
    same_head = iota(shape, 0) // per_head == lane // rows
    place = iota(shape, 1) // HALF == iota(shape, 0) % per_head
    spread = one_hot(iota((LANES, LANES), 0) % HALF == iota((LANES, LANES), 1) % HALF)
    columns = [[] for _ in range(SLOTS)]
    for k in range(near):
        pair = parts[k * pipe_count:(k + 1) * pipe_count]
        scale, _, total = factors(pair)
        row = (d ^ k) * rows + lane % rows
        for s in range(SLOTS):
            mask = same_head & (row == slot_ref[s:s + 1])
            columns[s] += [weigh(f / total, mask, block) for f in scale]
    matrix = jnp.concatenate([jnp.concatenate(c, axis=1) for c in columns], axis=0)
    tall = jnp.dot(matrix, stacked(parts, block), preferred_element_type=jnp.float32)
    place = jnp.concatenate([place] * SLOTS, axis=0)
    tall = jnp.where(place, tall, 0.0).astype(jnp.bfloat16)
    xs = [
        jnp.dot(tall[s * stretch:(s + 1) * stretch], spread, preferred_element_type=jnp.float32)
        for s in range(SLOTS)
    ]
    index = iota(shape, 0)
    sums = sums_ref[...]
    for k in range(local):
        reach = 1 << k
        upper = index // reach % 2
        table, at = table_of(tables, k)
        for s in range(SLOTS):
            ahead = jnp.roll(xs[s], -reach, axis=0)
            behind = jnp.roll(xs[s], reach, axis=0)
            partner = jnp.where(upper == 0, ahead, behind)
            xs[s] = level(xs[s], partner, upper, table.at[at, s], sums)
    x = jnp.concatenate(xs, axis=0)
    x_ref[...] = x.astype(jnp.bfloat16)
    z_ref[...] = packed(x)


def table_of(tables, k):
    for table in tables:
        if k < table.shape[0]:
            return table, k
        k -= table.shape[0]


def local_levels(slots, parts, sums, tables, local, rows, pipe_count):
    stretch = tables[0].shape[2]
    count = len(parts)
    shape = (SLOTS * stretch, LANES)
    return pl.pallas_call(
        functools.partial(local_kernel, count, len(tables), local, rows, pipe_count),
        out_shape=[
            jax.ShapeDtypeStruct(shape, jnp.bfloat16),
            jax.ShapeDtypeStruct((shape[0] // 4, LANES), jnp.bfloat16),
        ],
        in_specs=[VMEM] * (count + len(tables) + 2),
        out_specs=[VMEM] * 2,
        compiler_params=pltpu.CompilerParams(vmem_limit_bytes=24 << 20),
        name="local_levels",
    )(slots, sums, *tables, *parts)


def far_level(bit, n, x_ref, z_ref, sums_ref, far_ref):
    upper = lax.axis_index("tensor") // (1 << bit) % 2
    partner = unpacked(z_ref[...])
    stretch = x_ref.shape[0] // SLOTS
    sums = sums_ref[...]
    out = []
    for s in range(SLOTS):
        part = slice(s * stretch, (s + 1) * stretch)
        out.append(level(x_ref[part].astype(jnp.float32), partner[part], upper, far_ref.at[n, s], sums))
    return jnp.concatenate(out, axis=0)


def cross_kernel(bit, n, x_ref, z_ref, sums_ref, far_ref, x_out, z_out):
    x = far_level(bit, n, x_ref, z_ref, sums_ref, far_ref)
    x_out[...] = x.astype(jnp.bfloat16)
    z_out[...] = packed(x)


def cross_level(x, z, sums, far, bit, n):
    return pl.pallas_call(
        functools.partial(cross_kernel, bit, n),
        out_shape=[
            jax.ShapeDtypeStruct(x.shape, x.dtype),
            jax.ShapeDtypeStruct(z.shape, z.dtype),
        ],
        in_specs=[VMEM] * 4,
        out_specs=[VMEM] * 2,
        compiler_params=pltpu.CompilerParams(vmem_limit_bytes=32 << 20),
        name="cross_level",
    )(x, z, sums, far)


def last_kernel(bit, n, count, slot_ref, x_ref, z_ref, sums_ref, far_ref, *outs):
    x = far_level(bit, n, x_ref, z_ref, sums_ref, far_ref)
    stretch = x.shape[0] // SLOTS
    per_head = HD // HALF
    heads = stretch // per_head
    lower = one_hot(iota((heads, stretch), 1) // per_head == iota((heads, stretch), 0))
    place = iota((stretch, LANES), 1) // HALF == iota((stretch, LANES), 0) % per_head
    home = holder()
    flat = []
    for s in range(SLOTS):
        tall = jnp.where(place, x[s * stretch:(s + 1) * stretch], 0.0).astype(jnp.bfloat16)
        flat.append(jnp.dot(lower, tall, preferred_element_type=jnp.float32))
    for k in range(count):
        second = slot_ref[1:2] == (home ^ k)
        outs[k][...] = jnp.where(second, flat[1], flat[0]).astype(jnp.bfloat16)


def last_level(slots, x, z, sums, far, bit, n, count):
    stretch = x.shape[0] // SLOTS
    heads = stretch * HALF // HD
    return pl.pallas_call(
        functools.partial(last_kernel, bit, n, count),
        out_shape=[jax.ShapeDtypeStruct((heads, HD), jnp.bfloat16)] * count,
        in_specs=[VMEM] * 5,
        out_specs=[VMEM] * count,
        compiler_params=pltpu.CompilerParams(vmem_limit_bytes=32 << 20),
        name="last_level",
    )(slots, x, z, sums, far)


def pick_kernel(count, slot_ref, *refs):
    parts, out = refs[:count], refs[count]
    which = slot_ref[SLOTS:SLOTS + 1]
    row = parts[0][...].astype(jnp.float32)
    for k in range(1, count):
        row = jnp.where(which == k, parts[k][...].astype(jnp.float32), row)
    row = row.astype(jnp.bfloat16)
    for h in range(row.shape[0]):
        out[0:1, h * HD:(h + 1) * HD] = row[h:h + 1]


def picked(slots, parts):
    heads = parts[0].shape[0]
    count = len(parts)
    return pl.pallas_call(
        functools.partial(pick_kernel, count),
        out_shape=jax.ShapeDtypeStruct((1, heads * HD), jnp.bfloat16),
        in_specs=[VMEM] * (count + 1),
        out_specs=VMEM,
        compiler_params=pltpu.CompilerParams(vmem_limit_bytes=8 << 20),
        name="pick",
    )(slots, *parts)


def shards(queries, key_cache, value_cache, lengths, languages, adapter):
    tensor, near, pipe = (lax.axis_size(a) for a in ("tensor", "dp", "pipe"))
    rows = queries.shape[0]
    holders = near * pipe
    levels, lang_share, stretch, _ = adapter.shape
    local = stretch.bit_length() - 1
    caches = [pltpu.with_memory_space_constraint(c, pltpu.HBM) for c in (key_cache, value_cache)]
    swap = [(0, 1), (1, 0)]
    sent = send_halves(*caches)
    other = [lax.ppermute(half, "pipe", swap) for half in sent]
    later, _ = lax.optimization_barrier((languages, sent[0]))
    langs = exchange([later] * near, "dp", near)
    spread = cores_exchange([queries] * (tensor // 2), tensor)
    wide, scores, own_value, sums = attend_own(spread, *caches)
    *parts, slots = attend(
        langs, lengths, wide, scores, own_value, *other, tensor // 2, lang_share
    )
    first = fetch(slots, parts[0], adapter, 0, FIRST)
    part = merged(cores_exchange(parts, tensor), first)
    second = fetch(slots, part, adapter, FIRST, local - FIRST)
    parts = exchange([part] * holders, ("dp", "pipe"), holders)
    x, z = local_levels(slots, parts, sums, (first, second), local, rows, pipe)
    far = fetch(slots, z, adapter, local, levels - local)
    for n in range(levels - local):
        z = lax.ppermute(z, "tensor", [(i, i ^ (1 << n)) for i in range(tensor)])
        if n < levels - local - 1:
            x, z = cross_level(x, z, sums, far, n, n)
        else:
            outs = last_level(slots, x, z, sums, far, n, n, holders)
    outs = exchange(outs, ("dp", "pipe"), holders)
    return picked(slots, outs)


def solution(mesh):
    in_specs = (
        P(("parts", "dp"), "tensor"),
        P(("parts", "dp"), None, ("tensor", "pipe"), None),
        P(("parts", "dp"), None, ("tensor", "pipe"), None),
        P(("parts", "dp")),
        P(("parts", "dp")),
        P(None, ("dp", "pipe"), "tensor", None),
    )
    out_specs = P(("parts", "dp", "pipe"), "tensor")
    return jax.shard_map(shards, mesh=mesh, in_specs=in_specs, out_specs=out_specs, check_vma=False)
```

time: 47 us -> 41.4 us (0.88)
  waiting for transfers between devices: 15.7 us -> 9.73 us
  local copies, waits for them, and re-layouts: 0.82 us -> 0.01 us
  Pallas kernels: 14.4 us -> 15.1 us
  starting transfers between devices: 15.7 us -> 16.2 us
    ppermute x13 -> x7, starting transfers between devices: 15.6 us -> 5.26 us  [exchange(): out.append(lax.ppermute(blocks[k], axis, route))]
    ppermute x0 -> x6, starting transfers between devices: none -> 7.81 us  [the longest x4 7.35 us: cores_exchange(): out.append(lax.ppermute(block, ('tensor', 'pipe'), route))]
    ppermute x2, waiting for transfers between devices: 8.35 us -> 3.72 us  [shards(): z = lax.ppermute(z, 'tensor', [(i, i ^ 1 << n) for i in range(tensor)])]
    ppermute x13 -> x7, waiting for transfers between devices: 7.31 us -> 2.7 us  [exchange(): out.append(lax.ppermute(blocks[k], axis, route))]
    ppermute x0 -> x6, waiting for transfers between devices: none -> 3.31 us  [the longest x4 2.7 us: cores_exchange(): out.append(lax.ppermute(block, ('tensor', 'pipe'), route))]
    ppermute x2, starting transfers between devices: 0.14 us -> 3.11 us  [shards(): z = lax.ppermute(z, 'tensor', [(i, i ^ 1 << n) for i in range(tensor)])]
    pallas_call x1 -> x3, Pallas kernels: 3.13 us -> 6.01 us  [fetch(): pl.pallas_call(functools.partial(fetch_kernel, first), out_shape=jax.Shap...]
    pallas_call x3 -> x4, Pallas kernels: 9.32 us -> 7.15 us  [the longest x1 2.59 us: local_levels(): pl.pallas_call(functools.partial(local_kernel, count, len(tables), local,...]
  transfers between devices with their start and end apart: 15 -> 15, of which waited for: 7 -> 7; matrix products, arithmetic and copies ran while one was open for 2% -> 0% of each run, Pallas kernels for 11% -> 23%
where the time goes in v2:
time: 41.4 us; the launch traced here: 41.1 us
  starting transfers between devices  16.2 us (39%)
  Pallas kernels  15.1 us (36%)
  waiting for transfers between devices  9.73 us (24%)
    ppermute x4, starting transfers between devices, cores_exchange(): out.append(lax.ppermute(block, ('tensor', 'pipe'), route))  7.35 us
    pallas_call x3, Pallas kernels, fetch(): pl.pallas_call(functools.partial(fetch_kernel, first), out_shape=jax.Shap...  6.01 us
    ppermute x7, starting transfers between devices, exchange(): out.append(lax.ppermute(blocks[k], axis, route))  5.26 us
    ppermute x2, waiting for transfers between devices, shards(): z = lax.ppermute(z, 'tensor', [(i, i ^ 1 << n) for i in range(tensor)])  3.72 us
    ppermute x2, starting transfers between devices, shards(): z = lax.ppermute(z, 'tensor', [(i, i ^ 1 << n) for i in range(tensor)])  3.11 us
    ppermute x7, waiting for transfers between devices, exchange(): out.append(lax.ppermute(blocks[k], axis, route))  2.7 us
    ppermute x4, waiting for transfers between devices, cores_exchange(): out.append(lax.ppermute(block, ('tensor', 'pipe'), route))  2.7 us
    pallas_call x1, Pallas kernels, local_levels(): pl.pallas_call(functools.partial(local_kernel, count, len(tables), local,...  2.59 us
  transfers between devices with their start and end apart: 15, of which 7 were waited for; matrix products, arithmetic and copies ran while one was open for 0% of the time, Pallas kernels for 23%

profile of v2, /device:TPU:0, one launch (start us, length us, event | category | flops | bytes accessed | tf_op | source)
XLA Modules:
  0.0 41.1 jit_solution(18059866017602665061)
XLA Ops:
  0.0 0.0 copy-start
  0.0 5.0 %collective-permute-start.2 = (bf16[2,4096]{1,0:T(2,128)(2,1)}, bf16[2,4096]{1,0:T(2,128)(2,1)S(1)}, u32[]{:S(2)}, u32[]{:S(2)}) collective-permute-start(bf16[2,4096]{1,0:T(2,128)(2,1)} %param.6), channel_id=1, source_target_pairs={{0,12},{1,9},{4,8},{5,13},{8,4},{9,1},{12,0},{13,5},{2,14},{3,11},... | collective-permute-start | bytes 49160 | tf_op jit(solution)/shard_map/ppermute | solution.py:66
  5.1 1.4 %collective-permute-start.1 = (bf16[2,4096]{1,0:T(2,128)(2,1)}, bf16[2,4096]{1,0:T(2,128)(2,1)S(1)}, u32[]{:S(2)}, u32[]{:S(2)}) collective-permute-start(bf16[2,4096]{1,0:T(2,128)(2,1)} %param.6), channel_id=1, source_target_pairs={{0,0},{1,5},{4,4},{5,1},{8,8},{9,13},{12,12},{13,9},{2,2},{3,7},{6... | collective-permute-start | bytes 49160 | tf_op jit(solution)/shard_map/ppermute | solution.py:66
  6.4 1.6 %send_halves.1 = (bf16[2,4,512,128]{3,2,1,0:T(8,128)(2,1)S(1)}, bf16[2,4,512,128]{3,2,1,0:T(8,128)(2,1)S(1)}) custom-call(bf16[2,8,512,128]{3,2,1,0:T(8,128)(2,1)} %refs_2_.2, bf16[2,8,512,128]{3,2,1,0:T(8,128)(2,1)} %refs_3_.1), custom_call_target="tpu_custom_call" | custom-call | tf_op jit(solution)/shard_map/send_halves/pallas_call | solution.py:101
  8.1 0.5 %collective-permute-start.3 = (bf16[2,4,512,128]{3,2,1,0:T(8,128)(2,1)S(1)}, bf16[2,4,512,128]{3,2,1,0:T(8,128)(2,1)S(1)}, u32[]{:S(2)}, u32[]{:S(2)}) collective-permute-start(bf16[2,4,512,128]{3,2,1,0:T(8,128)(2,1)S(1)} %get-tuple-element.23), channel_id=1, source_target_pairs={{0,1},{1,0},{2,3},{3,2},{4,5},{5,4},{6,7},{7,6},{8,9},{9,8},{10,11... | collective-permute-start | bytes 3145736 | tf_op jit(solution)/shard_map/ppermute | solution.py:573
  8.5 0.0 copy-done
  8.5 1.5 %collective-permute-start = (s32[2]{0:T(128)S(1)}, s32[2]{0:T(128)S(1)}, u32[]{:S(2)}, u32[]{:S(2)}) collective-permute-start(s32[2]{0:T(128)S(1)} %copy-done), channel_id=1, source_target_pairs={{0,2},{2,0},{1,3},{3,1},{4,6},{6,4},{5,7},{7,5},{8,10},{10,8},{9,1... | collective-permute-start | bytes 32 | tf_op jit(solution)/shard_map/ppermute | solution.py:35
  10.0 0.0 copy-start.1
  10.0 0.0 collective-permute-start.4
  10.0 0.0 collective-permute-done.2.refs_1_
  10.0 0.0 collective-permute-done.1.refs_0_
  10.0 1.8 %attend_own.1 = (bf16[4,32,256]{2,1,0:T(8,128)(2,1)S(1)}, f32[4,32,512]{2,1,0:T(8,128)S(1)}, bf16[2,4,512,128]{3,2,1,0:T(8,128)(2,1)S(1)}, bf16[2048,128]{1,0:T(8,128)(2,1)S(1)}) custom-call(bf16[2,4096]{1,0:T(2,128)(2,1)S(1)} %collective-permute-done.1.refs_0_, bf16[2,4096]{1,0:T(2,128)(2,1)S(1)} %collective-permute-done.2.refs_1_, ...), custom_call_target="tpu_custom_call" | custom-call | flops 20000000000 | bytes 4194304 | tf_op jit(solution)/shard_map/attend_own/pallas_call | solution.py:196
  11.8 0.3 collective-permute-done.refs_1_
  12.1 0.6 %collective-permute-done.4.refs_7_ = bf16[2,4,512,128]{3,2,1,0:T(8,128)(2,1)S(1)} collective-permute-done((bf16[2,4,512,128]{3,2,1,0:T(8,128)(2,1)S(1)}, bf16[2,4,512,128]{3,2,1,0:T(8,128)(2,1)S(1)}, u32[]{:S(2)}, u32[]{:S(2)}) %collective-permute-start.4) | collective-permute-done | bytes 1048608 | tf_op jit(solution)/shard_map/ppermute | solution.py:573
  12.7 0.0 collective-permute-done.3.refs_6_
  12.7 0.0 copy-done.1
  12.7 1.2 %attend.1 = (bf16[80,128]{1,0:T(8,128)(2,1)S(1)}, bf16[80,128]{1,0:T(8,128)(2,1)S(1)}, s32[8,128]{1,0:T(8,128)S(1)}) custom-call(s32[2]{0:T(128)S(1)} %copy-done, s32[2]{0:T(128)S(1)} %collective-permute-done.refs_1_, s32[2]{0:T(128)S(1)} %copy-done.1, bf16[4,32,256]{2,1,0:T(8,128)(2,1)S(1)} %get-tuple-element.25.refs_3_, ...), custom_call_target="tpu_custom_call" | custom-call | tf_op jit(solution)/shard_map/attend/pallas_call | solution.py:318
  13.8 0.3 collective-permute-start.6
  14.1 0.7 %collective-permute-start.5 = (bf16[80,128]{1,0:T(8,128)(2,1)S(1)}, bf16[80,128]{1,0:T(8,128)(2,1)S(1)}, u32[]{:S(2)}, u32[]{:S(2)}) collective-permute-start(bf16[80,128]{1,0:T(8,128)(2,1)S(1)} %get-tuple-element.31._), channel_id=1, source_target_pairs={{0,0},{1,5},{4,4},{5,1},{8,8},{9,13},{12,12},{13,9},{2,2},{3,7},{6... | collective-permute-start | bytes 61448 | tf_op jit(solution)/shard_map/ppermute | solution.py:66
  14.8 2.0 %fetch.3.refs_2_.refs_0_ = bf16[3,2,128,2048]{3,2,1,0:T(8,128)(2,1)S(1)} custom-call(s32[8,128]{1,0:T(8,128)S(1)} %get-tuple-element.29.slot_ref, bf16[80,128]{1,0:T(8,128)(2,1)S(1)} %get-tuple-element.31._, bf16[9,8,128,2048]{3,2,1,0:T(8,128)(2,1)} %table_hbm.5), custom_call_target="tpu_custom_call" | custom-call | tf_op jit(solution)/shard_map/fetch/pallas_call | solution.py:341
  16.8 2.7 %collective-permute-done.6.refs_1_ = bf16[80,128]{1,0:T(8,128)(2,1)S(1)} collective-permute-done((bf16[80,128]{1,0:T(8,128)(2,1)S(1)}, bf16[80,128]{1,0:T(8,128)(2,1)S(1)}, u32[]{:S(2)}, u32[]{:S(2)}) %collective-permute-start.6) | collective-permute-done | bytes 20512 | tf_op jit(solution)/shard_map/ppermute | solution.py:66
  19.5 0.0 collective-permute-done.5.refs_0_
  19.5 0.1 merge.1._.refs_2_
  19.6 0.4 collective-permute-start.9
  20.0 0.8 %collective-permute-start.8 = (bf16[80,128]{1,0:T(8,128)(2,1)S(1)}, bf16[80,128]{1,0:T(8,128)(2,1)S(1)}, u32[]{:S(2)}, u32[]{:S(2)}) collective-permute-start(bf16[80,128]{1,0:T(8,128)(2,1)S(1)} %merge.1._.refs_2_), channel_id=1, source_target_pairs={{0,2},{1,3},{2,0},{3,1},{4,6},{5,7},{6,4},{7,5},{8,10},{9,11},{10,... | collective-permute-start | bytes 61448 | tf_op jit(solution)/shard_map/ppermute | solution.py:35
  20.8 0.7 %collective-permute-start.7 = (bf16[80,128]{1,0:T(8,128)(2,1)S(1)}, bf16[80,128]{1,0:T(8,128)(2,1)S(1)}, u32[]{:S(2)}, u32[]{:S(2)}) collective-permute-start(bf16[80,128]{1,0:T(8,128)(2,1)S(1)} %merge.1._.refs_2_), channel_id=1, source_target_pairs={{0,1},{1,0},{2,3},{3,2},{4,5},{5,4},{6,7},{7,6},{8,9},{9,8},{10,11... | collective-permute-start | bytes 61448 | tf_op jit(solution)/shard_map/ppermute | solution.py:35
  21.5 2.3 %fetch.4.refs_1_ = bf16[4,2,128,2048]{3,2,1,0:T(8,128)(2,1)S(1)} custom-call(s32[8,128]{1,0:T(8,128)S(1)} %get-tuple-element.29.slot_ref, bf16[80,128]{1,0:T(8,128)(2,1)S(1)} %merge.1._.refs_2_, bf16[9,8,128,2048]{3,2,1,0:T(8,128)(2,1)} %table_hbm.5), custom_call_target="tpu_custom_call" | custom-call | tf_op jit(solution)/shard_map/fetch/pallas_call | solution.py:341
  23.8 0.0 collective-permute-done.9.refs_5_
  23.9 0.1 collective-permute-done.8.refs_4_
  23.9 0.0 collective-permute-done.7.refs_3_
  23.9 2.6 %local_levels.1 = (bf16[256,128]{1,0:T(8,128)(2,1)S(1)}, bf16[64,128]{1,0:T(8,128)(2,1)S(1)}) custom-call(s32[8,128]{1,0:T(8,128)S(1)} %get-tuple-element.29.slot_ref, bf16[2048,128]{1,0:T(8,128)(2,1)S(1)} %get-tuple-element.30.sums_ref, bf16[3,2,128,2048]{3,2,1,0:T(8,128)(2,1)S(1)} %fetch.3.refs_2_.refs_0_, bf16[4,2,128,2048]{3,2,1,0:T(8,128)(2,1)S(1)} %fetch.4.refs_1_, ...), custom_call_target="tpu_custom_call" | custom-call | tf_op jit(solution)/shard_map/local_levels/pallas_call | solution.py:465
  26.5 0.8 %collective-permute-start.10 = (bf16[64,128]{1,0:T(8,128)(2,1)S(1)}, bf16[64,128]{1,0:T(8,128)(2,1)S(1)}, u32[]{:S(2)}, u32[]{:S(2)}) collective-permute-start(bf16[64,128]{1,0:T(8,128)(2,1)S(1)} %get-tuple-element.34._), channel_id=1, source_target_pairs={{0,4},{4,0},{8,12},{12,8},{1,5},{5,1},{9,13},{13,9},{2,6},{6,2},{1... | collective-permute-start | bytes 49160 | tf_op jit(solution)/shard_map/ppermute | solution.py:588
  27.3 1.7 %fetch.5.far_ref = bf16[2,2,128,2048]{3,2,1,0:T(8,128)(2,1)S(1)} custom-call(s32[8,128]{1,0:T(8,128)S(1)} %get-tuple-element.29.slot_ref, bf16[64,128]{1,0:T(8,128)(2,1)S(1)} %get-tuple-element.34._, bf16[9,8,128,2048]{3,2,1,0:T(8,128)(2,1)} %table_hbm.5), custom_call_target="tpu_custom_call" | custom-call | tf_op jit(solution)/shard_map/fetch/pallas_call | solution.py:341
  29.0 1.3 %collective-permute-done.10.z_ref = bf16[64,128]{1,0:T(8,128)(2,1)S(1)} collective-permute-done((bf16[64,128]{1,0:T(8,128)(2,1)S(1)}, bf16[64,128]{1,0:T(8,128)(2,1)S(1)}, u32[]{:S(2)}, u32[]{:S(2)}) %collective-permute-start.10) | collective-permute-done | bytes 16416 | tf_op jit(solution)/shard_map/ppermute | solution.py:588
  30.3 0.5 %cross_level.1 = (bf16[256,128]{1,0:T(8,128)(2,1)S(1)}, bf16[64,128]{1,0:T(8,128)(2,1)S(1)}) custom-call(bf16[256,128]{1,0:T(8,128)(2,1)S(1)} %get-tuple-element.33.x_ref, bf16[64,128]{1,0:T(8,128)(2,1)S(1)} %collective-permute-done.10.z_ref, bf16[2048,128]{1,0:T(8,128)(2,1)S(1)} %get-tuple-element.30.sums_ref, bf16[2,2,128,2048]{3,2,1,0:T(8,128)(2,1)S(1)} %fetch.5.far_ref), custom_call_target="tpu_custom_call" | custom-call | tf_op jit(solution)/shard_map/cross_level/pallas_call | solution.py:497
  30.9 2.3 %collective-permute-start.11 = (bf16[64,128]{1,0:T(8,128)(2,1)S(1)}, bf16[64,128]{1,0:T(8,128)(2,1)S(1)}, u32[]{:S(2)}, u32[]{:S(2)}) collective-permute-start(bf16[64,128]{1,0:T(8,128)(2,1)S(1)} %get-tuple-element.36), channel_id=1, source_target_pairs={{0,8},{4,12},{8,0},{12,4},{1,9},{5,13},{9,1},{13,5},{2,10},{6,14},... | collective-permute-start | bytes 49160 | tf_op jit(solution)/shard_map/ppermute | solution.py:588
  33.1 2.4 %collective-permute-done.11.z_ref = bf16[64,128]{1,0:T(8,128)(2,1)S(1)} collective-permute-done((bf16[64,128]{1,0:T(8,128)(2,1)S(1)}, bf16[64,128]{1,0:T(8,128)(2,1)S(1)}, u32[]{:S(2)}, u32[]{:S(2)}) %collective-permute-start.11) | collective-permute-done | bytes 16416 | tf_op jit(solution)/shard_map/ppermute | solution.py:588
  35.6 0.6 %last_level.1 = (bf16[32,128]{1,0:T(8,128)(2,1)S(1)}, bf16[32,128]{1,0:T(8,128)(2,1)S(1)}, bf16[32,128]{1,0:T(8,128)(2,1)S(1)}, bf16[32,128]{1,0:T(8,128)(2,1)S(1)}) custom-call(s32[8,128]{1,0:T(8,128)S(1)} %get-tuple-element.29.slot_ref, bf16[256,128]{1,0:T(8,128)(2,1)S(1)} %get-tuple-element.35.x_ref, bf16[64,128]{1,0:T(8,128)(2,1)S(1)} %collective-permute-done.11.z_ref, ...), custom_call_target="tpu_custom_call" | custom-call | tf_op jit(solution)/shard_map/last_level/pallas_call | solution.py:530
  36.2 0.0 collective-permute-start.12
  36.2 1.2 %collective-permute-start.13 = (bf16[32,128]{1,0:T(8,128)(2,1)S(1)}, bf16[32,128]{1,0:T(8,128)(2,1)S(1)}, u32[]{:S(2)}, u32[]{:S(2)}) collective-permute-start(bf16[32,128]{1,0:T(8,128)(2,1)S(1)} %get-tuple-element.39), channel_id=1, source_target_pairs={{0,2},{1,3},{2,0},{3,1},{4,6},{5,7},{6,4},{7,5},{8,10},{9,11},{10,... | collective-permute-start | bytes 24584 | tf_op jit(solution)/shard_map/ppermute | solution.py:35
  37.4 0.7 %collective-permute-start.14 = (bf16[32,128]{1,0:T(8,128)(2,1)S(1)}, bf16[32,128]{1,0:T(8,128)(2,1)S(1)}, u32[]{:S(2)}, u32[]{:S(2)}) collective-permute-start(bf16[32,128]{1,0:T(8,128)(2,1)S(1)} %get-tuple-element.40), channel_id=1, source_target_pairs={{0,3},{1,2},{2,1},{3,0},{4,7},{5,6},{6,5},{7,4},{8,11},{9,10},{10,... | collective-permute-start | bytes 24584 | tf_op jit(solution)/shard_map/ppermute | solution.py:35
  38.1 0.0 collective-permute-done.12.refs_1_
  38.1 1.8 %collective-permute-done.13.refs_2_ = bf16[32,128]{1,0:T(8,128)(2,1)S(1)} collective-permute-done((bf16[32,128]{1,0:T(8,128)(2,1)S(1)}, bf16[32,128]{1,0:T(8,128)(2,1)S(1)}, u32[]{:S(2)}, u32[]{:S(2)}) %collective-permute-start.13) | collective-permute-done | bytes 8224 | tf_op jit(solution)/shard_map/ppermute | solution.py:35
  39.9 0.6 %collective-permute-done.14.refs_3_ = bf16[32,128]{1,0:T(8,128)(2,1)S(1)} collective-permute-done((bf16[32,128]{1,0:T(8,128)(2,1)S(1)}, bf16[32,128]{1,0:T(8,128)(2,1)S(1)}, u32[]{:S(2)}, u32[]{:S(2)}) %collective-permute-start.14) | collective-permute-done | bytes 8224 | tf_op jit(solution)/shard_map/ppermute | solution.py:35
  40.5 0.6 %pick.1 = bf16[1,4096]{1,0:T(2,128)(2,1)} custom-call(s32[8,128]{1,0:T(8,128)S(1)} %get-tuple-element.29.slot_ref, bf16[32,128]{1,0:T(8,128)(2,1)S(1)} %get-tuple-element.37.refs_0_, bf16[32,128]{1,0:T(8,128)(2,1)S(1)} %collective-permute-done.12.refs_1_, bf16[32,128]{1,0:T(8,128)(2,1)S(1)} %collective-permute-done.13.refs_2_, ...), custom_call_target="tpu_custom_call" | custom-call | tf_op jit(solution)/shard_map/pick/pallas_call | solution.py:554
Async XLA Ops:
  0.0 8.5 %copy-start = (s32[2]{0:T(128)S(1)}, s32[2]{0:T(128)}, u32[]{:S(2)}) copy-start(s32[2]{0:T(128)} %refs_0_.2) | copy-start | bytes 28
  0.0 10.0 %collective-permute-start.2 = (bf16[2,4096]{1,0:T(2,128)(2,1)}, bf16[2,4096]{1,0:T(2,128)(2,1)S(1)}, u32[]{:S(2)}, u32[]{:S(2)}) collective-permute-start(bf16[2,4096]{1,0:T(2,128)(2,1)} %param.6), channel_id=1, source_target_pairs={{0,12},{1,9},{4,8},{5,13},{8,4},{9,1},{12,0},{13,5},{2,14},{3,11},... | collective-permute-start | bytes 49160 | tf_op jit(solution)/shard_map/ppermute | solution.py:66
  5.1 5.0 %collective-permute-start.1 = (bf16[2,4096]{1,0:T(2,128)(2,1)}, bf16[2,4096]{1,0:T(2,128)(2,1)S(1)}, u32[]{:S(2)}, u32[]{:S(2)}) collective-permute-start(bf16[2,4096]{1,0:T(2,128)(2,1)} %param.6), channel_id=1, source_target_pairs={{0,0},{1,5},{4,4},{5,1},{8,8},{9,13},{12,12},{13,9},{2,2},{3,7},{6... | collective-permute-start | bytes 49160 | tf_op jit(solution)/shard_map/ppermute | solution.py:66
  8.1 4.6 %collective-permute-start.3 = (bf16[2,4,512,128]{3,2,1,0:T(8,128)(2,1)S(1)}, bf16[2,4,512,128]{3,2,1,0:T(8,128)(2,1)S(1)}, u32[]{:S(2)}, u32[]{:S(2)}) collective-permute-start(bf16[2,4,512,128]{3,2,1,0:T(8,128)(2,1)S(1)} %get-tuple-element.23), channel_id=1, source_target_pairs={{0,1},{1,0},{2,3},{3,2},{4,5},{5,4},{6,7},{7,6},{8,9},{9,8},{10,11... | collective-permute-start | bytes 3145736 | tf_op jit(solution)/shard_map/ppermute | solution.py:573
  8.5 3.5 %collective-permute-start = (s32[2]{0:T(128)S(1)}, s32[2]{0:T(128)S(1)}, u32[]{:S(2)}, u32[]{:S(2)}) collective-permute-start(s32[2]{0:T(128)S(1)} %copy-done), channel_id=1, source_target_pairs={{0,2},{2,0},{1,3},{3,1},{4,6},{6,4},{5,7},{7,5},{8,10},{10,8},{9,1... | collective-permute-start | bytes 32 | tf_op jit(solution)/shard_map/ppermute | solution.py:35
  10.0 2.7 %copy-start.1 = (s32[2]{0:T(128)S(1)}, s32[2]{0:T(128)}, u32[]{:S(2)}) copy-start(s32[2]{0:T(128)} %refs_2_.3) | copy-start | bytes 28
  10.0 2.7 %collective-permute-start.4 = (bf16[2,4,512,128]{3,2,1,0:T(8,128)(2,1)S(1)}, bf16[2,4,512,128]{3,2,1,0:T(8,128)(2,1)S(1)}, u32[]{:S(2)}, u32[]{:S(2)}) collective-permute-start(bf16[2,4,512,128]{3,2,1,0:T(8,128)(2,1)S(1)} %get-tuple-element.28), channel_id=1, source_target_pairs={{0,1},{1,0},{2,3},{3,2},{4,5},{5,4},{6,7},{7,6},{8,9},{9,8},{10,11... | collective-permute-start | bytes 3145736 | tf_op jit(solution)/shard_map/ppermute | solution.py:573
  13.8 5.6 %collective-permute-start.6 = (bf16[80,128]{1,0:T(8,128)(2,1)S(1)}, bf16[80,128]{1,0:T(8,128)(2,1)S(1)}, u32[]{:S(2)}, u32[]{:S(2)}) collective-permute-start(bf16[80,128]{1,0:T(8,128)(2,1)S(1)} %get-tuple-element.32), channel_id=1, source_target_pairs={{0,12},{1,9},{4,8},{5,13},{8,4},{9,1},{12,0},{13,5},{2,14},{3,11},... | collective-permute-start | bytes 61448 | tf_op jit(solution)/shard_map/ppermute | solution.py:66
  14.1 5.4 %collective-permute-start.5 = (bf16[80,128]{1,0:T(8,128)(2,1)S(1)}, bf16[80,128]{1,0:T(8,128)(2,1)S(1)}, u32[]{:S(2)}, u32[]{:S(2)}) collective-permute-start(bf16[80,128]{1,0:T(8,128)(2,1)S(1)} %get-tuple-element.31._), channel_id=1, source_target_pairs={{0,0},{1,5},{4,4},{5,1},{8,8},{9,13},{12,12},{13,9},{2,2},{3,7},{6... | collective-permute-start | bytes 61448 | tf_op jit(solution)/shard_map/ppermute | solution.py:66
  19.6 4.2 %collective-permute-start.9 = (bf16[80,128]{1,0:T(8,128)(2,1)S(1)}, bf16[80,128]{1,0:T(8,128)(2,1)S(1)}, u32[]{:S(2)}, u32[]{:S(2)}) collective-permute-start(bf16[80,128]{1,0:T(8,128)(2,1)S(1)} %merge.1._.refs_2_), channel_id=1, source_target_pairs={{0,3},{1,2},{2,1},{3,0},{4,7},{5,6},{6,5},{7,4},{8,11},{9,10},{10,... | collective-permute-start | bytes 61448 | tf_op jit(solution)/shard_map/ppermute | solution.py:35
  20.0 3.9 %collective-permute-start.8 = (bf16[80,128]{1,0:T(8,128)(2,1)S(1)}, bf16[80,128]{1,0:T(8,128)(2,1)S(1)}, u32[]{:S(2)}, u32[]{:S(2)}) collective-permute-start(bf16[80,128]{1,0:T(8,128)(2,1)S(1)} %merge.1._.refs_2_), channel_id=1, source_target_pairs={{0,2},{1,3},{2,0},{3,1},{4,6},{5,7},{6,4},{7,5},{8,10},{9,11},{10,... | collective-permute-start | bytes 61448 | tf_op jit(solution)/shard_map/ppermute | solution.py:35
  20.8 3.1 %collective-permute-start.7 = (bf16[80,128]{1,0:T(8,128)(2,1)S(1)}, bf16[80,128]{1,0:T(8,128)(2,1)S(1)}, u32[]{:S(2)}, u32[]{:S(2)}) collective-permute-start(bf16[80,128]{1,0:T(8,128)(2,1)S(1)} %merge.1._.refs_2_), channel_id=1, source_target_pairs={{0,1},{1,0},{2,3},{3,2},{4,5},{5,4},{6,7},{7,6},{8,9},{9,8},{10,11... | collective-permute-start | bytes 61448 | tf_op jit(solution)/shard_map/ppermute | solution.py:35
  26.5 3.8 %collective-permute-start.10 = (bf16[64,128]{1,0:T(8,128)(2,1)S(1)}, bf16[64,128]{1,0:T(8,128)(2,1)S(1)}, u32[]{:S(2)}, u32[]{:S(2)}) collective-permute-start(bf16[64,128]{1,0:T(8,128)(2,1)S(1)} %get-tuple-element.34._), channel_id=1, source_target_pairs={{0,4},{4,0},{8,12},{12,8},{1,5},{5,1},{9,13},{13,9},{2,6},{6,2},{1... | collective-permute-start | bytes 49160 | tf_op jit(solution)/shard_map/ppermute | solution.py:588
  30.9 4.7 %collective-permute-start.11 = (bf16[64,128]{1,0:T(8,128)(2,1)S(1)}, bf16[64,128]{1,0:T(8,128)(2,1)S(1)}, u32[]{:S(2)}, u32[]{:S(2)}) collective-permute-start(bf16[64,128]{1,0:T(8,128)(2,1)S(1)} %get-tuple-element.36), channel_id=1, source_target_pairs={{0,8},{4,12},{8,0},{12,4},{1,9},{5,13},{9,1},{13,5},{2,10},{6,14},... | collective-permute-start | bytes 49160 | tf_op jit(solution)/shard_map/ppermute | solution.py:588
  36.2 1.9 %collective-permute-start.12 = (bf16[32,128]{1,0:T(8,128)(2,1)S(1)}, bf16[32,128]{1,0:T(8,128)(2,1)S(1)}, u32[]{:S(2)}, u32[]{:S(2)}) collective-permute-start(bf16[32,128]{1,0:T(8,128)(2,1)S(1)} %get-tuple-element.38), channel_id=1, source_target_pairs={{0,1},{1,0},{2,3},{3,2},{4,5},{5,4},{6,7},{7,6},{8,9},{9,8},{10,11... | collective-permute-start | bytes 24584 | tf_op jit(solution)/shard_map/ppermute | solution.py:35
  36.2 3.7 %collective-permute-start.13 = (bf16[32,128]{1,0:T(8,128)(2,1)S(1)}, bf16[32,128]{1,0:T(8,128)(2,1)S(1)}, u32[]{:S(2)}, u32[]{:S(2)}) collective-permute-start(bf16[32,128]{1,0:T(8,128)(2,1)S(1)} %get-tuple-element.39), channel_id=1, source_target_pairs={{0,2},{1,3},{2,0},{3,1},{4,6},{5,7},{6,4},{7,5},{8,10},{9,11},{10,... | collective-permute-start | bytes 24584 | tf_op jit(solution)/shard_map/ppermute | solution.py:35
  37.4 3.1 %collective-permute-start.14 = (bf16[32,128]{1,0:T(8,128)(2,1)S(1)}, bf16[32,128]{1,0:T(8,128)(2,1)S(1)}, u32[]{:S(2)}, u32[]{:S(2)}) collective-permute-start(bf16[32,128]{1,0:T(8,128)(2,1)S(1)} %get-tuple-element.40), channel_id=1, source_target_pairs={{0,3},{1,2},{2,1},{3,0},{4,7},{5,6},{6,5},{7,4},{8,11},{9,10},{10,... | collective-permute-start | bytes 24584 | tf_op jit(solution)/shard_map/ppermute | solution.py:35

commit v3 on v2

--- a/solution.py
+++ b/solution.py
@@ -19,7 +19,7 @@
 WIDE = HALF * B
 NEG = -1e30
 FLOOR = -1e29
-FIRST = 3
+FIRST = 2
 STATS = 16
 
 VMEM = pl.BlockSpec(memory_space=pltpu.VMEM)
@@ -142,16 +142,13 @@
 
 
 def own_kernel(count, *refs):
-    q_refs, (key_hbm, value_hbm) = refs[:count], refs[count:count + 2]
-    wide_ref, score_ref, value_ref, sums_ref, key_buf, sems = refs[count + 2:]
-    key_copies = start_half(0, key_hbm, key_buf, sems.at[0])
-    value_copies = start_half(0, value_hbm, value_ref, sems.at[1])
+    q_refs, key_ref = refs[:count], refs[count]
+    wide_ref, score_ref, sums_ref = refs[count + 1:]
     rows = q_refs[0].shape[0]
     chunks, tall, _ = wide_ref.shape
     size = tall // rows
     sums_ref[...] = one_hot(iota(sums_ref.shape, 0) // B == iota(sums_ref.shape, 1) % HALF)
     which = iota((tall, HD), 0) % rows
-    wide = []
     for n in range(chunks):
         k, c = divmod(n, chunks // count)
         q = jnp.concatenate(
@@ -159,13 +156,7 @@
         )
         q = jnp.concatenate([jnp.where(which == r, q, jnp.zeros_like(q)) for r in range(rows)], axis=1)
         wide_ref[n] = q
-        wide.append(q)
-    for copy in key_copies:
-        copy.wait()
-    for n in range(chunks):
-        score_ref[n] = scores_of(wide[n], key_buf, group_of(n, chunks, count, size))
-    for copy in value_copies:
-        copy.wait()
+        score_ref[n] = scores_of(q, key_ref, group_of(n, chunks, count, size, True))
 
 
 def beside(ref, group):
@@ -178,39 +169,33 @@
     )
 
 
-def group_of(n, chunks, count, size):
+def group_of(n, chunks, count, size, of_all=False):
     k, c = divmod(n, chunks // count)
     tensor = 2 * count
     shard = lax.axis_index("tensor") ^ reach_of(k, lax.axis_index("pipe"), tensor)
-    return (place_of(shard, tensor) * (HQ // tensor) + c * size) // GROUP
-
-
-def attend_own(queries, key_cache, value_cache):
+    place = shard if of_all else place_of(shard, tensor)
+    return (place * (HQ // tensor) + c * size) // GROUP
+
+
+def attend_own(queries, key_cache):
     count = len(queries)
     rows, width = queries[0].shape
     share = width // HD
     size = min(GROUP, share)
     span = key_cache.shape[2]
     chunks, tall = count * share // size, size * rows
-    half = (rows, KVH // 2, span, HD)
     return pl.pallas_call(
         functools.partial(own_kernel, count),
         out_shape=[
             jax.ShapeDtypeStruct((chunks, tall, rows * HD), jnp.bfloat16),
             jax.ShapeDtypeStruct((chunks, tall, span), jnp.float32),
-            jax.ShapeDtypeStruct(half, jnp.bfloat16),
             jax.ShapeDtypeStruct((WIDE, LANES), jnp.bfloat16),
         ],
-        in_specs=[VMEM] * count + [HBM] * 2,
-        out_specs=[VMEM] * 4,
-        scratch_shapes=[
-            pltpu.VMEM(half, jnp.bfloat16),
-            pltpu.SemaphoreType.DMA((2, rows, KVH // 2)),
-        ],
+        in_specs=[VMEM] * (count + 1),
+        out_specs=[VMEM] * 3,
         compiler_params=pltpu.CompilerParams(vmem_limit_bytes=16 << 20),
-        cost_estimate=pl.CostEstimate(flops=int(2e10), bytes_accessed=1 << 22, transcendentals=0),
         name="attend_own",
-    )(*queries, key_cache, value_cache)
+    )(*queries, key_cache)
 
 
 def attend_kernel(count, near, lang_share, *refs):
@@ -253,7 +238,7 @@
     visible = start * span + place < length
     for n in range(chunks):
         k, c = divmod(n, chunks // count)
-        group = group_of(n, chunks, count, size)
+        group, whole = group_of(n, chunks, count, size), group_of(n, chunks, count, size, True)
         scores = jnp.concatenate([score_ref[n], other[n]], axis=1)
         scores = jnp.where(visible, scores * (1.0 / math.sqrt(HD)), NEG)
         top = jnp.maximum(jnp.max(scores, axis=1, keepdims=True), FLOOR)
@@ -264,10 +249,10 @@
         both = sum(
             jnp.dot(
                 weights[:, side * span:(side + 1) * span],
-                beside(values, group),
+                beside(values, place),
                 preferred_element_type=jnp.float32,
             )
-            for side, values in enumerate((own_value_ref, value_ref))
+            for side, (values, place) in enumerate(((own_value_ref, whole), (value_ref, group)))
         )
         which = iota((tall, LANES), 0) % rows
         weighted = both[:, :HD]
@@ -571,12 +556,11 @@
     swap = [(0, 1), (1, 0)]
     sent = send_halves(*caches)
     other = [lax.ppermute(half, "pipe", swap) for half in sent]
-    later, _ = lax.optimization_barrier((languages, sent[0]))
-    langs = exchange([later] * near, "dp", near)
+    langs = exchange([languages] * near, "dp", near)
     spread = cores_exchange([queries] * (tensor // 2), tensor)
-    wide, scores, own_value, sums = attend_own(spread, *caches)
+    wide, scores, sums = attend_own(spread, key_cache)
     *parts, slots = attend(
-        langs, lengths, wide, scores, own_value, *other, tensor // 2, lang_share
+        langs, lengths, wide, scores, value_cache, *other, tensor // 2, lang_share
     )
     first = fetch(slots, parts[0], adapter, 0, FIRST)
     part = merged(cores_exchange(parts, tensor), first)

time: 41.4 us -> 41.3 us (level)
  starting transfers between devices: 16.2 us -> 17.2 us
  Pallas kernels: 15.1 us -> 14.3 us
    ppermute x7, waiting for transfers between devices: 2.7 us -> 4.2 us  [exchange(): out.append(lax.ppermute(blocks[k], axis, route))]
    ppermute x4, waiting for transfers between devices: 2.7 us -> 1.36 us  [cores_exchange(): out.append(lax.ppermute(block, ('tensor', 'pipe'), route))]
    pallas_call x1, Pallas kernels: 1.77 us -> 0.6 us  [attend_own(): pl.pallas_call(functools.partial(own_kernel, count), out_shape=[jax.Shape...]
    ppermute x4, starting transfers between devices: 7.35 us -> 8.29 us  [cores_exchange(): out.append(lax.ppermute(block, ('tensor', 'pipe'), route))]
    ppermute x2, waiting for transfers between devices: 0.62 us -> 0.01 us  [shards(): other = [lax.ppermute(half, 'pipe', swap) for half in sent]]
  transfers between devices with their start and end apart: 15 -> 15, of which waited for: 7 -> 6; matrix products, arithmetic and copies ran while one was open for 0% -> 0% of each run, Pallas kernels for 23% -> 16%
where the time goes in v3:
time: 41.3 us; the launch traced here: 41.1 us
  starting transfers between devices  17.2 us (42%)
  Pallas kernels  14.3 us (35%)
  waiting for transfers between devices  9.43 us (23%)
    ppermute x4, starting transfers between devices, cores_exchange(): out.append(lax.ppermute(block, ('tensor', 'pipe'), route))  8.29 us
    pallas_call x3, Pallas kernels, fetch(): pl.pallas_call(functools.partial(fetch_kernel, first), out_shape=jax.Shap...  6.01 us
    ppermute x7, starting transfers between devices, exchange(): out.append(lax.ppermute(blocks[k], axis, route))  5.32 us
    ppermute x7, waiting for transfers between devices, exchange(): out.append(lax.ppermute(blocks[k], axis, route))  4.2 us
    ppermute x2, waiting for transfers between devices, shards(): z = lax.ppermute(z, 'tensor', [(i, i ^ 1 << n) for i in range(tensor)])  3.87 us
    ppermute x2, starting transfers between devices, shards(): z = lax.ppermute(z, 'tensor', [(i, i ^ 1 << n) for i in range(tensor)])  2.96 us
    pallas_call x1, Pallas kernels, local_levels(): pl.pallas_call(functools.partial(local_kernel, count, len(tables), local,...  2.57 us
    pallas_call x1, Pallas kernels, send_halves(): pl.pallas_call(send_kernel, out_shape=[half, half], in_specs=[HBM, HBM],...  1.79 us
  transfers between devices with their start and end apart: 15, of which 6 were waited for; matrix products, arithmetic and copies ran while one was open for 0% of the time, Pallas kernels for 16%

profile of v3, /device:TPU:0, one launch (start us, length us, event | category | flops | bytes accessed | tf_op | source)
XLA Modules:
  0.0 41.1 jit_solution(4774520870100781246)
XLA Ops:
  0.0 0.0 copy-start
  0.0 0.0 copy-start.4
  0.0 0.0 copy-start.2
  0.0 1.8 %send_halves.1 = (bf16[2,4,512,128]{3,2,1,0:T(8,128)(2,1)S(1)}, bf16[2,4,512,128]{3,2,1,0:T(8,128)(2,1)S(1)}) custom-call(bf16[2,8,512,128]{3,2,1,0:T(8,128)(2,1)} %refs_0_.2, bf16[2,8,512,128]{3,2,1,0:T(8,128)(2,1)} %refs_5_.1), custom_call_target="tpu_custom_call" | custom-call | tf_op jit(solution)/shard_map/send_halves/pallas_call | solution.py:101
  1.8 0.0 copy-start.1
  1.8 0.0 copy-start.3
  1.8 0.5 %collective-permute-start.3 = (bf16[2,4,512,128]{3,2,1,0:T(8,128)(2,1)S(1)}, bf16[2,4,512,128]{3,2,1,0:T(8,128)(2,1)S(1)}, u32[]{:S(2)}, u32[]{:S(2)}) collective-permute-start(bf16[2,4,512,128]{3,2,1,0:T(8,128)(2,1)S(1)} %get-tuple-element.23), channel_id=1, source_target_pairs={{0,1},{1,0},{2,3},{3,2},{4,5},{5,4},{6,7},{7,6},{8,9},{9,8},{10,11... | collective-permute-start | bytes 3145736 | tf_op jit(solution)/shard_map/ppermute | solution.py:558
  2.4 0.1 collective-permute-start.4
  2.4 0.0 copy-done.4
  2.4 5.0 %collective-permute-start.2 = (bf16[2,4096]{1,0:T(2,128)(2,1)S(1)}, bf16[2,4096]{1,0:T(2,128)(2,1)S(1)}, u32[]{:S(2)}, u32[]{:S(2)}) collective-permute-start(bf16[2,4096]{1,0:T(2,128)(2,1)S(1)} %copy-done.4), channel_id=1, source_target_pairs={{0,12},{1,9},{4,8},{5,13},{8,4},{9,1},{12,0},{13,5},{2,14},{3,11},... | collective-permute-start | bytes 49160 | tf_op jit(solution)/shard_map/ppermute | solution.py:66
  7.5 0.7 %collective-permute-start.1 = (bf16[2,4096]{1,0:T(2,128)(2,1)S(1)}, bf16[2,4096]{1,0:T(2,128)(2,1)S(1)}, u32[]{:S(2)}, u32[]{:S(2)}) collective-permute-start(bf16[2,4096]{1,0:T(2,128)(2,1)S(1)} %copy-done.4), channel_id=1, source_target_pairs={{0,0},{1,5},{4,4},{5,1},{8,8},{9,13},{12,12},{13,9},{2,2},{3,7},{6... | collective-permute-start | bytes 49160 | tf_op jit(solution)/shard_map/ppermute | solution.py:66
  8.1 0.0 copy-done.2
  8.1 1.6 %collective-permute-start = (s32[2]{0:T(128)S(1)}, s32[2]{0:T(128)S(1)}, u32[]{:S(2)}, u32[]{:S(2)}) collective-permute-start(s32[2]{0:T(128)S(1)} %copy-done.2), channel_id=1, source_target_pairs={{0,2},{2,0},{1,3},{3,1},{4,6},{6,4},{5,7},{7,5},{8,10},{10,8},{9,1... | collective-permute-start | bytes 32 | tf_op jit(solution)/shard_map/ppermute | solution.py:35
  9.7 0.0 collective-permute-done.2.refs_1_
  9.7 0.0 collective-permute-done.1.refs_0_
  9.7 0.0 copy-done
  9.7 0.6 %attend_own.1 = (bf16[4,32,256]{2,1,0:T(8,128)(2,1)S(1)}, f32[4,32,512]{2,1,0:T(8,128)S(1)}, bf16[2048,128]{1,0:T(8,128)(2,1)S(1)}) custom-call(bf16[2,4096]{1,0:T(2,128)(2,1)S(1)} %collective-permute-done.1.refs_0_, bf16[2,4096]{1,0:T(2,128)(2,1)S(1)} %collective-permute-done.2.refs_1_, bf16[2,8,512,128]{3,2,1,0:T(8,128)(2,1)S(1)} %copy-done), custom_call_target="tpu_custom_call" | custom-call | tf_op jit(solution)/shard_map/attend_own/pallas_call | solution.py:187
  10.3 1.4 %collective-permute-done.refs_1_ = s32[2]{0:T(128)S(1)} collective-permute-done((s32[2]{0:T(128)S(1)}, s32[2]{0:T(128)S(1)}, u32[]{:S(2)}, u32[]{:S(2)}) %collective-permute-start) | collective-permute-done | bytes 40 | tf_op jit(solution)/shard_map/ppermute | solution.py:35
  11.7 0.0 collective-permute-done.3.refs_6_
  11.7 0.0 collective-permute-done.4.refs_7_
  11.8 0.0 copy-done.1
  11.8 0.0 copy-done.3
  11.8 1.4 %attend.1 = (bf16[80,128]{1,0:T(8,128)(2,1)S(1)}, bf16[80,128]{1,0:T(8,128)(2,1)S(1)}, s32[8,128]{1,0:T(8,128)S(1)}) custom-call(s32[2]{0:T(128)S(1)} %copy-done.2, s32[2]{0:T(128)S(1)} %collective-permute-done.refs_1_, s32[2]{0:T(128)S(1)} %copy-done.3, bf16[4,32,256]{2,1,0:T(8,128)(2,1)S(1)} %get-tuple-element.21.refs_3_, ...), custom_call_target="tpu_custom_call" | custom-call | tf_op jit(solution)/shard_map/attend/pallas_call | solution.py:303
  13.2 2.0 %collective-permute-start.6 = (bf16[80,128]{1,0:T(8,128)(2,1)S(1)}, bf16[80,128]{1,0:T(8,128)(2,1)S(1)}, u32[]{:S(2)}, u32[]{:S(2)}) collective-permute-start(bf16[80,128]{1,0:T(8,128)(2,1)S(1)} %get-tuple-element.28), channel_id=1, source_target_pairs={{0,12},{1,9},{4,8},{5,13},{8,4},{9,1},{12,0},{13,5},{2,14},{3,11},... | collective-permute-start | bytes 61448 | tf_op jit(solution)/shard_map/ppermute | solution.py:66
  15.1 0.7 %collective-permute-start.5 = (bf16[80,128]{1,0:T(8,128)(2,1)S(1)}, bf16[80,128]{1,0:T(8,128)(2,1)S(1)}, u32[]{:S(2)}, u32[]{:S(2)}) collective-permute-start(bf16[80,128]{1,0:T(8,128)(2,1)S(1)} %get-tuple-element.27._), channel_id=1, source_target_pairs={{0,0},{1,5},{4,4},{5,1},{8,8},{9,13},{12,12},{13,9},{2,2},{3,7},{6... | collective-permute-start | bytes 61448 | tf_op jit(solution)/shard_map/ppermute | solution.py:66
  15.8 1.7 %fetch.3.refs_2_.refs_0_ = bf16[2,2,128,2048]{3,2,1,0:T(8,128)(2,1)S(1)} custom-call(s32[8,128]{1,0:T(8,128)S(1)} %get-tuple-element.25.slot_ref, bf16[80,128]{1,0:T(8,128)(2,1)S(1)} %get-tuple-element.27._, bf16[9,8,128,2048]{3,2,1,0:T(8,128)(2,1)} %table_hbm.5), custom_call_target="tpu_custom_call" | custom-call | tf_op jit(solution)/shard_map/fetch/pallas_call | solution.py:326
  17.5 1.3 %collective-permute-done.6.refs_1_ = bf16[80,128]{1,0:T(8,128)(2,1)S(1)} collective-permute-done((bf16[80,128]{1,0:T(8,128)(2,1)S(1)}, bf16[80,128]{1,0:T(8,128)(2,1)S(1)}, u32[]{:S(2)}, u32[]{:S(2)}) %collective-permute-start.6) | collective-permute-done | bytes 20512 | tf_op jit(solution)/shard_map/ppermute | solution.py:66
  18.8 0.0 collective-permute-done.5.refs_0_
  18.8 0.1 merge.1._.refs_2_
  19.0 0.6 %collective-permute-start.9 = (bf16[80,128]{1,0:T(8,128)(2,1)S(1)}, bf16[80,128]{1,0:T(8,128)(2,1)S(1)}, u32[]{:S(2)}, u32[]{:S(2)}) collective-permute-start(bf16[80,128]{1,0:T(8,128)(2,1)S(1)} %merge.1._.refs_2_), channel_id=1, source_target_pairs={{0,3},{1,2},{2,1},{3,0},{4,7},{5,6},{6,5},{7,4},{8,11},{9,10},{10,... | collective-permute-start | bytes 61448 | tf_op jit(solution)/shard_map/ppermute | solution.py:35
  19.5 1.0 %collective-permute-start.8 = (bf16[80,128]{1,0:T(8,128)(2,1)S(1)}, bf16[80,128]{1,0:T(8,128)(2,1)S(1)}, u32[]{:S(2)}, u32[]{:S(2)}) collective-permute-start(bf16[80,128]{1,0:T(8,128)(2,1)S(1)} %merge.1._.refs_2_), channel_id=1, source_target_pairs={{0,2},{1,3},{2,0},{3,1},{4,6},{5,7},{6,4},{7,5},{8,10},{9,11},{10,... | collective-permute-start | bytes 61448 | tf_op jit(solution)/shard_map/ppermute | solution.py:35
  20.5 0.3 collective-permute-start.7
  20.8 2.7 %fetch.4.refs_1_ = bf16[5,2,128,2048]{3,2,1,0:T(8,128)(2,1)S(1)} custom-call(s32[8,128]{1,0:T(8,128)S(1)} %get-tuple-element.25.slot_ref, bf16[80,128]{1,0:T(8,128)(2,1)S(1)} %merge.1._.refs_2_, bf16[9,8,128,2048]{3,2,1,0:T(8,128)(2,1)} %table_hbm.5), custom_call_target="tpu_custom_call" | custom-call | tf_op jit(solution)/shard_map/fetch/pallas_call | solution.py:326
  23.5 0.0 collective-permute-done.9.refs_5_
  23.5 0.0 collective-permute-done.8.refs_4_
  23.5 0.0 collective-permute-done.7.refs_3_
  23.5 2.6 %local_levels.1 = (bf16[256,128]{1,0:T(8,128)(2,1)S(1)}, bf16[64,128]{1,0:T(8,128)(2,1)S(1)}) custom-call(s32[8,128]{1,0:T(8,128)S(1)} %get-tuple-element.25.slot_ref, bf16[2048,128]{1,0:T(8,128)(2,1)S(1)} %get-tuple-element.26.sums_ref, bf16[2,2,128,2048]{3,2,1,0:T(8,128)(2,1)S(1)} %fetch.3.refs_2_.refs_0_, bf16[5,2,128,2048]{3,2,1,0:T(8,128)(2,1)S(1)} %fetch.4.refs_1_, ...), custom_call_target="tpu_custom_call" | custom-call | tf_op jit(solution)/shard_map/local_levels/pallas_call | solution.py:450
  26.1 0.8 %collective-permute-start.10 = (bf16[64,128]{1,0:T(8,128)(2,1)S(1)}, bf16[64,128]{1,0:T(8,128)(2,1)S(1)}, u32[]{:S(2)}, u32[]{:S(2)}) collective-permute-start(bf16[64,128]{1,0:T(8,128)(2,1)S(1)} %get-tuple-element.30._), channel_id=1, source_target_pairs={{0,4},{4,0},{8,12},{12,8},{1,5},{5,1},{9,13},{13,9},{2,6},{6,2},{1... | collective-permute-start | bytes 49160 | tf_op jit(solution)/shard_map/ppermute | solution.py:572
  27.0 1.7 %fetch.5.far_ref = bf16[2,2,128,2048]{3,2,1,0:T(8,128)(2,1)S(1)} custom-call(s32[8,128]{1,0:T(8,128)S(1)} %get-tuple-element.25.slot_ref, bf16[64,128]{1,0:T(8,128)(2,1)S(1)} %get-tuple-element.30._, bf16[9,8,128,2048]{3,2,1,0:T(8,128)(2,1)} %table_hbm.5), custom_call_target="tpu_custom_call" | custom-call | tf_op jit(solution)/shard_map/fetch/pallas_call | solution.py:326
  28.6 1.3 %collective-permute-done.10.z_ref = bf16[64,128]{1,0:T(8,128)(2,1)S(1)} collective-permute-done((bf16[64,128]{1,0:T(8,128)(2,1)S(1)}, bf16[64,128]{1,0:T(8,128)(2,1)S(1)}, u32[]{:S(2)}, u32[]{:S(2)}) %collective-permute-start.10) | collective-permute-done | bytes 16416 | tf_op jit(solution)/shard_map/ppermute | solution.py:572
  29.9 0.6 %cross_level.1 = (bf16[256,128]{1,0:T(8,128)(2,1)S(1)}, bf16[64,128]{1,0:T(8,128)(2,1)S(1)}) custom-call(bf16[256,128]{1,0:T(8,128)(2,1)S(1)} %get-tuple-element.29.x_ref, bf16[64,128]{1,0:T(8,128)(2,1)S(1)} %collective-permute-done.10.z_ref, bf16[2048,128]{1,0:T(8,128)(2,1)S(1)} %get-tuple-element.26.sums_ref, bf16[2,2,128,2048]{3,2,1,0:T(8,128)(2,1)S(1)} %fetch.5.far_ref), custom_call_target="tpu_custom_call" | custom-call | tf_op jit(solution)/shard_map/cross_level/pallas_call | solution.py:482
  30.5 2.1 %collective-permute-start.11 = (bf16[64,128]{1,0:T(8,128)(2,1)S(1)}, bf16[64,128]{1,0:T(8,128)(2,1)S(1)}, u32[]{:S(2)}, u32[]{:S(2)}) collective-permute-start(bf16[64,128]{1,0:T(8,128)(2,1)S(1)} %get-tuple-element.32), channel_id=1, source_target_pairs={{0,8},{4,12},{8,0},{12,4},{1,9},{5,13},{9,1},{13,5},{2,10},{6,14},... | collective-permute-start | bytes 49160 | tf_op jit(solution)/shard_map/ppermute | solution.py:572
  32.6 2.6 %collective-permute-done.11.z_ref = bf16[64,128]{1,0:T(8,128)(2,1)S(1)} collective-permute-done((bf16[64,128]{1,0:T(8,128)(2,1)S(1)}, bf16[64,128]{1,0:T(8,128)(2,1)S(1)}, u32[]{:S(2)}, u32[]{:S(2)}) %collective-permute-start.11) | collective-permute-done | bytes 16416 | tf_op jit(solution)/shard_map/ppermute | solution.py:572
  35.2 0.6 %last_level.1 = (bf16[32,128]{1,0:T(8,128)(2,1)S(1)}, bf16[32,128]{1,0:T(8,128)(2,1)S(1)}, bf16[32,128]{1,0:T(8,128)(2,1)S(1)}, bf16[32,128]{1,0:T(8,128)(2,1)S(1)}) custom-call(s32[8,128]{1,0:T(8,128)S(1)} %get-tuple-element.25.slot_ref, bf16[256,128]{1,0:T(8,128)(2,1)S(1)} %get-tuple-element.31.x_ref, bf16[64,128]{1,0:T(8,128)(2,1)S(1)} %collective-permute-done.11.z_ref, ...), custom_call_target="tpu_custom_call" | custom-call | tf_op jit(solution)/shard_map/last_level/pallas_call | solution.py:515
  35.8 0.0 collective-permute-start.12
  35.8 1.6 %collective-permute-start.13 = (bf16[32,128]{1,0:T(8,128)(2,1)S(1)}, bf16[32,128]{1,0:T(8,128)(2,1)S(1)}, u32[]{:S(2)}, u32[]{:S(2)}) collective-permute-start(bf16[32,128]{1,0:T(8,128)(2,1)S(1)} %get-tuple-element.35), channel_id=1, source_target_pairs={{0,2},{1,3},{2,0},{3,1},{4,6},{5,7},{6,4},{7,5},{8,10},{9,11},{10,... | collective-permute-start | bytes 24584 | tf_op jit(solution)/shard_map/ppermute | solution.py:35
  37.4 0.3 collective-permute-start.14
  37.7 0.0 collective-permute-done.12.refs_1_
  37.7 1.8 %collective-permute-done.13.refs_2_ = bf16[32,128]{1,0:T(8,128)(2,1)S(1)} collective-permute-done((bf16[32,128]{1,0:T(8,128)(2,1)S(1)}, bf16[32,128]{1,0:T(8,128)(2,1)S(1)}, u32[]{:S(2)}, u32[]{:S(2)}) %collective-permute-start.13) | collective-permute-done | bytes 8224 | tf_op jit(solution)/shard_map/ppermute | solution.py:35
  39.6 0.9 %collective-permute-done.14.refs_3_ = bf16[32,128]{1,0:T(8,128)(2,1)S(1)} collective-permute-done((bf16[32,128]{1,0:T(8,128)(2,1)S(1)}, bf16[32,128]{1,0:T(8,128)(2,1)S(1)}, u32[]{:S(2)}, u32[]{:S(2)}) %collective-permute-start.14) | collective-permute-done | bytes 8224 | tf_op jit(solution)/shard_map/ppermute | solution.py:35
  40.5 0.6 %pick.1 = bf16[1,4096]{1,0:T(2,128)(2,1)} custom-call(s32[8,128]{1,0:T(8,128)S(1)} %get-tuple-element.25.slot_ref, bf16[32,128]{1,0:T(8,128)(2,1)S(1)} %get-tuple-element.33.refs_0_, bf16[32,128]{1,0:T(8,128)(2,1)S(1)} %collective-permute-done.12.refs_1_, bf16[32,128]{1,0:T(8,128)(2,1)S(1)} %collective-permute-done.13.refs_2_, ...), custom_call_target="tpu_custom_call" | custom-call | tf_op jit(solution)/shard_map/pick/pallas_call | solution.py:539
Async XLA Ops:
  0.0 9.7 %copy-start = (bf16[2,8,512,128]{3,2,1,0:T(8,128)(2,1)S(1)}, bf16[2,8,512,128]{3,2,1,0:T(8,128)(2,1)}, u32[]{:S(2)}) copy-start(bf16[2,8,512,128]{3,2,1,0:T(8,128)(2,1)} %refs_0_.2) | copy-start | bytes 6291460
  0.0 2.4 %copy-start.4 = (bf16[2,4096]{1,0:T(2,128)(2,1)S(1)}, bf16[2,4096]{1,0:T(2,128)(2,1)}, u32[]{:S(2)}) copy-start(bf16[2,4096]{1,0:T(2,128)(2,1)} %param.6) | copy-start | bytes 49156
  0.0 8.1 %copy-start.2 = (s32[2]{0:T(128)S(1)}, s32[2]{0:T(128)}, u32[]{:S(2)}) copy-start(s32[2]{0:T(128)} %refs_0_.3) | copy-start | bytes 28
  1.8 9.9 %copy-start.1 = (bf16[2,8,512,128]{3,2,1,0:T(8,128)(2,1)S(1)}, bf16[2,8,512,128]{3,2,1,0:T(8,128)(2,1)}, u32[]{:S(2)}) copy-start(bf16[2,8,512,128]{3,2,1,0:T(8,128)(2,1)} %refs_5_.1) | copy-start | bytes 6291460
  1.8 9.9 %copy-start.3 = (s32[2]{0:T(128)S(1)}, s32[2]{0:T(128)}, u32[]{:S(2)}) copy-start(s32[2]{0:T(128)} %refs_2_.3) | copy-start | bytes 28
  1.8 9.9 %collective-permute-start.3 = (bf16[2,4,512,128]{3,2,1,0:T(8,128)(2,1)S(1)}, bf16[2,4,512,128]{3,2,1,0:T(8,128)(2,1)S(1)}, u32[]{:S(2)}, u32[]{:S(2)}) collective-permute-start(bf16[2,4,512,128]{3,2,1,0:T(8,128)(2,1)S(1)} %get-tuple-element.23), channel_id=1, source_target_pairs={{0,1},{1,0},{2,3},{3,2},{4,5},{5,4},{6,7},{7,6},{8,9},{9,8},{10,11... | collective-permute-start | bytes 3145736 | tf_op jit(solution)/shard_map/ppermute | solution.py:558
  2.4 9.4 %collective-permute-start.4 = (bf16[2,4,512,128]{3,2,1,0:T(8,128)(2,1)S(1)}, bf16[2,4,512,128]{3,2,1,0:T(8,128)(2,1)S(1)}, u32[]{:S(2)}, u32[]{:S(2)}) collective-permute-start(bf16[2,4,512,128]{3,2,1,0:T(8,128)(2,1)S(1)} %get-tuple-element.24), channel_id=1, source_target_pairs={{0,1},{1,0},{2,3},{3,2},{4,5},{5,4},{6,7},{7,6},{8,9},{9,8},{10,11... | collective-permute-start | bytes 3145736 | tf_op jit(solution)/shard_map/ppermute | solution.py:558
  2.4 7.3 %collective-permute-start.2 = (bf16[2,4096]{1,0:T(2,128)(2,1)S(1)}, bf16[2,4096]{1,0:T(2,128)(2,1)S(1)}, u32[]{:S(2)}, u32[]{:S(2)}) collective-permute-start(bf16[2,4096]{1,0:T(2,128)(2,1)S(1)} %copy-done.4), channel_id=1, source_target_pairs={{0,12},{1,9},{4,8},{5,13},{8,4},{9,1},{12,0},{13,5},{2,14},{3,11},... | collective-permute-start | bytes 49160 | tf_op jit(solution)/shard_map/ppermute | solution.py:66
  7.5 2.2 %collective-permute-start.1 = (bf16[2,4096]{1,0:T(2,128)(2,1)S(1)}, bf16[2,4096]{1,0:T(2,128)(2,1)S(1)}, u32[]{:S(2)}, u32[]{:S(2)}) collective-permute-start(bf16[2,4096]{1,0:T(2,128)(2,1)S(1)} %copy-done.4), channel_id=1, source_target_pairs={{0,0},{1,5},{4,4},{5,1},{8,8},{9,13},{12,12},{13,9},{2,2},{3,7},{6... | collective-permute-start | bytes 49160 | tf_op jit(solution)/shard_map/ppermute | solution.py:66
  8.1 3.6 %collective-permute-start = (s32[2]{0:T(128)S(1)}, s32[2]{0:T(128)S(1)}, u32[]{:S(2)}, u32[]{:S(2)}) collective-permute-start(s32[2]{0:T(128)S(1)} %copy-done.2), channel_id=1, source_target_pairs={{0,2},{2,0},{1,3},{3,1},{4,6},{6,4},{5,7},{7,5},{8,10},{10,8},{9,1... | collective-permute-start | bytes 32 | tf_op jit(solution)/shard_map/ppermute | solution.py:35
  13.2 5.6 %collective-permute-start.6 = (bf16[80,128]{1,0:T(8,128)(2,1)S(1)}, bf16[80,128]{1,0:T(8,128)(2,1)S(1)}, u32[]{:S(2)}, u32[]{:S(2)}) collective-permute-start(bf16[80,128]{1,0:T(8,128)(2,1)S(1)} %get-tuple-element.28), channel_id=1, source_target_pairs={{0,12},{1,9},{4,8},{5,13},{8,4},{9,1},{12,0},{13,5},{2,14},{3,11},... | collective-permute-start | bytes 61448 | tf_op jit(solution)/shard_map/ppermute | solution.py:66
  15.1 3.7 %collective-permute-start.5 = (bf16[80,128]{1,0:T(8,128)(2,1)S(1)}, bf16[80,128]{1,0:T(8,128)(2,1)S(1)}, u32[]{:S(2)}, u32[]{:S(2)}) collective-permute-start(bf16[80,128]{1,0:T(8,128)(2,1)S(1)} %get-tuple-element.27._), channel_id=1, source_target_pairs={{0,0},{1,5},{4,4},{5,1},{8,8},{9,13},{12,12},{13,9},{2,2},{3,7},{6... | collective-permute-start | bytes 61448 | tf_op jit(solution)/shard_map/ppermute | solution.py:66
  19.0 4.5 %collective-permute-start.9 = (bf16[80,128]{1,0:T(8,128)(2,1)S(1)}, bf16[80,128]{1,0:T(8,128)(2,1)S(1)}, u32[]{:S(2)}, u32[]{:S(2)}) collective-permute-start(bf16[80,128]{1,0:T(8,128)(2,1)S(1)} %merge.1._.refs_2_), channel_id=1, source_target_pairs={{0,3},{1,2},{2,1},{3,0},{4,7},{5,6},{6,5},{7,4},{8,11},{9,10},{10,... | collective-permute-start | bytes 61448 | tf_op jit(solution)/shard_map/ppermute | solution.py:35
  19.5 4.0 %collective-permute-start.8 = (bf16[80,128]{1,0:T(8,128)(2,1)S(1)}, bf16[80,128]{1,0:T(8,128)(2,1)S(1)}, u32[]{:S(2)}, u32[]{:S(2)}) collective-permute-start(bf16[80,128]{1,0:T(8,128)(2,1)S(1)} %merge.1._.refs_2_), channel_id=1, source_target_pairs={{0,2},{1,3},{2,0},{3,1},{4,6},{5,7},{6,4},{7,5},{8,10},{9,11},{10,... | collective-permute-start | bytes 61448 | tf_op jit(solution)/shard_map/ppermute | solution.py:35
  20.5 3.0 %collective-permute-start.7 = (bf16[80,128]{1,0:T(8,128)(2,1)S(1)}, bf16[80,128]{1,0:T(8,128)(2,1)S(1)}, u32[]{:S(2)}, u32[]{:S(2)}) collective-permute-start(bf16[80,128]{1,0:T(8,128)(2,1)S(1)} %merge.1._.refs_2_), channel_id=1, source_target_pairs={{0,1},{1,0},{2,3},{3,2},{4,5},{5,4},{6,7},{7,6},{8,9},{9,8},{10,11... | collective-permute-start | bytes 61448 | tf_op jit(solution)/shard_map/ppermute | solution.py:35
  26.1 3.8 %collective-permute-start.10 = (bf16[64,128]{1,0:T(8,128)(2,1)S(1)}, bf16[64,128]{1,0:T(8,128)(2,1)S(1)}, u32[]{:S(2)}, u32[]{:S(2)}) collective-permute-start(bf16[64,128]{1,0:T(8,128)(2,1)S(1)} %get-tuple-element.30._), channel_id=1, source_target_pairs={{0,4},{4,0},{8,12},{12,8},{1,5},{5,1},{9,13},{13,9},{2,6},{6,2},{1... | collective-permute-start | bytes 49160 | tf_op jit(solution)/shard_map/ppermute | solution.py:572
  30.5 4.7 %collective-permute-start.11 = (bf16[64,128]{1,0:T(8,128)(2,1)S(1)}, bf16[64,128]{1,0:T(8,128)(2,1)S(1)}, u32[]{:S(2)}, u32[]{:S(2)}) collective-permute-start(bf16[64,128]{1,0:T(8,128)(2,1)S(1)} %get-tuple-element.32), channel_id=1, source_target_pairs={{0,8},{4,12},{8,0},{12,4},{1,9},{5,13},{9,1},{13,5},{2,10},{6,14},... | collective-permute-start | bytes 49160 | tf_op jit(solution)/shard_map/ppermute | solution.py:572
  35.8 1.9 %collective-permute-start.12 = (bf16[32,128]{1,0:T(8,128)(2,1)S(1)}, bf16[32,128]{1,0:T(8,128)(2,1)S(1)}, u32[]{:S(2)}, u32[]{:S(2)}) collective-permute-start(bf16[32,128]{1,0:T(8,128)(2,1)S(1)} %get-tuple-element.34), channel_id=1, source_target_pairs={{0,1},{1,0},{2,3},{3,2},{4,5},{5,4},{6,7},{7,6},{8,9},{9,8},{10,11... | collective-permute-start | bytes 24584 | tf_op jit(solution)/shard_map/ppermute | solution.py:35
  35.8 3.7 %collective-permute-start.13 = (bf16[32,128]{1,0:T(8,128)(2,1)S(1)}, bf16[32,128]{1,0:T(8,128)(2,1)S(1)}, u32[]{:S(2)}, u32[]{:S(2)}) collective-permute-start(bf16[32,128]{1,0:T(8,128)(2,1)S(1)} %get-tuple-element.35), channel_id=1, source_target_pairs={{0,2},{1,3},{2,0},{3,1},{4,6},{5,7},{6,4},{7,5},{8,10},{9,11},{10,... | collective-permute-start | bytes 24584 | tf_op jit(solution)/shard_map/ppermute | solution.py:35
  37.4 3.1 %collective-permute-start.14 = (bf16[32,128]{1,0:T(8,128)(2,1)S(1)}, bf16[32,128]{1,0:T(8,128)(2,1)S(1)}, u32[]{:S(2)}, u32[]{:S(2)}) collective-permute-start(bf16[32,128]{1,0:T(8,128)(2,1)S(1)} %get-tuple-element.36), channel_id=1, source_target_pairs={{0,3},{1,2},{2,1},{3,0},{4,7},{5,6},{6,5},{7,4},{8,11},{9,10},{10,... | collective-permute-start | bytes 24584 | tf_op jit(solution)/shard_map/ppermute | solution.py:35

commit v4 on v3

--- a/solution.py
+++ b/solution.py
@@ -109,15 +109,15 @@
     )(key_cache, value_cache)
 
 
-def slots_of(lang_refs, rows, share):
+def slots_of(named, share):
     home = holder()
     d = lax.axis_index("dp")
     found = jnp.int32(0)
     row_ids = [jnp.int32(-1)] * SLOTS
     langs = [jnp.int32(0)] * SLOTS
-    for k, lang_ref in enumerate(lang_refs):
-        for i in range(rows):
-            lang = lang_ref[i]
+    for k, row_langs in enumerate(named):
+        rows = len(row_langs)
+        for i, lang in enumerate(row_langs):
             mine = lang // share == home
             for s in range(SLOTS):
                 take = mine & (found == s)
@@ -198,15 +198,12 @@
     )(*queries, key_cache)
 
 
-def attend_kernel(count, near, lang_share, *refs):
-    scalars, refs = refs[:near + 1], refs[near + 1:]
+def attend_kernel(count, near, length_any, *refs):
+    refs = refs[near:]
     wide_ref, score_ref, own_value_ref, key_ref, value_ref = refs[:5]
-    out_refs, (slot_ref, lang_ref, lang_sems) = refs[5:count + 5], refs[count + 5:]
-    lang_copies = [
-        pltpu.make_async_copy(src, lang_ref.at[k], lang_sems.at[k]) for k, src in enumerate(scalars)
-    ]
-    for copy in lang_copies:
-        copy.start()
+    out_refs, (length_ref, length_sem) = refs[5:count + 5], refs[count + 5:]
+    length_copy = pltpu.make_async_copy(length_any, length_ref, length_sem)
+    length_copy.start()
     rows, _, span, _ = key_ref.shape
     chunks, tall, _ = wide_ref.shape
     size = tall // rows
@@ -215,26 +212,16 @@
     other = [
         scores_of(wide_ref[n], key_ref, group_of(n, chunks, count, size)) for n in range(chunks)
     ]
-    for copy in lang_copies:
-        copy.wait()
-    row_ids, langs = slots_of([lang_ref.at[k] for k in range(near)], rows, lang_share)
-    row = iota(slot_ref.shape, 0)
-    own = lang_ref[0, p] // lang_share
-    slots = jnp.where(row == SLOTS, own ^ holder(), -1)
-    for s in range(SLOTS):
-        slots = jnp.where(row == s, row_ids[s], slots)
-        slots = jnp.where(row == SLOTS + 1 + s, langs[s], slots)
-    slot_ref[...] = slots
-
+    length_copy.wait()
     block = share * rows
     spot = iota((tall, LANES), 1) % block - iota((tall, LANES), 0)
     tops, totals = [0.0] * count, [0.0] * count
     place = iota((tall, 2 * span), 1)
     start = jnp.where(place < span, p, (1 ^ p) - 1) + 2 * t
     which = iota((tall, 2 * span), 0) % rows
-    length = lang_ref[near, 0]
+    length = length_ref[0]
     for r in range(1, rows):
-        length = jnp.where(which == r, lang_ref[near, r], length)
+        length = jnp.where(which == r, length_ref[r], length)
     visible = start * span + place < length
     for n in range(chunks):
         k, c = divmod(n, chunks // count)
@@ -295,23 +282,66 @@
     return jnp.concatenate([part[:block] for part in parts for _ in range(LANES // block)], axis=0)
 
 
-def attend(langs, lengths, wide, scores, own_value, key, value, count, lang_share):
+def attend(lengths, langs, wide, scores, own_value, key, value, count):
     near = len(langs)
     chunks, tall, _ = wide.shape
     rows = key.shape[0]
     chunk = jax.ShapeDtypeStruct((chunks // count * tall + STATS, LANES), jnp.bfloat16)
     return pl.pallas_call(
-        functools.partial(attend_kernel, count, near, lang_share),
-        out_shape=[chunk] * count + [jax.ShapeDtypeStruct((8, LANES), jnp.int32)],
+        functools.partial(attend_kernel, count, near),
+        out_shape=[chunk] * count,
         in_specs=[ANY] * (near + 1) + [VMEM] * 5,
-        out_specs=[VMEM] * (count + 1),
-        scratch_shapes=[
-            pltpu.SMEM((near + 1, rows), jnp.int32),
-            pltpu.SemaphoreType.DMA((near + 1,)),
-        ],
+        out_specs=[VMEM] * count,
+        scratch_shapes=[pltpu.SMEM((rows,), jnp.int32), pltpu.SemaphoreType.DMA],
         compiler_params=pltpu.CompilerParams(vmem_limit_bytes=16 << 20),
         name="attend",
-    )(*langs, lengths, wide, scores, own_value, key, value)
+    )(lengths, *langs, wide, scores, own_value, key, value)
+
+
+def first_kernel(near, *refs):
+    lang_refs, (_, table_hbm, table_ref, slot_ref, sems) = refs[:near], refs[near:]
+    share = table_hbm.shape[1]
+    named = []
+    for lang_ref in lang_refs:
+        vector = lang_ref[...].astype(jnp.float32)
+        lane = iota(vector.shape, 1)
+        named.append(
+            [
+                jnp.max(jnp.where(lane == i, vector, -1.0)).astype(jnp.int32)
+                for i in range(vector.shape[1])
+            ]
+        )
+    row_ids, langs = slots_of(named, share)
+    copies = start_tables(0, langs, table_hbm, table_ref, sems)
+    pipe = lax.axis_index("pipe")
+    own = named[0][0]
+    for i in range(1, len(named[0])):
+        own = jnp.where(pipe == i, named[0][i], own)
+    row = iota(slot_ref.shape, 0)
+    slots = jnp.where(row == SLOTS, (own // share) ^ holder(), -1)
+    for s in range(SLOTS):
+        slots = jnp.where(row == s, row_ids[s], slots)
+        slots = jnp.where(row == SLOTS + 1 + s, langs[s], slots)
+    slot_ref[...] = slots
+    for copy in copies:
+        copy.wait()
+
+
+def fetch_first(langs, after, adapter, count):
+    _, _, stretch, wide = adapter.shape
+    near = len(langs)
+    return pl.pallas_call(
+        functools.partial(first_kernel, near),
+        out_shape=[
+            jax.ShapeDtypeStruct((count, SLOTS, stretch, wide), jnp.bfloat16),
+            jax.ShapeDtypeStruct((8, LANES), jnp.int32),
+        ],
+        in_specs=[VMEM] * near + [ANY, HBM],
+        out_specs=[VMEM, VMEM],
+        scratch_shapes=[pltpu.SemaphoreType.DMA((count, SLOTS))],
+        compiler_params=pltpu.CompilerParams(vmem_limit_bytes=16 << 20),
+        name="fetch_first",
+    )(*langs, after, adapter)
 
 
 def fetch_kernel(first, slot_ref, _, table_hbm, table_ref, sems):
@@ -550,19 +580,17 @@
     tensor, near, pipe = (lax.axis_size(a) for a in ("tensor", "dp", "pipe"))
     rows = queries.shape[0]
     holders = near * pipe
-    levels, lang_share, stretch, _ = adapter.shape
+    levels, _, stretch, _ = adapter.shape
     local = stretch.bit_length() - 1
     caches = [pltpu.with_memory_space_constraint(c, pltpu.HBM) for c in (key_cache, value_cache)]
     swap = [(0, 1), (1, 0)]
     sent = send_halves(*caches)
     other = [lax.ppermute(half, "pipe", swap) for half in sent]
-    langs = exchange([languages] * near, "dp", near)
+    langs = exchange([languages.reshape(1, rows)] * near, "dp", near)
     spread = cores_exchange([queries] * (tensor // 2), tensor)
     wide, scores, sums = attend_own(spread, key_cache)
-    *parts, slots = attend(
-        langs, lengths, wide, scores, value_cache, *other, tensor // 2, lang_share
-    )
-    first = fetch(slots, parts[0], adapter, 0, FIRST)
+    parts = attend(lengths, langs, wide, scores, value_cache, *other, tensor // 2)
+    first, slots = fetch_first(langs, parts[0], adapter, FIRST)
     part = merged(cores_exchange(parts, tensor), first)
     second = fetch(slots, part, adapter, FIRST, local - FIRST)
     parts = exchange([part] * holders, ("dp", "pipe"), holders)

time: 41.3 us -> 41 us (level)
    pallas_call x3 -> x2, Pallas kernels: 6.01 us -> 4.34 us  [fetch(): pl.pallas_call(functools.partial(fetch_kernel, first), out_shape=jax.Shap...]
    pallas_call x1 -> x2, Pallas kernels: 1.41 us -> 2.84 us  [the longest x1 1.71 us: fetch_first(): pl.pallas_call(functools.partial(first_kernel, near), out_shape=[jax.Shap...]
where the time goes in v4:
time: 41 us; the launch traced here: 40.8 us
  starting transfers between devices  17.2 us (42%)
  Pallas kernels  14.1 us (34%)
  waiting for transfers between devices  9.4 us (23%)
    ppermute x4, starting transfers between devices, cores_exchange(): out.append(lax.ppermute(block, ('tensor', 'pipe'), route))  8.29 us
    ppermute x7, starting transfers between devices, exchange(): out.append(lax.ppermute(blocks[k], axis, route))  5.32 us
    pallas_call x2, Pallas kernels, fetch(): pl.pallas_call(functools.partial(fetch_kernel, first), out_shape=jax.Shap...  4.34 us
    ppermute x7, waiting for transfers between devices, exchange(): out.append(lax.ppermute(blocks[k], axis, route))  4.2 us
    ppermute x2, waiting for transfers between devices, shards(): z = lax.ppermute(z, 'tensor', [(i, i ^ 1 << n) for i in range(tensor)])  3.87 us
    ppermute x2, starting transfers between devices, shards(): z = lax.ppermute(z, 'tensor', [(i, i ^ 1 << n) for i in range(tensor)])  2.96 us
    pallas_call x1, Pallas kernels, local_levels(): pl.pallas_call(functools.partial(local_kernel, count, len(tables), local,...  2.57 us
    pallas_call x1, Pallas kernels, send_halves(): pl.pallas_call(send_kernel, out_shape=[half, half], in_specs=[HBM, HBM],...  1.79 us
  transfers between devices with their start and end apart: 15, of which 6 were waited for; matrix products, arithmetic and copies ran while one was open for 0% of the time, Pallas kernels for 16%

profile of v4, /device:TPU:0, one launch (start us, length us, event | category | flops | bytes accessed | tf_op | source)
XLA Modules:
  0.0 40.8 jit_solution(8139019923871708653)
XLA Ops:
  0.0 0.0 copy-start
  0.0 0.0 copy-start.4
  0.0 0.0 copy-start.2
  0.0 1.8 %send_halves.1 = (bf16[2,4,512,128]{3,2,1,0:T(8,128)(2,1)S(1)}, bf16[2,4,512,128]{3,2,1,0:T(8,128)(2,1)S(1)}) custom-call(bf16[2,8,512,128]{3,2,1,0:T(8,128)(2,1)} %refs_0_.1, bf16[2,8,512,128]{3,2,1,0:T(8,128)(2,1)} %refs_4_.1), custom_call_target="tpu_custom_call" | custom-call | tf_op jit(solution)/shard_map/send_halves/pallas_call | solution.py:101
  1.8 0.0 copy-start.1
  1.8 0.0 copy-start.3
  1.8 0.5 %collective-permute-start.3 = (bf16[2,4,512,128]{3,2,1,0:T(8,128)(2,1)S(1)}, bf16[2,4,512,128]{3,2,1,0:T(8,128)(2,1)S(1)}, u32[]{:S(2)}, u32[]{:S(2)}) collective-permute-start(bf16[2,4,512,128]{3,2,1,0:T(8,128)(2,1)S(1)} %get-tuple-element.24), channel_id=1, source_target_pairs={{0,1},{1,0},{2,3},{3,2},{4,5},{5,4},{6,7},{7,6},{8,9},{9,8},{10,11... | collective-permute-start | bytes 3145736 | tf_op jit(solution)/shard_map/ppermute | solution.py:588
  2.4 0.1 collective-permute-start.4
  2.4 0.0 copy-done.4
  2.4 5.0 %collective-permute-start.2 = (bf16[2,4096]{1,0:T(2,128)(2,1)S(1)}, bf16[2,4096]{1,0:T(2,128)(2,1)S(1)}, u32[]{:S(2)}, u32[]{:S(2)}) collective-permute-start(bf16[2,4096]{1,0:T(2,128)(2,1)S(1)} %copy-done.4), channel_id=1, source_target_pairs={{0,12},{1,9},{4,8},{5,13},{8,4},{9,1},{12,0},{13,5},{2,14},{3,11},... | collective-permute-start | bytes 49160 | tf_op jit(solution)/shard_map/ppermute | solution.py:66
  7.5 0.7 %collective-permute-start.1 = (bf16[2,4096]{1,0:T(2,128)(2,1)S(1)}, bf16[2,4096]{1,0:T(2,128)(2,1)S(1)}, u32[]{:S(2)}, u32[]{:S(2)}) collective-permute-start(bf16[2,4096]{1,0:T(2,128)(2,1)S(1)} %copy-done.4), channel_id=1, source_target_pairs={{0,0},{1,5},{4,4},{5,1},{8,8},{9,13},{12,12},{13,9},{2,2},{3,7},{6... | collective-permute-start | bytes 49160 | tf_op jit(solution)/shard_map/ppermute | solution.py:66
  8.1 0.0 copy-done.2
  8.1 1.6 %collective-permute-start = (s32[1,2]{1,0:T(1,128)S(1)}, s32[1,2]{1,0:T(1,128)S(1)}, u32[]{:S(2)}, u32[]{:S(2)}) collective-permute-start(s32[1,2]{1,0:T(1,128)S(1)} %bitcast.1), channel_id=1, source_target_pairs={{0,2},{2,0},{1,3},{3,1},{4,6},{6,4},{5,7},{7,5},{8,10},{10,8},{9,1... | collective-permute-start | bytes 32 | tf_op jit(solution)/shard_map/ppermute | solution.py:35
  9.7 0.0 collective-permute-done.2.refs_1_
  9.7 0.0 collective-permute-done.1.refs_0_
  9.7 0.0 copy-done
  9.7 0.6 %attend_own.1 = (bf16[4,32,256]{2,1,0:T(8,128)(2,1)S(1)}, f32[4,32,512]{2,1,0:T(8,128)S(1)}, bf16[2048,128]{1,0:T(8,128)(2,1)S(1)}) custom-call(bf16[2,4096]{1,0:T(2,128)(2,1)S(1)} %collective-permute-done.1.refs_0_, bf16[2,4096]{1,0:T(2,128)(2,1)S(1)} %collective-permute-done.2.refs_1_, bf16[2,8,512,128]{3,2,1,0:T(8,128)(2,1)S(1)} %copy-done), custom_call_target="tpu_custom_call" | custom-call | tf_op jit(solution)/shard_map/attend_own/pallas_call | solution.py:187
  10.3 1.4 %collective-permute-done.refs_1_ = s32[1,2]{1,0:T(1,128)S(1)} collective-permute-done((s32[1,2]{1,0:T(1,128)S(1)}, s32[1,2]{1,0:T(1,128)S(1)}, u32[]{:S(2)}, u32[]{:S(2)}) %collective-permute-start) | collective-permute-done | bytes 40 | tf_op jit(solution)/shard_map/ppermute | solution.py:35
  11.7 0.0 collective-permute-done.3.refs_5_
  11.7 0.0 collective-permute-done.4.refs_6_
  11.8 0.0 copy-done.1
  11.8 0.0 copy-done.3
  11.8 1.1 %attend.1 = (bf16[80,128]{1,0:T(8,128)(2,1)S(1)}, bf16[80,128]{1,0:T(8,128)(2,1)S(1)}) custom-call(s32[2]{0:T(128)S(1)} %copy-done.3, s32[1,2]{1,0:T(1,128)S(1)} %bitcast.2, s32[1,2]{1,0:T(1,128)S(1)} %collective-permute-done.refs_1_, bf16[4,32,256]{2,1,0:T(8,128)(2,1)S(1)} %get-tuple-element.22.refs_2_, f32[4,32,512]{2,1,0:T(8,128)S(1)} %get-tuple-element.23.refs_3_, ...), custom_call_target="tpu_custom_call" | custom-call | tf_op jit(solution)/shard_map/attend/pallas_call | solution.py:290
  12.9 2.0 %collective-permute-start.6 = (bf16[80,128]{1,0:T(8,128)(2,1)S(1)}, bf16[80,128]{1,0:T(8,128)(2,1)S(1)}, u32[]{:S(2)}, u32[]{:S(2)}) collective-permute-start(bf16[80,128]{1,0:T(8,128)(2,1)S(1)} %get-tuple-element.30), channel_id=1, source_target_pairs={{0,12},{1,9},{4,8},{5,13},{8,4},{9,1},{12,0},{13,5},{2,14},{3,11},... | collective-permute-start | bytes 61448 | tf_op jit(solution)/shard_map/ppermute | solution.py:66
  14.9 0.7 %collective-permute-start.5 = (bf16[80,128]{1,0:T(8,128)(2,1)S(1)}, bf16[80,128]{1,0:T(8,128)(2,1)S(1)}, u32[]{:S(2)}, u32[]{:S(2)}) collective-permute-start(bf16[80,128]{1,0:T(8,128)(2,1)S(1)} %get-tuple-element.26.refs_2_), channel_id=1, source_target_pairs={{0,0},{1,5},{4,4},{5,1},{8,8},{9,13},{12,12},{13,9},{2,2},{3,7},{6... | collective-permute-start | bytes 61448 | tf_op jit(solution)/shard_map/ppermute | solution.py:66
  15.5 1.7 %fetch_first.1 = (bf16[2,2,128,2048]{3,2,1,0:T(8,128)(2,1)S(1)}, s32[8,128]{1,0:T(8,128)S(1)}) custom-call(s32[1,2]{1,0:T(1,128)S(1)} %bitcast.3, s32[1,2]{1,0:T(1,128)S(1)} %collective-permute-done.refs_1_, bf16[80,128]{1,0:T(8,128)(2,1)S(1)} %get-tuple-element.26.refs_2_, bf16[9,8,128,2048]{3,2,1,0:T(8,128)(2,1)} %table_hbm.3), custom_call_target="tpu_custom_call" | custom-call | tf_op jit(solution)/shard_map/fetch_first/pallas_call | solution.py:333
  17.2 1.3 %collective-permute-done.6.refs_1_ = bf16[80,128]{1,0:T(8,128)(2,1)S(1)} collective-permute-done((bf16[80,128]{1,0:T(8,128)(2,1)S(1)}, bf16[80,128]{1,0:T(8,128)(2,1)S(1)}, u32[]{:S(2)}, u32[]{:S(2)}) %collective-permute-start.6) | collective-permute-done | bytes 20512 | tf_op jit(solution)/shard_map/ppermute | solution.py:66
  18.6 0.0 collective-permute-done.5.refs_0_
  18.6 0.1 merge.1._.refs_2_
  18.7 0.6 %collective-permute-start.9 = (bf16[80,128]{1,0:T(8,128)(2,1)S(1)}, bf16[80,128]{1,0:T(8,128)(2,1)S(1)}, u32[]{:S(2)}, u32[]{:S(2)}) collective-permute-start(bf16[80,128]{1,0:T(8,128)(2,1)S(1)} %merge.1._.refs_2_), channel_id=1, source_target_pairs={{0,3},{1,2},{2,1},{3,0},{4,7},{5,6},{6,5},{7,4},{8,11},{9,10},{10,... | collective-permute-start | bytes 61448 | tf_op jit(solution)/shard_map/ppermute | solution.py:35
  19.3 1.0 %collective-permute-start.8 = (bf16[80,128]{1,0:T(8,128)(2,1)S(1)}, bf16[80,128]{1,0:T(8,128)(2,1)S(1)}, u32[]{:S(2)}, u32[]{:S(2)}) collective-permute-start(bf16[80,128]{1,0:T(8,128)(2,1)S(1)} %merge.1._.refs_2_), channel_id=1, source_target_pairs={{0,2},{1,3},{2,0},{3,1},{4,6},{5,7},{6,4},{7,5},{8,10},{9,11},{10,... | collective-permute-start | bytes 61448 | tf_op jit(solution)/shard_map/ppermute | solution.py:35
  20.3 0.3 collective-permute-start.7
  20.6 2.7 %fetch.2.refs_1_ = bf16[5,2,128,2048]{3,2,1,0:T(8,128)(2,1)S(1)} custom-call(s32[8,128]{1,0:T(8,128)S(1)} %get-tuple-element.27.slot_ref, bf16[80,128]{1,0:T(8,128)(2,1)S(1)} %merge.1._.refs_2_, bf16[9,8,128,2048]{3,2,1,0:T(8,128)(2,1)} %table_hbm.3), custom_call_target="tpu_custom_call" | custom-call | tf_op jit(solution)/shard_map/fetch/pallas_call | solution.py:356
  23.2 0.0 collective-permute-done.9.refs_5_
  23.3 0.0 collective-permute-done.8.refs_4_
  23.3 0.0 collective-permute-done.7.refs_3_
  23.3 2.6 %local_levels.1 = (bf16[256,128]{1,0:T(8,128)(2,1)S(1)}, bf16[64,128]{1,0:T(8,128)(2,1)S(1)}) custom-call(s32[8,128]{1,0:T(8,128)S(1)} %get-tuple-element.27.slot_ref, bf16[2048,128]{1,0:T(8,128)(2,1)S(1)} %get-tuple-element.28.sums_ref, bf16[2,2,128,2048]{3,2,1,0:T(8,128)(2,1)S(1)} %get-tuple-element.29.refs_2_.refs_0_, ...), custom_call_target="tpu_custom_call" | custom-call | tf_op jit(solution)/shard_map/local_levels/pallas_call | solution.py:480
  25.9 0.8 %collective-permute-start.10 = (bf16[64,128]{1,0:T(8,128)(2,1)S(1)}, bf16[64,128]{1,0:T(8,128)(2,1)S(1)}, u32[]{:S(2)}, u32[]{:S(2)}) collective-permute-start(bf16[64,128]{1,0:T(8,128)(2,1)S(1)} %get-tuple-element.32._), channel_id=1, source_target_pairs={{0,4},{4,0},{8,12},{12,8},{1,5},{5,1},{9,13},{13,9},{2,6},{6,2},{1... | collective-permute-start | bytes 49160 | tf_op jit(solution)/shard_map/ppermute | solution.py:600
  26.7 1.7 %fetch.3.far_ref = bf16[2,2,128,2048]{3,2,1,0:T(8,128)(2,1)S(1)} custom-call(s32[8,128]{1,0:T(8,128)S(1)} %get-tuple-element.27.slot_ref, bf16[64,128]{1,0:T(8,128)(2,1)S(1)} %get-tuple-element.32._, bf16[9,8,128,2048]{3,2,1,0:T(8,128)(2,1)} %table_hbm.3), custom_call_target="tpu_custom_call" | custom-call | tf_op jit(solution)/shard_map/fetch/pallas_call | solution.py:356
  28.4 1.3 %collective-permute-done.10.z_ref = bf16[64,128]{1,0:T(8,128)(2,1)S(1)} collective-permute-done((bf16[64,128]{1,0:T(8,128)(2,1)S(1)}, bf16[64,128]{1,0:T(8,128)(2,1)S(1)}, u32[]{:S(2)}, u32[]{:S(2)}) %collective-permute-start.10) | collective-permute-done | bytes 16416 | tf_op jit(solution)/shard_map/ppermute | solution.py:600
  29.7 0.6 %cross_level.1 = (bf16[256,128]{1,0:T(8,128)(2,1)S(1)}, bf16[64,128]{1,0:T(8,128)(2,1)S(1)}) custom-call(bf16[256,128]{1,0:T(8,128)(2,1)S(1)} %get-tuple-element.31.x_ref, bf16[64,128]{1,0:T(8,128)(2,1)S(1)} %collective-permute-done.10.z_ref, bf16[2048,128]{1,0:T(8,128)(2,1)S(1)} %get-tuple-element.28.sums_ref, bf16[2,2,128,2048]{3,2,1,0:T(8,128)(2,1)S(1)} %fetch.3.far_ref), custom_call_target="tpu_custom_call" | custom-call | tf_op jit(solution)/shard_map/cross_level/pallas_call | solution.py:512
  30.2 2.1 %collective-permute-start.11 = (bf16[64,128]{1,0:T(8,128)(2,1)S(1)}, bf16[64,128]{1,0:T(8,128)(2,1)S(1)}, u32[]{:S(2)}, u32[]{:S(2)}) collective-permute-start(bf16[64,128]{1,0:T(8,128)(2,1)S(1)} %get-tuple-element.34), channel_id=1, source_target_pairs={{0,8},{4,12},{8,0},{12,4},{1,9},{5,13},{9,1},{13,5},{2,10},{6,14},... | collective-permute-start | bytes 49160 | tf_op jit(solution)/shard_map/ppermute | solution.py:600
  32.3 2.6 %collective-permute-done.11.z_ref = bf16[64,128]{1,0:T(8,128)(2,1)S(1)} collective-permute-done((bf16[64,128]{1,0:T(8,128)(2,1)S(1)}, bf16[64,128]{1,0:T(8,128)(2,1)S(1)}, u32[]{:S(2)}, u32[]{:S(2)}) %collective-permute-start.11) | collective-permute-done | bytes 16416 | tf_op jit(solution)/shard_map/ppermute | solution.py:600
  34.9 0.6 %last_level.1 = (bf16[32,128]{1,0:T(8,128)(2,1)S(1)}, bf16[32,128]{1,0:T(8,128)(2,1)S(1)}, bf16[32,128]{1,0:T(8,128)(2,1)S(1)}, bf16[32,128]{1,0:T(8,128)(2,1)S(1)}) custom-call(s32[8,128]{1,0:T(8,128)S(1)} %get-tuple-element.27.slot_ref, bf16[256,128]{1,0:T(8,128)(2,1)S(1)} %get-tuple-element.33.x_ref, bf16[64,128]{1,0:T(8,128)(2,1)S(1)} %collective-permute-done.11.z_ref, ...), custom_call_target="tpu_custom_call" | custom-call | tf_op jit(solution)/shard_map/last_level/pallas_call | solution.py:545
  35.6 0.0 collective-permute-start.12
  35.6 1.6 %collective-permute-start.13 = (bf16[32,128]{1,0:T(8,128)(2,1)S(1)}, bf16[32,128]{1,0:T(8,128)(2,1)S(1)}, u32[]{:S(2)}, u32[]{:S(2)}) collective-permute-start(bf16[32,128]{1,0:T(8,128)(2,1)S(1)} %get-tuple-element.37), channel_id=1, source_target_pairs={{0,2},{1,3},{2,0},{3,1},{4,6},{5,7},{6,4},{7,5},{8,10},{9,11},{10,... | collective-permute-start | bytes 24584 | tf_op jit(solution)/shard_map/ppermute | solution.py:35
  37.1 0.3 collective-permute-start.14
  37.5 0.0 collective-permute-done.12.refs_1_
  37.5 1.8 %collective-permute-done.13.refs_2_ = bf16[32,128]{1,0:T(8,128)(2,1)S(1)} collective-permute-done((bf16[32,128]{1,0:T(8,128)(2,1)S(1)}, bf16[32,128]{1,0:T(8,128)(2,1)S(1)}, u32[]{:S(2)}, u32[]{:S(2)}) %collective-permute-start.13) | collective-permute-done | bytes 8224 | tf_op jit(solution)/shard_map/ppermute | solution.py:35
  39.3 0.9 %collective-permute-done.14.refs_3_ = bf16[32,128]{1,0:T(8,128)(2,1)S(1)} collective-permute-done((bf16[32,128]{1,0:T(8,128)(2,1)S(1)}, bf16[32,128]{1,0:T(8,128)(2,1)S(1)}, u32[]{:S(2)}, u32[]{:S(2)}) %collective-permute-start.14) | collective-permute-done | bytes 8224 | tf_op jit(solution)/shard_map/ppermute | solution.py:35
  40.2 0.6 %pick.1 = bf16[1,4096]{1,0:T(2,128)(2,1)} custom-call(s32[8,128]{1,0:T(8,128)S(1)} %get-tuple-element.27.slot_ref, bf16[32,128]{1,0:T(8,128)(2,1)S(1)} %get-tuple-element.35.refs_0_, bf16[32,128]{1,0:T(8,128)(2,1)S(1)} %collective-permute-done.12.refs_1_, bf16[32,128]{1,0:T(8,128)(2,1)S(1)} %collective-permute-done.13.refs_2_, ...), custom_call_target="tpu_custom_call" | custom-call | tf_op jit(solution)/shard_map/pick/pallas_call | solution.py:569
Async XLA Ops:
  0.0 9.7 %copy-start = (bf16[2,8,512,128]{3,2,1,0:T(8,128)(2,1)S(1)}, bf16[2,8,512,128]{3,2,1,0:T(8,128)(2,1)}, u32[]{:S(2)}) copy-start(bf16[2,8,512,128]{3,2,1,0:T(8,128)(2,1)} %refs_0_.1) | copy-start | bytes 6291460
  0.0 2.4 %copy-start.4 = (bf16[2,4096]{1,0:T(2,128)(2,1)S(1)}, bf16[2,4096]{1,0:T(2,128)(2,1)}, u32[]{:S(2)}) copy-start(bf16[2,4096]{1,0:T(2,128)(2,1)} %param.6) | copy-start | bytes 49156
  0.0 8.1 %copy-start.2 = (s32[2]{0:T(128)S(1)}, s32[2]{0:T(128)}, u32[]{:S(2)}) copy-start(s32[2]{0:T(128)} %param.10) | copy-start | bytes 28
  1.8 9.9 %copy-start.1 = (bf16[2,8,512,128]{3,2,1,0:T(8,128)(2,1)S(1)}, bf16[2,8,512,128]{3,2,1,0:T(8,128)(2,1)}, u32[]{:S(2)}) copy-start(bf16[2,8,512,128]{3,2,1,0:T(8,128)(2,1)} %refs_4_.1) | copy-start | bytes 6291460
  1.8 9.9 %copy-start.3 = (s32[2]{0:T(128)S(1)}, s32[2]{0:T(128)}, u32[]{:S(2)}) copy-start(s32[2]{0:T(128)} %length_any.1) | copy-start | bytes 28
  1.8 9.9 %collective-permute-start.3 = (bf16[2,4,512,128]{3,2,1,0:T(8,128)(2,1)S(1)}, bf16[2,4,512,128]{3,2,1,0:T(8,128)(2,1)S(1)}, u32[]{:S(2)}, u32[]{:S(2)}) collective-permute-start(bf16[2,4,512,128]{3,2,1,0:T(8,128)(2,1)S(1)} %get-tuple-element.24), channel_id=1, source_target_pairs={{0,1},{1,0},{2,3},{3,2},{4,5},{5,4},{6,7},{7,6},{8,9},{9,8},{10,11... | collective-permute-start | bytes 3145736 | tf_op jit(solution)/shard_map/ppermute | solution.py:588
  2.4 9.4 %collective-permute-start.4 = (bf16[2,4,512,128]{3,2,1,0:T(8,128)(2,1)S(1)}, bf16[2,4,512,128]{3,2,1,0:T(8,128)(2,1)S(1)}, u32[]{:S(2)}, u32[]{:S(2)}) collective-permute-start(bf16[2,4,512,128]{3,2,1,0:T(8,128)(2,1)S(1)} %get-tuple-element.25), channel_id=1, source_target_pairs={{0,1},{1,0},{2,3},{3,2},{4,5},{5,4},{6,7},{7,6},{8,9},{9,8},{10,11... | collective-permute-start | bytes 3145736 | tf_op jit(solution)/shard_map/ppermute | solution.py:588
  2.4 7.3 %collective-permute-start.2 = (bf16[2,4096]{1,0:T(2,128)(2,1)S(1)}, bf16[2,4096]{1,0:T(2,128)(2,1)S(1)}, u32[]{:S(2)}, u32[]{:S(2)}) collective-permute-start(bf16[2,4096]{1,0:T(2,128)(2,1)S(1)} %copy-done.4), channel_id=1, source_target_pairs={{0,12},{1,9},{4,8},{5,13},{8,4},{9,1},{12,0},{13,5},{2,14},{3,11},... | collective-permute-start | bytes 49160 | tf_op jit(solution)/shard_map/ppermute | solution.py:66
  7.5 2.2 %collective-permute-start.1 = (bf16[2,4096]{1,0:T(2,128)(2,1)S(1)}, bf16[2,4096]{1,0:T(2,128)(2,1)S(1)}, u32[]{:S(2)}, u32[]{:S(2)}) collective-permute-start(bf16[2,4096]{1,0:T(2,128)(2,1)S(1)} %copy-done.4), channel_id=1, source_target_pairs={{0,0},{1,5},{4,4},{5,1},{8,8},{9,13},{12,12},{13,9},{2,2},{3,7},{6... | collective-permute-start | bytes 49160 | tf_op jit(solution)/shard_map/ppermute | solution.py:66
  8.1 3.6 %collective-permute-start = (s32[1,2]{1,0:T(1,128)S(1)}, s32[1,2]{1,0:T(1,128)S(1)}, u32[]{:S(2)}, u32[]{:S(2)}) collective-permute-start(s32[1,2]{1,0:T(1,128)S(1)} %bitcast.1), channel_id=1, source_target_pairs={{0,2},{2,0},{1,3},{3,1},{4,6},{6,4},{5,7},{7,5},{8,10},{10,8},{9,1... | collective-permute-start | bytes 32 | tf_op jit(solution)/shard_map/ppermute | solution.py:35
  12.9 5.6 %collective-permute-start.6 = (bf16[80,128]{1,0:T(8,128)(2,1)S(1)}, bf16[80,128]{1,0:T(8,128)(2,1)S(1)}, u32[]{:S(2)}, u32[]{:S(2)}) collective-permute-start(bf16[80,128]{1,0:T(8,128)(2,1)S(1)} %get-tuple-element.30), channel_id=1, source_target_pairs={{0,12},{1,9},{4,8},{5,13},{8,4},{9,1},{12,0},{13,5},{2,14},{3,11},... | collective-permute-start | bytes 61448 | tf_op jit(solution)/shard_map/ppermute | solution.py:66
  14.9 3.7 %collective-permute-start.5 = (bf16[80,128]{1,0:T(8,128)(2,1)S(1)}, bf16[80,128]{1,0:T(8,128)(2,1)S(1)}, u32[]{:S(2)}, u32[]{:S(2)}) collective-permute-start(bf16[80,128]{1,0:T(8,128)(2,1)S(1)} %get-tuple-element.26.refs_2_), channel_id=1, source_target_pairs={{0,0},{1,5},{4,4},{5,1},{8,8},{9,13},{12,12},{13,9},{2,2},{3,7},{6... | collective-permute-start | bytes 61448 | tf_op jit(solution)/shard_map/ppermute | solution.py:66
  18.7 4.5 %collective-permute-start.9 = (bf16[80,128]{1,0:T(8,128)(2,1)S(1)}, bf16[80,128]{1,0:T(8,128)(2,1)S(1)}, u32[]{:S(2)}, u32[]{:S(2)}) collective-permute-start(bf16[80,128]{1,0:T(8,128)(2,1)S(1)} %merge.1._.refs_2_), channel_id=1, source_target_pairs={{0,3},{1,2},{2,1},{3,0},{4,7},{5,6},{6,5},{7,4},{8,11},{9,10},{10,... | collective-permute-start | bytes 61448 | tf_op jit(solution)/shard_map/ppermute | solution.py:35
  19.3 4.0 %collective-permute-start.8 = (bf16[80,128]{1,0:T(8,128)(2,1)S(1)}, bf16[80,128]{1,0:T(8,128)(2,1)S(1)}, u32[]{:S(2)}, u32[]{:S(2)}) collective-permute-start(bf16[80,128]{1,0:T(8,128)(2,1)S(1)} %merge.1._.refs_2_), channel_id=1, source_target_pairs={{0,2},{1,3},{2,0},{3,1},{4,6},{5,7},{6,4},{7,5},{8,10},{9,11},{10,... | collective-permute-start | bytes 61448 | tf_op jit(solution)/shard_map/ppermute | solution.py:35
  20.3 3.0 %collective-permute-start.7 = (bf16[80,128]{1,0:T(8,128)(2,1)S(1)}, bf16[80,128]{1,0:T(8,128)(2,1)S(1)}, u32[]{:S(2)}, u32[]{:S(2)}) collective-permute-start(bf16[80,128]{1,0:T(8,128)(2,1)S(1)} %merge.1._.refs_2_), channel_id=1, source_target_pairs={{0,1},{1,0},{2,3},{3,2},{4,5},{5,4},{6,7},{7,6},{8,9},{9,8},{10,11... | collective-permute-start | bytes 61448 | tf_op jit(solution)/shard_map/ppermute | solution.py:35
  25.9 3.8 %collective-permute-start.10 = (bf16[64,128]{1,0:T(8,128)(2,1)S(1)}, bf16[64,128]{1,0:T(8,128)(2,1)S(1)}, u32[]{:S(2)}, u32[]{:S(2)}) collective-permute-start(bf16[64,128]{1,0:T(8,128)(2,1)S(1)} %get-tuple-element.32._), channel_id=1, source_target_pairs={{0,4},{4,0},{8,12},{12,8},{1,5},{5,1},{9,13},{13,9},{2,6},{6,2},{1... | collective-permute-start | bytes 49160 | tf_op jit(solution)/shard_map/ppermute | solution.py:600
  30.2 4.7 %collective-permute-start.11 = (bf16[64,128]{1,0:T(8,128)(2,1)S(1)}, bf16[64,128]{1,0:T(8,128)(2,1)S(1)}, u32[]{:S(2)}, u32[]{:S(2)}) collective-permute-start(bf16[64,128]{1,0:T(8,128)(2,1)S(1)} %get-tuple-element.34), channel_id=1, source_target_pairs={{0,8},{4,12},{8,0},{12,4},{1,9},{5,13},{9,1},{13,5},{2,10},{6,14},... | collective-permute-start | bytes 49160 | tf_op jit(solution)/shard_map/ppermute | solution.py:600
  35.6 1.9 %collective-permute-start.12 = (bf16[32,128]{1,0:T(8,128)(2,1)S(1)}, bf16[32,128]{1,0:T(8,128)(2,1)S(1)}, u32[]{:S(2)}, u32[]{:S(2)}) collective-permute-start(bf16[32,128]{1,0:T(8,128)(2,1)S(1)} %get-tuple-element.36), channel_id=1, source_target_pairs={{0,1},{1,0},{2,3},{3,2},{4,5},{5,4},{6,7},{7,6},{8,9},{9,8},{10,11... | collective-permute-start | bytes 24584 | tf_op jit(solution)/shard_map/ppermute | solution.py:35
  35.6 3.7 %collective-permute-start.13 = (bf16[32,128]{1,0:T(8,128)(2,1)S(1)}, bf16[32,128]{1,0:T(8,128)(2,1)S(1)}, u32[]{:S(2)}, u32[]{:S(2)}) collective-permute-start(bf16[32,128]{1,0:T(8,128)(2,1)S(1)} %get-tuple-element.37), channel_id=1, source_target_pairs={{0,2},{1,3},{2,0},{3,1},{4,6},{5,7},{6,4},{7,5},{8,10},{9,11},{10,... | collective-permute-start | bytes 24584 | tf_op jit(solution)/shard_map/ppermute | solution.py:35
  37.1 3.1 %collective-permute-start.14 = (bf16[32,128]{1,0:T(8,128)(2,1)S(1)}, bf16[32,128]{1,0:T(8,128)(2,1)S(1)}, u32[]{:S(2)}, u32[]{:S(2)}) collective-permute-start(bf16[32,128]{1,0:T(8,128)(2,1)S(1)} %get-tuple-element.38), channel_id=1, source_target_pairs={{0,3},{1,2},{2,1},{3,0},{4,7},{5,6},{6,5},{7,4},{8,11},{9,10},{10,... | collective-permute-start | bytes 24584 | tf_op jit(solution)/shard_map/ppermute | solution.py:35
